TPU v7x, 32 devices: a whole 2x2x4 slice. The times are simulated.
32 devices in a mesh: dp: 16 (over z, x, core), tensor: 2 (over y).
Axes of the slice: x: 2, y: 2, z: 4, core: 2. Of those that a mesh axis runs over, the one named last changes fastest.
Arguments:
- activations: bfloat16 [73856, 1024], P(('dp', 'tensor')), may hold values from -6 to 6
- first_gain: bfloat16 [1024], P('dp'), may hold values from 0.25 to 1.75
- first_shift: bfloat16 [1024], P('dp'), may hold values from -4 to 4
- heads_weight: bfloat16 [3, 1024, 1024], P(None, 'dp', 'tensor'), may hold values from -0.1875 to 0.1875
- heads_bias: bfloat16 [2, 16, 64], P(None, 'tensor', 'dp'), may hold values from -4 to 4
- merge_weight: bfloat16 [1024, 1024], P('tensor', 'dp'), may hold values from -2 to 2
- merge_bias: bfloat16 [1024], P('dp'), may hold values from -4 to 4
- second_gain: bfloat16 [1024], P('dp'), may hold values from 0.25 to 1.75
- second_shift: bfloat16 [1024], P('dp'), may hold values from -4 to 4
- expand_weight: bfloat16 [1024, 4096], P('dp', 'tensor'), may hold values from -0.1875 to 0.1875
- expand_bias: bfloat16 [32, 128], P('tensor', 'dp'), may hold values from -6 to 6
- reduce_weight: bfloat16 [4096, 1024], P('tensor', 'dp'), may hold values from -0.125 to 0.125
- reduce_bias: bfloat16 [1024], P('dp'), may hold values from -4 to 4
- output_grad: bfloat16 [73856, 1024], P(('dp', 'tensor')), may hold values from -6 to 6
- real_images: int32 [16], P('dp'), may hold values from 1 to 8, as said below
Outputs:
- block_output: bfloat16 [73856, 1024], P(('dp', 'tensor'))
- input_grad: bfloat16 [73856, 1024], P(('dp', 'tensor'))
- first_gain_grad: float32 [1024], P('dp')
- first_shift_grad: float32 [1024], P('dp')
- heads_weight_grad: float32 [3, 1024, 1024], P(None, 'dp', 'tensor')
- heads_bias_grad: float32 [2, 16, 64], P(None, 'tensor', 'dp')
- merge_weight_grad: float32 [1024, 1024], P('tensor', 'dp')
- merge_bias_grad: float32 [1024], P('dp')
- second_gain_grad: float32 [1024], P('dp')
- second_shift_grad: float32 [1024], P('dp')
- expand_weight_grad: float32 [1024, 4096], P('dp', 'tensor')
- expand_bias_grad: float32 [32, 128], P('tensor', 'dp')
- reduce_weight_grad: float32 [4096, 1024], P('tensor', 'dp')
- reduce_bias_grad: float32 [1024], P('dp')
Inputs may be any that keep to these rules, and one draw needn't show every extreme that they name: `real_images`: entry s counts the live images among the 8 slots of dp index s, which come first; some entry equals 8.
All inputs are finite; a program needn't handle non-finite values.
Results may differ from a plain program's by a relative error of at most 0.02.
Values may be sent and summed in bfloat16 or wider, within the bound.
A program may use at most 320 MiB of HBM per device.

v0:
```python
import jax
import jax.numpy as jnp
from jax import lax
from jax.sharding import PartitionSpec as P

HEAD_DIM = 64
SEQ = 577


EPSILON = 1e-06


def normalize(values, gain, shift):
    center = values - jnp.mean(values, axis=-1, keepdims=True)
    second = jnp.mean(center * center, axis=-1, keepdims=True)
    return center * lax.rsqrt(second + EPSILON) * gain + shift


def exact_gelu(values):
    return jax.nn.gelu(values, approximate=False)


def split_triple(block):
    length = block.shape[0]
    width = block.shape[2]
    heads = width // HEAD_DIM
    query = block[:, 0].reshape(length, heads, HEAD_DIM)
    keys = block[:, 1].reshape(length, heads, HEAD_DIM)
    values = block[:, 2].reshape(length, heads, HEAD_DIM)
    return (query, keys, values)


def attend(block):
    query, keys, values = split_triple(block)
    scores = jnp.einsum(
        "qhd,khd->hqk", query, keys, preferred_element_type=jnp.float32
    ) * HEAD_DIM ** (-0.5)
    top = jnp.max(scores, axis=-1, keepdims=True)
    expo = jnp.exp(scores - top)
    total = jnp.sum(expo, axis=-1, keepdims=True)
    probs = (expo / total).astype(jnp.bfloat16)
    context = jnp.einsum("hqk,khd->qhd", probs, values, preferred_element_type=jnp.float32)
    logsum = (top + jnp.log(total))[..., 0]
    return (context.reshape(block.shape[0], block.shape[2]).astype(jnp.bfloat16), logsum)


def attend_back(parts):
    block, logsum, grad_context = parts
    query, keys, values = split_triple(block)
    scale = HEAD_DIM ** (-0.5)
    grad_heads = grad_context.reshape(query.shape)
    scores = jnp.einsum("qhd,khd->hqk", query, keys, preferred_element_type=jnp.float32) * scale
    probs = jnp.exp(scores - logsum[..., None])
    grad_values = jnp.einsum(
        "hqk,qhd->khd", probs.astype(jnp.bfloat16), grad_heads, preferred_element_type=jnp.float32
    )
    grad_probs = jnp.einsum("qhd,khd->hqk", grad_heads, values, preferred_element_type=jnp.float32)
    inner = jnp.sum(probs * grad_probs, axis=-1, keepdims=True)
    grad_scores = (probs * (grad_probs - inner) * scale).astype(jnp.bfloat16)
    grad_query = jnp.einsum("hqk,khd->qhd", grad_scores, keys, preferred_element_type=jnp.float32)
    grad_keys = jnp.einsum("hqk,qhd->khd", grad_scores, query, preferred_element_type=jnp.float32)
    stacked = jnp.stack([grad_query, grad_keys, grad_values], axis=1)
    return stacked.reshape(block.shape).astype(jnp.bfloat16)


def gather_rows(values):
    return lax.all_gather(values, "tensor", axis=0, tiled=True)


def gather_grads(values):
    return lax.all_gather(values, "tensor", axis=0, tiled=True)


def sum_rows(term):
    return lax.psum_scatter(
        term.astype(jnp.bfloat16), "tensor", scatter_dimension=0, tiled=True
    ).astype(jnp.float32)


def sum_inputs(term):
    return lax.psum_scatter(
        term.astype(jnp.bfloat16), "tensor", scatter_dimension=0, tiled=True
    ).astype(jnp.float32)


def forward(inputs, weights):
    (
        gain_one,
        shift_one,
        heads_weight,
        heads_bias,
        merge_weight,
        merge_bias,
        gain_two,
        shift_two,
        expand_weight,
        expand_bias,
        reduce_weight,
        reduce_bias,
    ) = weights
    normed_one = normalize(
        inputs, gain_one.astype(jnp.float32), shift_one.astype(jnp.float32)
    ).astype(jnp.bfloat16)
    gathered_one = gather_rows(normed_one)
    width = heads_weight.shape[2]
    triple = jnp.einsum(
        "td,sdc->tsc", gathered_one, heads_weight, preferred_element_type=jnp.float32
    )
    bias_pair = heads_bias.astype(jnp.float32).reshape(2, width)
    bias_triple = jnp.stack([bias_pair[0], jnp.zeros((width,), jnp.float32), bias_pair[1]])
    triple = (triple + bias_triple).astype(jnp.bfloat16)
    images = triple.shape[0] // SEQ
    context, logsum = lax.map(attend, triple.reshape(images, SEQ, 3, width))
    context = context.reshape(images * SEQ, width)
    merge_term = jnp.dot(context, merge_weight, preferred_element_type=jnp.float32)
    resid = inputs + sum_rows(merge_term) + merge_bias.astype(jnp.float32)
    normed_two = normalize(
        resid, gain_two.astype(jnp.float32), shift_two.astype(jnp.float32)
    ).astype(jnp.bfloat16)
    gathered_two = gather_rows(normed_two)
    hidden_pre = jnp.dot(gathered_two, expand_weight, preferred_element_type=jnp.float32)
    hidden_pre = hidden_pre + expand_bias.astype(jnp.float32).reshape(-1)
    active = exact_gelu(hidden_pre).astype(jnp.bfloat16)
    reduce_term = jnp.dot(active, reduce_weight, preferred_element_type=jnp.float32)
    output = resid + sum_rows(reduce_term) + reduce_bias.astype(jnp.float32)
    return (
        output,
        (gathered_one, triple, logsum, context, resid, gathered_two, hidden_pre, active),
    )


def shards(
    activations,
    first_gain,
    first_shift,
    heads_weight,
    heads_bias,
    merge_weight,
    merge_bias,
    second_gain,
    second_shift,
    expand_weight,
    expand_bias,
    reduce_weight,
    reduce_bias,
    output_grad,
    real_images,
):
    local = (
        first_gain,
        first_shift,
        heads_weight,
        heads_bias,
        merge_weight,
        merge_bias,
        second_gain,
        second_shift,
        expand_weight,
        expand_bias,
        reduce_weight,
        reduce_bias,
    )
    weights_now = (
        lax.all_gather(local[0], "dp", axis=0, tiled=True),
        lax.all_gather(local[1], "dp", axis=0, tiled=True),
        lax.all_gather(local[2], "dp", axis=1, tiled=True),
        lax.all_gather(local[3], "dp", axis=2, tiled=True),
        lax.all_gather(local[4], "dp", axis=1, tiled=True),
        lax.all_gather(local[5], "dp", axis=0, tiled=True),
        lax.all_gather(local[6], "dp", axis=0, tiled=True),
        lax.all_gather(local[7], "dp", axis=0, tiled=True),
        lax.all_gather(local[8], "dp", axis=0, tiled=True),
        lax.all_gather(local[9], "dp", axis=1, tiled=True),
        lax.all_gather(local[10], "dp", axis=1, tiled=True),
        lax.all_gather(local[11], "dp", axis=0, tiled=True),
    )
    inputs = activations.astype(jnp.float32)
    output, saved = forward(inputs, weights_now)
    weights_back = (
        lax.all_gather(local[0], "dp", axis=0, tiled=True),
        lax.all_gather(local[1], "dp", axis=0, tiled=True),
        lax.all_gather(local[2], "dp", axis=1, tiled=True),
        lax.all_gather(local[3], "dp", axis=2, tiled=True),
        lax.all_gather(local[4], "dp", axis=1, tiled=True),
        lax.all_gather(local[5], "dp", axis=0, tiled=True),
        lax.all_gather(local[6], "dp", axis=0, tiled=True),
        lax.all_gather(local[7], "dp", axis=0, tiled=True),
        lax.all_gather(local[8], "dp", axis=0, tiled=True),
        lax.all_gather(local[9], "dp", axis=1, tiled=True),
        lax.all_gather(local[10], "dp", axis=1, tiled=True),
        lax.all_gather(local[11], "dp", axis=0, tiled=True),
    )
    saved = forward(inputs, weights_back)[1]
    gathered_one, triple, logsum, context, resid, gathered_two, hidden_pre, active = saved
    (
        gain_one,
        shift_one,
        wide_heads,
        wide_bias,
        wide_merge,
        merge_shift,
        gain_two,
        shift_two,
        wide_expand,
        wide_expand_bias,
        wide_reduce,
        reduce_shift,
    ) = weights_back
    rows = inputs.shape[0]
    per_device = rows // SEQ
    image_ids = lax.axis_index("tensor") * per_device + lax.iota(jnp.int32, rows) // SEQ
    live = (image_ids < real_images[0]).astype(jnp.float32)
    grad_out = output_grad.astype(jnp.float32) * live[:, None]
    grad_out_full = gather_grads(grad_out.astype(jnp.bfloat16))
    grad_reduce_bias = jnp.sum(grad_out, axis=0)
    grad_reduce_weight = lax.dot_general(
        active, grad_out_full, (((0,), (0,)), ((), ())), preferred_element_type=jnp.float32
    )
    grad_active = lax.dot_general(
        grad_out_full, wide_reduce, (((1,), (1,)), ((), ())), preferred_element_type=jnp.float32
    )
    gelu_pull = jax.vjp(exact_gelu, hidden_pre)[1]
    grad_pre = gelu_pull(grad_active)[0].astype(jnp.bfloat16)
    grad_expand_bias = jnp.sum(grad_pre, axis=0, dtype=jnp.float32).reshape(wide_expand_bias.shape)
    grad_expand_weight = lax.dot_general(
        gathered_two, grad_pre, (((0,), (0,)), ((), ())), preferred_element_type=jnp.float32
    )
    expand_term = lax.dot_general(
        grad_pre, wide_expand, (((1,), (1,)), ((), ())), preferred_element_type=jnp.float32
    )
    grad_normed_two = sum_inputs(expand_term)
    pull_two = jax.vjp(
        normalize, resid, gain_two.astype(jnp.float32), shift_two.astype(jnp.float32)
    )[1]
    back_resid, grad_second_gain, grad_second_shift = pull_two(grad_normed_two)
    grad_resid = grad_out + back_resid
    grad_merge_bias = jnp.sum(grad_resid, axis=0)
    grad_resid_full = gather_grads(grad_resid.astype(jnp.bfloat16))
    grad_merge_weight = lax.dot_general(
        context, grad_resid_full, (((0,), (0,)), ((), ())), preferred_element_type=jnp.float32
    )
    grad_context = lax.dot_general(
        grad_resid_full, wide_merge, (((1,), (1,)), ((), ())), preferred_element_type=jnp.float32
    ).astype(jnp.bfloat16)
    images = context.shape[0] // SEQ
    width = context.shape[1]
    grad_triple = lax.map(
        attend_back,
        (triple.reshape(images, SEQ, 3, width), logsum, grad_context.reshape(images, SEQ, width)),
    )
    grad_triple = grad_triple.reshape(images * SEQ, 3, width)
    triple_sums = jnp.sum(grad_triple, axis=0, dtype=jnp.float32)
    grad_heads_bias = jnp.stack([triple_sums[0], triple_sums[2]]).reshape(wide_bias.shape)
    grad_heads_weight = jnp.einsum(
        "td,tsc->sdc", gathered_one, grad_triple, preferred_element_type=jnp.float32
    )
    heads_term = jnp.einsum(
        "tsc,sdc->td", grad_triple, wide_heads, preferred_element_type=jnp.float32
    )
    grad_normed_one = sum_inputs(heads_term)
    pull_one = jax.vjp(
        normalize, inputs, gain_one.astype(jnp.float32), shift_one.astype(jnp.float32)
    )[1]
    back_input, grad_first_gain, grad_first_shift = pull_one(grad_normed_one)
    input_grad = (grad_resid + back_input).astype(jnp.bfloat16)
    shared = lax.psum(
        (
            grad_first_gain,
            grad_first_shift,
            grad_merge_bias,
            grad_second_gain,
            grad_second_shift,
            grad_reduce_bias,
        ),
        "tensor",
    )
    grads = (
        lax.psum_scatter(
            shared[0].astype(jnp.bfloat16), "dp", scatter_dimension=0, tiled=True
        ).astype(jnp.float32),
        lax.psum_scatter(
            shared[1].astype(jnp.bfloat16), "dp", scatter_dimension=0, tiled=True
        ).astype(jnp.float32),
        lax.psum_scatter(
            grad_heads_weight.astype(jnp.bfloat16), "dp", scatter_dimension=1, tiled=True
        ).astype(jnp.float32),
        lax.psum_scatter(
            grad_heads_bias.astype(jnp.bfloat16), "dp", scatter_dimension=2, tiled=True
        ).astype(jnp.float32),
        lax.psum_scatter(
            grad_merge_weight.astype(jnp.bfloat16), "dp", scatter_dimension=1, tiled=True
        ).astype(jnp.float32),
        lax.psum_scatter(
            shared[2].astype(jnp.bfloat16), "dp", scatter_dimension=0, tiled=True
        ).astype(jnp.float32),
        lax.psum_scatter(
            shared[3].astype(jnp.bfloat16), "dp", scatter_dimension=0, tiled=True
        ).astype(jnp.float32),
        lax.psum_scatter(
            shared[4].astype(jnp.bfloat16), "dp", scatter_dimension=0, tiled=True
        ).astype(jnp.float32),
        lax.psum_scatter(
            grad_expand_weight.astype(jnp.bfloat16), "dp", scatter_dimension=0, tiled=True
        ).astype(jnp.float32),
        lax.psum_scatter(
            grad_expand_bias.astype(jnp.bfloat16), "dp", scatter_dimension=1, tiled=True
        ).astype(jnp.float32),
        lax.psum_scatter(
            grad_reduce_weight.astype(jnp.bfloat16), "dp", scatter_dimension=1, tiled=True
        ).astype(jnp.float32),
        lax.psum_scatter(
            shared[5].astype(jnp.bfloat16), "dp", scatter_dimension=0, tiled=True
        ).astype(jnp.float32),
    )
    return (
        output.astype(jnp.bfloat16),
        input_grad,
        grads[0],
        grads[1],
        grads[2],
        grads[3],
        grads[4],
        grads[5],
        grads[6],
        grads[7],
        grads[8],
        grads[9],
        grads[10],
        grads[11],
    )


def solution(mesh):
    return jax.shard_map(
        shards,
        mesh=mesh,
        in_specs=(
            P(("dp", "tensor"), None),
            P("dp"),
            P("dp"),
            P(None, "dp", "tensor"),
            P(None, "tensor", "dp"),
            P("tensor", "dp"),
            P("dp"),
            P("dp"),
            P("dp"),
            P("dp", "tensor"),
            P("tensor", "dp"),
            P("tensor", "dp"),
            P("dp"),
            P(("dp", "tensor"), None),
            P("dp"),
        ),
        out_specs=(
            P(("dp", "tensor"), None),
            P(("dp", "tensor"), None),
            P("dp"),
            P("dp"),
            P(None, "dp", "tensor"),
            P(None, "tensor", "dp"),
            P("tensor", "dp"),
            P("dp"),
            P("dp"),
            P("dp"),
            P("dp", "tensor"),
            P("tensor", "dp"),
            P("tensor", "dp"),
            P("dp"),
        ),
        check_vma=False,
    )
```

profile of v0, /device:TPU:0, one launch (start us, length us, event | category | flops | bytes accessed | tf_op | source)
XLA Modules:
  0.0 2572.0 jit_solution(3246822091127171579)
XLA Ops:
  13.4 62.9 %all-reduce.27 = (bf16[1024]{0:T(1024)(128)(2,1)}, bf16[1024]{0:T(1024)(128)(2,1)}, bf16[1024]{0:T(1024)(128)(2,1)}, bf16[1024]{0:T(1024)(128)(2,1)S(1)}, bf16[1024]{0:T(1024)(128)(2,1)S(1)}) all-reduce(bf16[1024]{0:T(1024)(128)(2,1)S(1)} %dynamic-update-slice.4, ...), channel_id=1, replica_groups=mesh['dp'=16,'tensor'=2] {'dp'}, use_global_device_ids=true, to_apply=%add.4 | all-reduce | flops 5120 | bytes 20480
  115.4 88.5 %all-gather.23.cloned.1.call-done = bf16[2,2308,1024]{2,1,0:T(8,128)(2,1)} async-done(((bf16[1,2308,1024]{2,1,0:T(8,128)(2,1)}), bf16[2,2308,1024]{2,1,0:T(8,128)(2,1)}) %all-gather.23.cloned.1.call-update) | async-done | bytes 9453584 | tf_op jit(solution)/shard_map/all_gather | solution.py:67
  213.0 38.3 %all-gather.15.cloned.1.call-done = bf16[3,1024,512]{2,1,0:T(8,128)(2,1)} async-done(((bf16[3,64,512]{2,1,0:T(8,128)(2,1)}), bf16[3,1024,512]{2,1,0:T(8,128)(2,1)}) %all-gather.15.cloned.1.call-update) | async-done | bytes 3145744 | tf_op jit(solution)/shard_map/all_gather | solution.py:166
  251.3 21.5 add_convert_fusion.1
  312.7 80.8 %while.33 = (s32[]{:T(128)}, bf16[8,577,512]{2,1,0:T(8,128)(2,1)}, f32[8,8,577]{2,1,0:T(8,128)S(1)}, bf16[8,577,3,512]{1,3,2,0:T(8,128)(2,1)}, s32[]{:T(128)}) while((s32[]{:T(128)}, bf16[8,577,512]{2,1,0:T(8,128)(2,1)}, f32[8,8,577]{2,1,0:T(8,128)S(1)}, bf16[8,577,3,512]{1,3,2,0:T(8,128)(2,1)}, s32[]{:T(128)}) %tuple.96), condition=%wide.region_13.14_spmd, body=%wide.region_10.0_spmd.sunk | while | flops 706100224 | bytes 43939152 | solution.py:113
  409.7 113.2 %fusion.2 = bf16[2312,1024]{1,0:T(8,128)(2,1)} fusion(bf16[4616,1024]{1,0:T(8,128)(2,1)} %convolution_convert_fusion.1), kind=kCustom, calls=%all-reduce-scatter.2 | all-reduce-scatter fusion | flops 4734977 | bytes 14189056
  527.5 23.8 concatenate.11
  590.9 122.0 %while.32 = (s32[]{:T(128)}, bf16[8,577,512]{2,1,0:T(8,128)(2,1)}, bf16[8,577,3,512]{1,3,2,0:T(8,128)(2,1)}, s32[]{:T(128)}) while((s32[]{:T(128)}, bf16[8,577,512]{2,1,0:T(8,128)(2,1)}, bf16[8,577,3,512]{1,3,2,0:T(8,128)(2,1)}, s32[]{:T(128)}) %tuple.131), condition=%wide.region_5.6_spmd, body=%wide.region_2.5_spmd.sunk | while | flops 695451712 | bytes 33168580 | solution.py:113
  747.6 100.8 %fusion.61 = (f32[4616,2048]{1,0:T(8,128)}, f32[4616,2048]{1,0:T(8,128)}) fusion(f32[2048]{0:T(1024)S(1)} %bitcast_convert_fusion.1, bf16[4616,1024]{1,0:T(8,128)(2,1)} %reshape.289, bf16[1024,2048]{1,0:T(8,128)(2,1)} %all-gather.19.cloned.1.call-done), kind=kOutput, calls=%fused_computation.54 | convolution fusion | flops 19956482048 | bytes 89284608 | tf_op jit(solution)/shard_map/dot_general | solution.py:121
  848.4 34.3 %fusion.134 = bf16[2048,1024]{0,1:T(8,128)(2,1)} fusion(bf16[4616,1024]{1,0:T(8,128)(2,1)} %reshape.291, f32[4616,2048]{1,0:T(8,128)} %get-tuple-element.249, f32[4616,2048]{1,0:T(8,128)} %get-tuple-element.250, f32[2048]{0:T(1024)S(1)} %bitcast_convert_fusion.1), kind=kOutput, calls=%fused_computation.172 | convolution fusion | flops 19400818688 | bytes 89284608 | tf_op jit(solution)/shard_map/dot_general | solution.py:216
  882.8 45.0 %fusion.185 = (bf16[2048]{0:T(1024)(128)(2,1)}, bf16[4616,2048]{1,0:T(8,128)(2,1)}) fusion(f32[4616,2048]{1,0:T(8,128)} %get-tuple-element.249, bf16[4616,1024]{1,0:T(8,128)(2,1)} %reshape.291, bf16[2048,1024]{0,1:T(8,128)(2,1)} %all-gather.21.cloned.1.call-done, f32[4616,2048]{1,0:T(8,128)} %get-tuple-element.250, f32[2048]{0:T(1024)S(1)} %bitcast_convert_fusion.1), kind=kOutput, calls=%fused_computation.250 | convolution fusion | flops 19512162304 | bytes 108195840 | tf_op jit(solution)/shard_map/dot_general | solution.py:219
  927.8 27.6 %convolution_convert_fusion.4 = bf16[1024,2048]{1,0:T(8,128)(2,1)} fusion(bf16[4616,1024]{1,0:T(8,128)(2,1)} %reshape.289, bf16[4616,2048]{1,0:T(8,128)(2,1)} %get-tuple-element.252), kind=kOutput, calls=%fused_computation.173 | convolution fusion | flops 19363004416 | bytes 32555008 | tf_op jit(solution)/shard_map/dot_general | solution.py:225
  955.5 26.4 %convolution_convert_fusion = bf16[4616,1024]{1,0:T(8,128)(2,1)} fusion(bf16[4616,2048]{1,0:T(8,128)(2,1)} %get-tuple-element.252, bf16[1024,2048]{1,0:T(8,128)(2,1)} %all-gather.19.cloned.1.call-done), kind=kOutput, calls=%fused_computation.158 | convolution fusion | flops 19365634048 | bytes 32555008 | tf_op jit(solution)/shard_map/dot_general | solution.py:228
  981.9 218.8 %fusion.176 = (bf16[2312,1024]{1,0:T(8,128)(2,1)}, bf16[2312,1024]{1,0:T(8,128)(2,1)}) fusion(bf16[4616,1024]{1,0:T(8,128)(2,1)} %convolution_convert_fusion, bf16[4616,1024]{1,0:T(8,128)(2,1)} %convolution_convert_fusion.2), kind=kCustom, calls=%all-reduce-scatter.6 | all-reduce-scatter fusion | flops 9469953 | bytes 28377600
  1207.1 23.5 concatenate.9
  1230.6 23.4 concatenate.12
  1315.8 109.9 %all-gather.31.cloned.1.call-done = bf16[2,2308,1024]{2,1,0:T(8,128)(2,1)} async-done(((bf16[1,2308,1024]{2,1,0:T(8,128)(2,1)}), bf16[2,2308,1024]{2,1,0:T(8,128)(2,1)}) %all-gather.31.cloned.1.call-update) | async-done | bytes 9453584 | tf_op jit(solution)/shard_map/all_gather | solution.py:71
  1453.6 495.7 %while.34 = (s32[]{:T(128)}, bf16[8,577,3,512]{1,3,2,0:T(8,128)(2,1)}, bf16[8,577,3,512]{1,3,2,0:T(8,128)(2,1)}, f32[8,8,577]{2,1,0:T(8,128)}, bf16[8,577,512]{2,1,0:T(8,128)(2,1)}, /*index=5*/s32[]{:T(128)}) while((s32[]{:T(128)}, bf16[8,577,3,512]{1,3,2,0:T(8,128)(2,1)}, bf16[8,577,3,512]{1,3,2,0:T(8,128)(2,1)}, f32[8,8,577]{2,1,0:T(8,128)}, ...), condition=%wide.region_22.23_spmd, body=%wide.region_20.22_spmd.sunk | while | flops 1766742784 | bytes 136384128 | solution.py:247
  2052.2 103.1 %fusion.60.clone.6 = bf16[4616,2048]{1,0:T(8,128)(2,1)} fusion(bf16[4616,1024]{1,0:T(8,128)(2,1)} %reshape.287, bf16[1024,2048]{1,0:T(8,128)(2,1)} %all-gather.19.cloned.1.call-done, f32[2048]{0:T(1024)S(1)} %copy-done.36), kind=kOutput, calls=%fused_computation.53.clone.clone.clone.clone.clone.1 | convolution fusion | flops 19984842752 | bytes 32563200 | tf_op jit(solution)/shard_map/dot_general | solution.py:121
  2155.3 25.2 fusion.125
  2180.5 217.4 %fusion.175 = (bf16[2312,1024]{1,0:T(8,128)(2,1)}, bf16[2312,1024]{1,0:T(8,128)(2,1)}) fusion(bf16[4616,1024]{1,0:T(8,128)(2,1)} %fusion.125, bf16[4616,1024]{1,0:T(8,128)(2,1)} %bitcast_convert_fusion), kind=kCustom, calls=%all-reduce-scatter.5 | all-reduce-scatter fusion | flops 9469953 | bytes 28377600
  2413.3 23.6 concatenate.13
  2456.5 59.0 %all-reduce.26 = (bf16[1024]{0:T(1024)(128)(2,1)S(1)}, bf16[1024]{0:T(1024)(128)(2,1)S(1)}, bf16[1024]{0:T(1024)(128)(2,1)S(1)}, bf16[2,8,64]{1,0,2:T(2,128)(2,1...) all-reduce(bf16[1024]{0:T(1024)(128)(2,1)S(1)} %copy-done.34, ...), channel_id=1, replica_groups=mesh['dp'=16,'tensor'=2] {'dp'}, use_global_device_ids=true, to_apply=%add.5 | all-reduce | flops 10240 | bytes 40960
  2520.4 23.3 concatenate.10
  (476 shorter events, 1141.9 us)
Async XLA Ops:
  7.2 196.7 %all-gather.23.cloned.1.call-start = ((), (), s32[]{:S(2)}) async-start(), calls=%async_computation.10 | async-start | bytes 14204928 | tf_op jit(solution)/shard_map/all_gather | solution.py:67
  88.1 163.2 %all-gather.15.cloned.1.call-start = ((), (), s32[]{:S(2)}) async-start(), calls=%async_computation.3 | async-start | bytes 3342336 | tf_op jit(solution)/shard_map/all_gather | solution.py:166
  88.8 310.7 %all-gather.17.cloned.1.call-start = ((), (), s32[]{:S(2)}) async-start(), calls=%async_computation.4 | async-start | bytes 1114112 | tf_op jit(solution)/shard_map/all_gather | solution.py:168
  89.5 629.6 %all-gather.29.cloned.1.call-start = ((), (), s32[]{:S(2)}) async-start(), calls=%async_computation.13 | async-start | bytes 14204928 | tf_op jit(solution)/shard_map/all_gather | solution.py:71
  97.4 641.1 %all-gather.27.cloned.1.call-start = ((), (), s32[]{:S(2)}) async-start(), calls=%async_computation.12 | async-start | bytes 14204928 | tf_op jit(solution)/shard_map/all_gather | solution.py:67
  409.7 117.7 %copy-start.40 = (bf16[1024]{0:T(1024)(128)(2,1)S(1)}, bf16[1024]{0:T(1024)(128)(2,1)}, u32[]{:S(2)}) copy-start(bf16[1024]{0:T(1024)(128)(2,1)} %get-tuple-element.213) | copy-start | bytes 6148
  409.7 117.7 %copy-start.39 = (bf16[1024]{0:T(1024)(128)(2,1)S(1)}, bf16[1024]{0:T(1024)(128)(2,1)}, u32[]{:S(2)}) copy-start(bf16[1024]{0:T(1024)(128)(2,1)} %get-tuple-element.212) | copy-start | bytes 6148
  523.6 3.8 collective-permute-start.2
  567.5 180.2 %all-gather.19.cloned.1.call-start = ((), (), s32[]{:S(2)}) async-start(), calls=%async_computation.5 | async-start | bytes 4456448 | tf_op jit(solution)/shard_map/all_gather | solution.py:172
  568.0 314.7 %all-gather.21.cloned.1.call-start = ((), (), s32[]{:S(2)}) async-start(), calls=%async_computation.6 | async-start | bytes 4456448 | tf_op jit(solution)/shard_map/all_gather | solution.py:174
  568.8 743.3 %reduce-scatter.19.cloned.1.call-start = ((), (), s32[]{:S(2)}) async-start(), calls=%async_computation.9 | async-start | bytes 4456448 | tf_op jit(solution)/shard_map/reduce_scatter | solution.py:308
  588.3 294.5 %copy-start.35 = (f32[2048]{0:T(1024)}, f32[2048]{0:T(1024)S(1)}, u32[]{:S(2)}) copy-start(f32[2048]{0:T(1024)S(1)} %bitcast_convert_fusion.1) | copy-start | bytes 24580
  882.7 431.2 %reduce-scatter.17.cloned.1.call-start = ((), (), s32[]{:S(2)}) async-start(), calls=%async_computation.8 | async-start | bytes 4456448 | tf_op jit(solution)/shard_map/reduce_scatter | solution.py:302
  955.5 470.2 %all-gather.31.cloned.1.call-start = ((), (), s32[]{:S(2)}) async-start(), calls=%async_computation.14 | async-start | bytes 14204928 | tf_op jit(solution)/shard_map/all_gather | solution.py:71
  1201.4 5.7 collective-permute-start
  1205.8 24.8 collective-permute-start.3
  1309.8 733.1 %all-gather.25.cloned.1.call-start = ((), (), s32[]{:S(2)}) async-start(), calls=%async_computation.11 | async-start | bytes 14204928 | tf_op jit(solution)/shard_map/all_gather | solution.py:67
  1312.0 123.2 %copy-start.33 = (bf16[1024]{0:T(1024)(128)(2,1)}, bf16[1024]{0:T(1024)(128)(2,1)S(1)}, u32[]{:S(2)}) copy-start(bf16[1024]{0:T(1024)(128)(2,1)S(1)} %dynamic-update-slice.5) | copy-start | bytes 6148
  1312.0 1249.8 %all-reduce.32.cloned.1.call-start = ((), (), s32[]{:S(2)}) async-start(), calls=%async_computation.15 | async-start | bytes 8388608
  1315.8 119.5 %copy-start.46 = (bf16[512,1024]{0,1:T(8,128)(2,1)S(1)}, bf16[512,1024]{0,1:T(8,128)(2,1)}, u32[]{:S(2)}) copy-start(bf16[512,1024]{0,1:T(8,128)(2,1)} %all-gather.17.cloned.1.call-done) | copy-start | bytes 3145732
  2022.3 541.4 %reduce-scatter.15.cloned.1.call-start = ((), (), s32[]{:S(2)}) async-start(), calls=%async_computation.7 | async-start | bytes 1114112 | tf_op jit(solution)/shard_map/reduce_scatter | solution.py:290
  2180.5 217.4 %copy-start.30 = (bf16[3,512]{1,0:T(4,128)(2,1)S(1)}, bf16[3,512]{1,0:T(4,128)(2,1)}, u32[]{:S(2)}) copy-start(bf16[3,512]{1,0:T(4,128)(2,1)} %reduce.2) | copy-start | bytes 9220
  2398.6 14.6 collective-permute-start.4
  2411.9 108.5 %collective-permute-start.1 = (bf16[4,1024]{1,0:T(4,128)(2,1)S(1)}, bf16[4,1024]{1,0:T(4,128)(2,1)S(1)}, u32[]{:S(2)}, u32[]{:S(2)}) collective-permute-start(bf16[4,1024]{1,0:T(4,128)(2,1)S(1)} %slice.69), channel_id=1, source_target_pairs={{0,1},{2,3},{4,5},{6,7},{8,9},{10,11},{12,13},{14,15},{16,17},{18,... | collective-permute-start | bytes 24584
  (55 other events, 1236.8 us)
Sparse Core Ops, SparseCore 0:
  88.2 115.6 all-gather.22
  206.0 45.1 all-gather.14
  253.5 36.7 all-gather.16
  292.2 117.2 all-gather.28
  567.6 118.0 all-gather.26
  687.7 50.7 all-gather.18
  740.6 49.0 all-gather.20
  882.8 70.7 reduce-scatter.18
  958.0 71.3 reduce-scatter.16
  1309.9 115.6 all-gather.30
  1427.8 118.3 all-gather.24
  2022.5 111.5 all-reduce.31
  2413.3 57.4 reduce-scatter.14
where the time goes:
time: 2580 us; the launch traced here: 2570 us
  matrix products  1020 us (40%)
  blocking collectives  715 us (28%)
  local copies, waits for them, and re-layouts  402 us (16%)
  waiting for transfers between devices  239 us (9%)
  other arithmetic  162 us (6%)
    unnamed x5, blocking collectives  671 us
    dot_general x2, matrix products, forward(): jnp.dot(gathered_two, expand_weight, preferred_element_type=jnp.float32)  204 us
    unnamed x139, local copies, waits for them, and re-layouts  183 us
    dot_general x8, matrix products, attend_back(): jnp.einsum('hqk,khd->qhd', grad_scores, keys, preferred_element_type=jnp....  166 us
    dot_general x8, matrix products, attend_back(): jnp.einsum('hqk,qhd->khd', grad_scores, query, preferred_element_type=jnp...  165 us
    all_gather x2, waiting for transfers between devices, gather_grads(): return lax.all_gather(values, 'tensor', axis=0, tiled=True)  110 us
    all_gather x3, waiting for transfers between devices, gather_rows(): return lax.all_gather(values, 'tensor', axis=0, tiled=True)  88.5 us
    dot_general x16, matrix products, attend(): jnp.einsum('hqk,khd->qhd', probs, values, preferred_element_type=jnp.floa...  68.5 us
  transfers between devices with their start and end apart: 18, of which 3 were waited for; matrix products, arithmetic and copies ran while one was open for 81% of the time, Pallas kernels for 0%

commit v1 on v0

v1 whole, which is shorter than its diff:
```python
import functools

import jax
import jax.numpy as jnp
from jax import lax
from jax.experimental import pallas as pl
from jax.experimental.pallas import tpu as pltpu
from jax.sharding import PartitionSpec as P

HEAD_DIM = 64
SEQ = 577
PAD = 592
EPSILON = 1e-06
LOG_SCALE = 0.125
bf16 = jnp.bfloat16
f32 = jnp.float32
NN = (((1,), (0,)), ((), ()))
NT = (((1,), (1,)), ((), ()))
TN = (((0,), (0,)), ((), ()))
VMEM_BYTES = 60 * 2**20
AXES = ("tensor", "dp")


def matmul(left, right, dims=NN):
    return lax.dot_general(left, right, dims, preferred_element_type=f32)


def norm_parts(values):
    center = values - jnp.mean(values, axis=-1, keepdims=True)
    second = jnp.mean(center * center, axis=-1, keepdims=True)
    inv = lax.rsqrt(second + EPSILON)
    return center * inv, inv


def gelu_and_slope(pre):
    size = jnp.abs(pre)
    bell = jnp.exp(pre * pre * -0.5)
    t = 1.0 / (1.0 + size * (0.3275911 * 0.7071067811865476))
    poly = t * (
        0.254829592
        + t * (-0.284496736 + t * (1.421413741 + t * (-1.453152027 + t * 1.061405429)))
    )
    tail = (0.5 * poly) * bell
    phi = jnp.where(pre >= 0, 1.0 - tail, tail)
    return pre * phi, phi + pre * (bell * 0.3989422804014327)


def full(shape):
    return pl.BlockSpec(shape, lambda *_: (0,) * len(shape), pipeline_mode=pl.Buffered(1))


def call(kernel, name, grid, in_specs, out_specs, out_shape, args, scratch=()):
    return pl.pallas_call(
        kernel,
        grid=grid,
        in_specs=in_specs,
        out_specs=out_specs,
        out_shape=[jax.ShapeDtypeStruct(s, d) for s, d in out_shape],
        scratch_shapes=list(scratch),
        compiler_params=pltpu.CompilerParams(vmem_limit_bytes=VMEM_BYTES),
        name=name,
    )(*args)


def qkv_kernel(x_ref, gain_ref, shift_ref, bias_ref, w_ref, normed_ref, triple_ref):
    hat, _ = norm_parts(x_ref[...].astype(f32))
    normed = (hat * gain_ref[...] + shift_ref[...]).astype(bf16)
    normed_ref[...] = normed
    tensor, dp, rows, _ = w_ref.shape
    width = w_ref.shape[3] // 3
    for s in range(3):
        for t in range(tensor):
            cols = slice(t * width, (t + 1) * width)
            w = w_ref[t, :, :, s * width : (s + 1) * width].reshape(dp * rows, width)
            out = matmul(normed, w)
            if s != 1:
                out = out + bias_ref[s // 2 : s // 2 + 1, cols]
            triple_ref[s, :, cols] = out.astype(bf16)


def attend_kernel(triple_ref, context_ref, stat_ref):
    rows = lax.broadcasted_iota(jnp.int32, (PAD, 1), 0)
    mask = jnp.where(rows < SEQ, 0.0, -1e30)
    for h in range(triple_ref.shape[2] // HEAD_DIM):
        cols = slice(HEAD_DIM * h, HEAD_DIM * (h + 1))
        query = triple_ref[0, :, cols] * bf16(LOG_SCALE)
        scores = matmul(triple_ref[1, :, cols], query, NT) + mask
        top = jnp.max(scores, axis=0, keepdims=True)
        expo = jnp.exp(scores - top)
        total = jnp.sum(expo, axis=0, keepdims=True)
        probs = (expo * (1.0 / total)).astype(bf16)
        context_ref[:, cols] = matmul(probs, triple_ref[2, :, cols], TN).astype(bf16)
        stat_ref[0, h : h + 1, :] = top + jnp.log(total)


def attend_back_kernel(triple_ref, stat_ref, grad_ref, out_ref):
    rows = lax.broadcasted_iota(jnp.int32, (PAD, 1), 0)
    mask = jnp.where(rows < SEQ, 0.0, -1e30)
    for h in range(triple_ref.shape[2] // HEAD_DIM):
        cols = slice(HEAD_DIM * h, HEAD_DIM * (h + 1))
        query = triple_ref[0, :, cols]
        keys = triple_ref[1, :, cols]
        grad = grad_ref[:, cols]
        scores = matmul(keys, query * bf16(LOG_SCALE), NT) + mask
        probs = jnp.exp(scores - stat_ref[0, h : h + 1, :])
        grad_probs = matmul(triple_ref[2, :, cols], grad, NT)
        inner = jnp.sum(probs * grad_probs, axis=0, keepdims=True)
        grad_scores = (probs * (grad_probs - inner) * LOG_SCALE).astype(bf16)
        out_ref[2, :, cols] = matmul(probs.astype(bf16), grad).astype(bf16)
        out_ref[1, :, cols] = matmul(grad_scores, query).astype(bf16)
        out_ref[0, :, cols] = matmul(grad_scores, keys, TN).astype(bf16)


def merge_kernel(ctx_ref, x_ref, bias_ref, gain_ref, shift_ref, w_ref, resid_ref, normed_ref):
    tensor, dp, rows, width = w_ref.shape
    total = x_ref[...].astype(f32) + bias_ref[...]
    for t in range(tensor):
        w = w_ref[t].reshape(dp * rows, width)
        total = total + matmul(ctx_ref[:, t * width : (t + 1) * width], w, NT)
    resid_ref[...] = total
    hat, _ = norm_parts(total)
    normed_ref[...] = (hat * gain_ref[...] + shift_ref[...]).astype(bf16)


def mlp_kernel(chunk, normed_ref, resid_ref, ebias_ref, rbias_ref, e_ref, r_ref, out_ref, act_ref, slope_ref):
    tensor, dp, rows, width = e_ref.shape
    normed = normed_ref[...]
    total = resid_ref[...] + rbias_ref[...]
    for t in range(tensor):
        for c in range(width // chunk):
            local = slice(c * chunk, (c + 1) * chunk)
            cols = slice(t * width + c * chunk, t * width + (c + 1) * chunk)
            e = e_ref[t, :, :, local].reshape(dp * rows, chunk)
            active, slope = gelu_and_slope(matmul(normed, e) + ebias_ref[:, cols])
            active = active.astype(bf16)
            act_ref[:, cols] = active
            slope_ref[:, cols] = slope.astype(bf16)
            r = r_ref[t, :, :, local].reshape(dp * rows, chunk)
            total = total + matmul(active, r, NT)
    out_ref[...] = total.astype(bf16)


def accumulate(first, ref, value):
    @pl.when(first)
    def _():
        ref[...] = value

    @pl.when(jnp.logical_not(first))
    def _():
        ref[...] += value


def norm_back(values, gain, grad):
    hat, inv = norm_parts(values)
    scaled = grad * gain
    back = (
        scaled
        - jnp.mean(scaled, axis=-1, keepdims=True)
        - hat * jnp.mean(scaled * hat, axis=-1, keepdims=True)
    ) * inv
    return back, jnp.sum(grad * hat, axis=0, keepdims=True), jnp.sum(grad, axis=0, keepdims=True)


def mlp_back_kernel(
    chunk, grad_ref, slope_ref, resid_ref, gain_ref, e_ref, r_ref, m_ref,
    pre_ref, low_ref, ctx_ref, sums_ref, esum_ref,
):
    tensor, dp, rows, width = e_ref.shape
    first = pl.program_id(0) == 0
    grad = grad_ref[...]
    total = jnp.zeros(grad.shape, f32)
    parts = []
    for t in range(tensor):
        for c in range(width // chunk):
            local = slice(c * chunk, (c + 1) * chunk)
            cols = slice(t * width + c * chunk, t * width + (c + 1) * chunk)
            r = r_ref[t, :, :, local].reshape(dp * rows, chunk)
            pre = (matmul(grad, r) * slope_ref[:, cols].astype(f32)).astype(bf16)
            pre_ref[:, cols] = pre
            parts.append(jnp.sum(pre.astype(f32), axis=0, keepdims=True))
            e = e_ref[t, :, :, local].reshape(dp * rows, chunk)
            total = total + matmul(pre, e, NT)
    grad = grad.astype(f32)
    back, gain_sum, shift_sum = norm_back(resid_ref[...], gain_ref[...], total)
    resid_grad = grad + back
    low = resid_grad.astype(bf16)
    low_ref[...] = low
    wide = m_ref.shape[3]
    for t in range(tensor):
        m = m_ref[t].reshape(dp * rows, wide)
        ctx_ref[:, t * wide : (t + 1) * wide] = matmul(low, m).astype(bf16)
    sums = jnp.concatenate(
        [
            jnp.sum(grad, axis=0, keepdims=True),
            gain_sum,
            shift_sum,
            jnp.sum(resid_grad, axis=0, keepdims=True),
        ],
        axis=0,
    )
    accumulate(first, sums_ref, sums)
    accumulate(first, esum_ref, jnp.concatenate(parts, axis=1))


def qkv_back_kernel(x_ref, low_ref, gain_ref, grad_ref, w_ref, out_ref, sums_ref, bsum_ref):
    tensor, dp, rows, _ = w_ref.shape
    width = w_ref.shape[3] // 3
    first = pl.program_id(0) == 0
    total = jnp.zeros(x_ref.shape, f32)
    for s in range(3):
        for t in range(tensor):
            w = w_ref[t, :, :, s * width : (s + 1) * width].reshape(dp * rows, width)
            total = total + matmul(grad_ref[s, :, t * width : (t + 1) * width], w, NT)
    back, gain_sum, shift_sum = norm_back(x_ref[...].astype(f32), gain_ref[...], total)
    out_ref[...] = (low_ref[...].astype(f32) + back).astype(bf16)
    accumulate(first, sums_ref, jnp.concatenate([gain_sum, shift_sum], axis=0))
    bias = [jnp.sum(grad_ref[s].astype(f32), axis=0, keepdims=True) for s in (0, 2)]
    accumulate(first, bsum_ref, jnp.concatenate(bias, axis=0))


def weight_grad_kernel(left_ref, right_ref, out_ref, turned):
    @pl.when(pl.program_id(0) == 0)
    def _():
        turned[...] = left_ref[...].T

    out = matmul(turned[...], right_ref[...].reshape(right_ref.shape[-2:]))
    out_ref[...] = out.astype(bf16).reshape(out_ref.shape)


def weight_grad(name, left, right, tensor, dp, block):
    count, rows, width = right.shape
    deep = left.shape[1]
    local = width // tensor
    block = min(block, local)
    per = local // block
    steps = count * tensor * per

    def where(i):
        return i // (tensor * per), (i // per) % tensor, i % per

    def right_map(i):
        s, t, b = where(i)
        return (s, 0, t * per + b)

    def out_map(i):
        s, t, b = where(i)
        return (t, 0, 0, s * per + b)

    return call(
        weight_grad_kernel,
        name,
        (steps,),
        [full((rows, deep)), pl.BlockSpec((1, rows, block), right_map)],
        [pl.BlockSpec((1, dp, deep // dp, block), out_map)],
        [((tensor, dp, deep // dp, count * local), bf16)],
        (left, right),
        [pltpu.VMEM((deep, rows), bf16)],
    )[0]


def shards(
    tensor,
    dp,
    activations,
    first_gain,
    first_shift,
    heads_weight,
    heads_bias,
    merge_weight,
    merge_bias,
    second_gain,
    second_shift,
    expand_weight,
    expand_bias,
    reduce_weight,
    reduce_bias,
    output_grad,
    real_images,
):
    rows, deep = activations.shape
    images = rows // SEQ
    part = deep // dp
    own = heads_weight.shape[2]
    hidden_own = expand_weight.shape[1]
    hidden = hidden_own * tensor
    heads = deep // HEAD_DIM

    def gather(shard):
        out = lax.all_gather(shard, AXES, axis=0, tiled=True)
        return out.reshape(tensor, dp, *shard.shape)

    small_parts = [
        first_gain, first_shift, merge_bias, second_gain, second_shift, reduce_bias,
        heads_bias.reshape(-1), expand_bias.reshape(-1),
    ]
    small = gather(jnp.concatenate(small_parts)[None, :])[:, :, 0]
    wide_heads = gather(heads_weight.transpose(1, 0, 2).reshape(part, 3 * own))
    wide_merge = gather(merge_weight.T)
    wide_expand = gather(expand_weight)
    wide_reduce = gather(reduce_weight.T)

    vectors = small[0, :, : 6 * part].astype(f32).reshape(dp, 6, part)
    vectors = vectors.transpose(1, 0, 2).reshape(6, 1, deep)
    gain_one, shift_one, merge_shift, gain_two, shift_two, reduce_shift = vectors
    hb = small[:, :, 6 * part : 6 * part + heads_bias.size].astype(f32)
    hb = hb.reshape((tensor, dp) + heads_bias.shape).transpose(2, 0, 3, 1, 4).reshape(2, deep)
    eb = small[:, :, 6 * part + heads_bias.size :].astype(f32)
    eb = eb.reshape((tensor, dp) + expand_bias.shape).transpose(0, 2, 1, 3).reshape(1, hidden)

    def padded(values):
        values = values.reshape(images, SEQ, deep)
        return jnp.pad(values, ((0, 0), (0, PAD - SEQ), (0, 0))).reshape(images * PAD, deep)

    def unpadded(values):
        return values.reshape(images, PAD, deep)[:, :SEQ].reshape(rows, deep)

    full_rows = images * PAD
    inputs = padded(activations)
    ids = lax.axis_index("tensor") * images + lax.iota(jnp.int32, images)
    live = (ids < real_images[0]).astype(bf16)
    grad = padded((output_grad.reshape(images, SEQ, deep) * live[:, None, None]).reshape(rows, deep))

    def by_rows(width, block=PAD):
        return pl.BlockSpec((block, width), lambda i: (i, 0))

    vec = full((1, deep))
    triple_spec = pl.BlockSpec((3, PAD, deep), lambda i: (0, i, 0))
    normed_one, triple = call(
        qkv_kernel,
        "qkv",
        (images,),
        [by_rows(deep), vec, vec, full((2, deep)), full(wide_heads.shape)],
        [by_rows(deep), triple_spec],
        [((full_rows, deep), bf16), ((3, full_rows, deep), bf16)],
        (inputs, gain_one, shift_one, hb, wide_heads),
    )

    group = 4
    groups = heads // group
    head_spec = pl.BlockSpec((3, PAD, group * HEAD_DIM), lambda i, g: (0, i, g))
    ctx_spec = pl.BlockSpec((PAD, group * HEAD_DIM), lambda i, g: (i, g))
    stat_spec = pl.BlockSpec((1, group, PAD), lambda i, g: (i * groups + g, 0, 0))
    context, stat = call(
        attend_kernel,
        "attend",
        (images, groups),
        [head_spec],
        [ctx_spec, stat_spec],
        [((full_rows, deep), bf16), ((images * groups, group, PAD), f32)],
        (triple,),
    )

    resid, normed_two = call(
        merge_kernel,
        "merge",
        (images,),
        [by_rows(deep), by_rows(deep), vec, vec, vec, full(wide_merge.shape)],
        [by_rows(deep), by_rows(deep)],
        [((full_rows, deep), f32), ((full_rows, deep), bf16)],
        (context, inputs, merge_shift, gain_two, shift_two, wide_merge),
    )

    chunk = min(512, hidden_own)
    half = PAD // 2
    output, active, slope = call(
        functools.partial(mlp_kernel, chunk),
        "mlp",
        (full_rows // half,),
        [
            by_rows(deep, half), by_rows(deep, half), full((1, hidden)), vec,
            full(wide_expand.shape), full(wide_reduce.shape),
        ],
        [by_rows(deep, half), by_rows(hidden, half), by_rows(hidden, half)],
        [((full_rows, deep), bf16), ((full_rows, hidden), bf16), ((full_rows, hidden), bf16)],
        (normed_two, resid, eb, reduce_shift, wide_expand, wide_reduce),
    )

    def scatter(grads):
        grads = grads.reshape(tensor * dp * grads.shape[2], grads.shape[3])
        return lax.psum_scatter(grads, AXES, scatter_dimension=0, tiled=True)

    def gradient(name, left, right, block=512):
        return scatter(weight_grad(name, left, right, tensor, dp, block))

    grad_reduce = gradient("grad_reduce", grad, active[None])

    pre_grad, resid_low, grad_context, sums_two, esum = call(
        functools.partial(mlp_back_kernel, chunk),
        "mlp_back",
        (full_rows // half,),
        [
            by_rows(deep, half), by_rows(hidden, half), by_rows(deep, half), vec,
            full(wide_expand.shape), full(wide_reduce.shape), full(wide_merge.shape),
        ],
        [
            by_rows(hidden, half), by_rows(deep, half), by_rows(deep, half),
            pl.BlockSpec((4, deep), lambda i: (0, 0)), pl.BlockSpec((1, hidden), lambda i: (0, 0)),
        ],
        [
            ((full_rows, hidden), bf16), ((full_rows, deep), bf16), ((full_rows, deep), bf16),
            ((4, deep), f32), ((1, hidden), f32),
        ],
        (grad, slope, resid, gain_two, wide_expand, wide_reduce, wide_merge),
    )
    grad_expand = gradient("grad_expand", normed_two, pre_grad[None])
    grad_merge = gradient("grad_merge", resid_low, context[None])

    grad_triple = call(
        attend_back_kernel,
        "attend_back",
        (images, groups),
        [head_spec, stat_spec, ctx_spec],
        [head_spec],
        [((3, full_rows, deep), bf16)],
        (triple, stat, grad_context),
    )[0]
    grad_heads = gradient("grad_heads", normed_one, grad_triple)

    input_grad, sums_one, bsum = call(
        qkv_back_kernel,
        "qkv_back",
        (images,),
        [by_rows(deep), by_rows(deep), vec, triple_spec, full(wide_heads.shape)],
        [by_rows(deep), pl.BlockSpec((2, deep), lambda i: (0, 0)), pl.BlockSpec((2, deep), lambda i: (0, 0))],
        [((full_rows, deep), bf16), ((2, deep), f32), ((2, deep), f32)],
        (inputs, resid_low, gain_one, grad_triple, wide_heads),
    )

    shared = jnp.concatenate([sums_one, sums_two[3:], sums_two[1:3], sums_two[:1]], axis=0)
    shared = shared.reshape(6, dp, part).transpose(1, 0, 2).reshape(1, dp, 6 * part)
    shared = jnp.broadcast_to(shared, (tensor, dp, 6 * part))
    hbs = heads_bias.shape
    bsum = bsum.reshape(2, tensor, hbs[1], dp, hbs[2]).transpose(1, 3, 0, 2, 4)
    ebs = expand_bias.shape
    esum = esum.reshape(tensor, ebs[0], dp, ebs[1]).transpose(0, 2, 1, 3)
    packed = jnp.concatenate(
        [shared, bsum.reshape(tensor, dp, -1), esum.reshape(tensor, dp, -1)], axis=2
    )
    packed = lax.psum_scatter(
        packed.reshape(tensor * dp, -1), AXES, scatter_dimension=0, tiled=True
    )[0]
    vector = packed[: 6 * part].reshape(6, part)
    hb_grad = packed[6 * part : 6 * part + heads_bias.size].reshape(hbs)
    eb_grad = packed[6 * part + heads_bias.size :].reshape(ebs)

    return (
        unpadded(output),
        unpadded(input_grad),
        vector[0],
        vector[1],
        grad_heads.astype(f32).reshape(part, 3, own).transpose(1, 0, 2),
        hb_grad,
        grad_merge.astype(f32).T,
        vector[2],
        vector[3],
        vector[4],
        grad_expand.astype(f32),
        eb_grad,
        grad_reduce.astype(f32).T,
        vector[5],
    )


def solution(mesh):
    rows = P(("dp", "tensor"), None)
    specs = (
        P("dp"),
        P("dp"),
        P(None, "dp", "tensor"),
        P(None, "tensor", "dp"),
        P("tensor", "dp"),
        P("dp"),
        P("dp"),
        P("dp"),
        P("dp", "tensor"),
        P("tensor", "dp"),
        P("tensor", "dp"),
        P("dp"),
    )
    return jax.shard_map(
        functools.partial(shards, mesh.shape["tensor"], mesh.shape["dp"]),
        mesh=mesh,
        in_specs=(rows,) + specs + (rows, P("dp")),
        out_specs=(rows, rows) + specs,
        check_vma=False,
    )
```

time: 2580 us -> 1260 us (0.49)
  matrix products: 1020 us -> 0 us
  blocking collectives: 715 us -> 43 us
  Pallas kernels: 0 us -> 450 us
  waiting for transfers between devices: 239 us -> 677 us
  local copies, waits for them, and re-layouts: 402 us -> 62.2 us
  other arithmetic: 162 us -> 10.8 us
    dot_general x78 -> x0, matrix products: 969 us -> none  [the longest x2 204 us: forward(): jnp.dot(gathered_two, expand_weight, preferred_element_type=jnp.float32)]
    unnamed x5 -> x1, blocking collectives: 671 us -> 43 us
    reduce_scatter x3 -> x4, waiting for transfers between devices: 0.02 us -> 545 us  [scatter(): return lax.psum_scatter(grads, AXES, scatter_dimension=0, tiled=True)]
    pallas_call x0 -> x11, Pallas kernels: none -> 450 us  [call(): pl.pallas_call(kernel, grid=grid, in_specs=in_specs, out_specs=out_specs,...]
    unnamed x139 -> x26, local copies, waits for them, and re-layouts: 183 us -> 3.35 us
    all_gather x9 -> x4, waiting for transfers between devices: 237 us -> 126 us  [gather(): out = lax.all_gather(shard, AXES, axis=0, tiled=True)]
    reduce_sum x18 -> x0, other arithmetic: 104 us -> none  [the longest x4 43.4 us: normalize(): return center * lax.rsqrt(second + EPSILON) * gain + shift]
    while x18 -> x0, local copies, waits for them, and re-layouts: 73.3 us -> none
  transfers between devices with their start and end apart: 18 -> 9, of which waited for: 3 -> 7; matrix products, arithmetic and copies ran while one was open for 81% -> 5% of each run, Pallas kernels for 0% -> 14%
where the time goes in v1:
time: 1260 us
  waiting for transfers between devices  677 us (54%)
  Pallas kernels  450 us (36%)
  local copies, waits for them, and re-layouts  62.2 us (5%)
  blocking collectives  43 us (3%)
  between operations  15.7 us (1%)
    reduce_scatter x4, waiting for transfers between devices, scatter(): return lax.psum_scatter(grads, AXES, scatter_dimension=0, tiled=True)  545 us
    pallas_call x11, Pallas kernels, call(): pl.pallas_call(kernel, grid=grid, in_specs=in_specs, out_specs=out_specs,...  450 us
    all_gather x4, waiting for transfers between devices, gather(): out = lax.all_gather(shard, AXES, axis=0, tiled=True)  126 us
    unnamed x1, blocking collectives  43 us
  transfers between devices with their start and end apart: 9, of which 7 were waited for; matrix products, arithmetic and copies ran while one was open for 5% of the time, Pallas kernels for 14%

profile of v1, /device:TPU:0, one launch (start us, length us, event | category | flops | bytes accessed | tf_op | source)
XLA Modules:
  0.0 1259.0 jit_solution(10596845768295624015)
XLA Ops:
  11.0 5.8 reshape.174
  17.2 5.3 pad.7
  24.2 43.0 %all-reduce.2 = bf16[18432]{0:T(1024)(128)(2,1)S(1)} all-reduce(bf16[18432]{0:T(1024)(128)(2,1)S(1)} %dynamic-update-slice), channel_id=2, replica_groups=mesh['dp'=16,'tensor'=2] {'tensor','dp'}, use_global_device_ids=true, to_apply=%add.2 | all-reduce | flops 18432 | bytes 73728
  73.7 5.9 reshape.191
  86.1 23.0 %qkv.1 = (bf16[2368,1024]{1,0:T(8,128)(2,1)}, bf16[3,2368,1024]{2,1,0:T(8,128)(2,1)}) custom-call(bf16[2368,1024]{1,0:T(8,128)(2,1)} %bitcast.62, f32[1,1024]{1,0:T(1,128)} %unstack.37.gain_ref, f32[1,1024]{1,0:T(1,128)} %unstack.39.shift_ref, f32[2,1024]{1,0:T(2,128)} %reshape.206.bias_ref, bf16[2,16,64,1536]{3,2,1,0:T(8,128)(2,1)} %bitcast.74), custom_call_target="tpu_custom_call" | custom-call | tf_op jit(solution)/shard_map/qkv/pallas_call | solution.py:53
  109.0 52.3 %attend.1 = (bf16[2368,1024]{1,0:T(8,128)(2,1)}, f32[16,4,592]{2,1,0:T(4,128)}) custom-call(bf16[3,2368,1024]{2,1,0:T(8,128)(2,1)} %get-tuple-element.31.triple_ref), custom_call_target="tpu_custom_call" | custom-call | tf_op jit(solution)/shard_map/attend/pallas_call | solution.py:53
  161.3 13.1 %merge.1 = (f32[2368,1024]{1,0:T(8,128)}, bf16[2368,1024]{1,0:T(8,128)(2,1)}) custom-call(bf16[2368,1024]{1,0:T(8,128)(2,1)} %get-tuple-element.32.ctx_ref, bf16[2368,1024]{1,0:T(8,128)(2,1)} %bitcast.63, f32[1,1024]{1,0:T(1,128)} %unstack.41.bias_ref, f32[1,1024]{1,0:T(1,128)} %unstack.43.gain_ref, f32[1,1024]{1,0:T(1,128)} %unstack.45.shift_ref, ...), custom_call_target="tpu_custom_call" | custom-call | tf_op jit(solution)/shard_map/merge/pallas_call | solution.py:53
  174.4 47.0 %all-gather.10.cloned.1.call-done = bf16[2048,2048]{1,0:T(8,128)(2,1)} async-done(((bf16[64,2048]{1,0:T(8,128)(2,1)}), bf16[2048,2048]{1,0:T(8,128)(2,1)}) %all-gather.10.cloned.1.call-update) | async-done | bytes 8388624 | tf_op jit(solution)/shard_map/all_gather | solution.py:289
  221.4 78.8 %all-gather.12.cloned.1.call-done = bf16[2048,2048]{1,0:T(8,128)(2,1)} async-done(((bf16[64,2048]{1,0:T(8,128)(2,1)}), bf16[2048,2048]{1,0:T(8,128)(2,1)}) %all-gather.12.cloned.1.call-update) | async-done | bytes 8388624 | tf_op jit(solution)/shard_map/all_gather | solution.py:289
  300.2 81.3 %mlp.1 = (bf16[2368,1024]{1,0:T(8,128)(2,1)}, bf16[2368,4096]{1,0:T(8,128)(2,1)}, bf16[2368,4096]{1,0:T(8,128)(2,1)}) custom-call(bf16[2368,1024]{1,0:T(8,128)(2,1)} %get-tuple-element.33.normed_ref.left_ref, f32[2368,1024]{1,0:T(8,128)} %get-tuple-element.34.resid_ref, f32[1,4096]{1,0:T(1,128)} %reshape.208.ebias_ref, f32[1,1024]{1,0:T(1,128)} %unstack.47.rbias_ref, ...), custom_call_target="tpu_custom_call" | custom-call | tf_op jit(solution)/shard_map/mlp/pallas_call | solution.py:53
  381.5 68.5 %mlp_back.1 = (bf16[2368,4096]{1,0:T(8,128)(2,1)}, bf16[2368,1024]{1,0:T(8,128)(2,1)}, bf16[2368,1024]{1,0:T(8,128)(2,1)}, f32[4,1024]{1,0:T(4,128)}, f32[1,4096]{1,0:T(1,128)}) custom-call(bf16[2368,1024]{1,0:T(8,128)(2,1)} %bitcast.65, bf16[2368,4096]{1,0:T(8,128)(2,1)} %get-tuple-element.36.slope_ref, f32[2368,1024]{1,0:T(8,128)} %get-tuple-element.34.resid_ref, ...), custom_call_target="tpu_custom_call" | custom-call | tf_op jit(solution)/shard_map/mlp_back/pallas_call | solution.py:53
  454.0 91.2 %attend_back.1.grad_ref.right_ref = bf16[3,2368,1024]{2,1,0:T(8,128)(2,1)} custom-call(bf16[3,2368,1024]{2,1,0:T(8,128)(2,1)} %get-tuple-element.31.triple_ref, f32[16,4,592]{2,1,0:T(4,128)} %get-tuple-element.38.stat_ref, bf16[2368,1024]{1,0:T(8,128)(2,1)} %get-tuple-element.39.grad_ref), custom_call_target="tpu_custom_call" | custom-call | tf_op jit(solution)/shard_map/attend_back/pallas_call | solution.py:53
  545.2 28.6 %qkv_back.1 = (bf16[2368,1024]{1,0:T(8,128)(2,1)}, f32[2,1024]{1,0:T(2,128)}, f32[2,1024]{1,0:T(2,128)}) custom-call(bf16[2368,1024]{1,0:T(8,128)(2,1)} %bitcast.64, bf16[2368,1024]{1,0:T(8,128)(2,1)} %get-tuple-element.37.low_ref.left_ref, f32[1,1024]{1,0:T(1,128)} %unstack.37.gain_ref, bf16[3,2368,1024]{2,1,0:T(8,128)(2,1)} %attend_back.1.grad_ref.right_ref, ...), custom_call_target="tpu_custom_call" | custom-call | tf_op jit(solution)/shard_map/qkv_back/pallas_call | solution.py:53
  577.0 11.2 grad_merge.1
  588.3 22.9 %grad_heads.1 = bf16[2,16,64,1536]{3,2,1,0:T(8,128)(2,1)} custom-call(bf16[2368,1024]{1,0:T(8,128)(2,1)} %get-tuple-element.45.left_ref, bf16[3,2368,1024]{2,1,0:T(8,128)(2,1)} %attend_back.1.grad_ref.right_ref), custom_call_target="tpu_custom_call" | custom-call | tf_op jit(solution)/shard_map/grad_heads/pallas_call | solution.py:53
  611.3 29.1 %grad_expand.1 = bf16[2,16,64,2048]{3,2,1,0:T(8,128)(2,1)} custom-call(bf16[2368,1024]{1,0:T(8,128)(2,1)} %get-tuple-element.33.normed_ref.left_ref, bf16[1,2368,4096]{2,1,0:T(8,128)(2,1)} %bitcast.77), custom_call_target="tpu_custom_call" | custom-call | tf_op jit(solution)/shard_map/grad_expand/pallas_call | solution.py:53
  640.5 28.9 %grad_reduce.1 = bf16[2,16,64,2048]{3,2,1,0:T(8,128)(2,1)} custom-call(bf16[2368,1024]{1,0:T(8,128)(2,1)} %bitcast.66, bf16[1,2368,4096]{2,1,0:T(8,128)(2,1)} %bitcast.76), custom_call_target="tpu_custom_call" | custom-call | tf_op jit(solution)/shard_map/grad_reduce/pallas_call | solution.py:53
  669.4 5.0 slice.89
  674.4 5.8 reshape.190
  685.2 5.8 reshape.194
  700.2 135.9 %reduce-scatter.7.cloned.1.call-done = bf16[64,512]{1,0:T(8,128)(2,1)} async-done(((bf16[2048,512]{1,0:T(8,128)(2,1)}), bf16[64,512]{1,0:T(8,128)(2,1)}) %reduce-scatter.7.cloned.1.call-update) | async-done | bytes 65552 | tf_op jit(solution)/shard_map/reduce_scatter | solution.py:380
  837.6 115.7 %reduce-scatter.5.cloned.1.call-done = bf16[64,1536]{1,0:T(8,128)(2,1)} async-done(((bf16[2048,1536]{1,0:T(8,128)(2,1)}), bf16[64,1536]{1,0:T(8,128)(2,1)}) %reduce-scatter.5.cloned.1.call-update) | async-done | bytes 196624 | tf_op jit(solution)/shard_map/reduce_scatter | solution.py:380
  955.4 147.8 %reduce-scatter.9.cloned.1.call-done = bf16[64,2048]{1,0:T(8,128)(2,1)} async-done(((bf16[2048,2048]{1,0:T(8,128)(2,1)}), bf16[64,2048]{1,0:T(8,128)(2,1)}) %reduce-scatter.9.cloned.1.call-update) | async-done | bytes 262160 | tf_op jit(solution)/shard_map/reduce_scatter | solution.py:380
  1105.0 145.4 %reduce-scatter.11.cloned.1.call-done = bf16[64,2048]{1,0:T(8,128)(2,1)} async-done(((bf16[2048,2048]{1,0:T(8,128)(2,1)}), bf16[64,2048]{1,0:T(8,128)(2,1)}) %reduce-scatter.11.cloned.1.call-update) | async-done | bytes 262160 | tf_op jit(solution)/shard_map/reduce_scatter | solution.py:380
  (99 shorter events, 46.0 us)
Async XLA Ops:
  7.2 78.9 %all-gather.6.cloned.1.call-start = ((), (), s32[]{:S(2)}) async-start(), calls=%async_computation.4 | async-start | bytes 6488064 | tf_op jit(solution)/shard_map/all_gather | solution.py:289
  8.9 152.5 %all-gather.8.cloned.1.call-start = ((), (), s32[]{:S(2)}) async-start(), calls=%async_computation.5 | async-start | bytes 2162688 | tf_op jit(solution)/shard_map/all_gather | solution.py:289
  9.6 211.8 %all-gather.10.cloned.1.call-start = ((), (), s32[]{:S(2)}) async-start(), calls=%async_computation.6 | async-start | bytes 8650752 | tf_op jit(solution)/shard_map/all_gather | solution.py:289
  10.4 289.8 %all-gather.12.cloned.1.call-start = ((), (), s32[]{:S(2)}) async-start(), calls=%async_computation.7 | async-start | bytes 8650752 | tf_op jit(solution)/shard_map/all_gather | solution.py:289
  10.4 6.4 copy-start
  10.4 6.6 copy-start.1
  10.9 684.2 %all-reduce.6.cloned.1.call-start = ((), (), s32[]{:S(2)}) async-start(), calls=%async_computation.12 | async-start | bytes 163840
  16.8 5.7 copy-start.2
  16.8 7.0 copy-start.3
  16.8 7.0 copy-start.4
  16.8 7.0 copy-start.5
  16.8 7.0 copy-start.6
  16.8 7.0 copy-start.7
  16.8 7.0 copy-start.8
  576.9 259.1 %reduce-scatter.7.cloned.1.call-start = ((), (), s32[]{:S(2)}) async-start(), calls=%async_computation.9 | async-start | bytes 2162688 | tf_op jit(solution)/shard_map/reduce_scatter | solution.py:380
  588.2 365.0 %reduce-scatter.5.cloned.1.call-start = ((), (), s32[]{:S(2)}) async-start(), calls=%async_computation.8 | async-start | bytes 6488064 | tf_op jit(solution)/shard_map/reduce_scatter | solution.py:380
  611.2 492.0 %reduce-scatter.9.cloned.1.call-start = ((), (), s32[]{:S(2)}) async-start(), calls=%async_computation.10 | async-start | bytes 8650752 | tf_op jit(solution)/shard_map/reduce_scatter | solution.py:380
  640.4 610.0 %reduce-scatter.11.cloned.1.call-start = ((), (), s32[]{:S(2)}) async-start(), calls=%async_computation.11 | async-start | bytes 8650752 | tf_op jit(solution)/shard_map/reduce_scatter | solution.py:380
Sparse Core Ops, SparseCore 0:
  11.5 72.8 all-gather.5
  87.2 54.9 all-gather.7
  145.0 76.3 all-gather.9
  224.1 76.0 all-gather.11
  577.1 118.0 all-reduce.5
  697.3 138.7 reduce-scatter.6
  842.6 110.5 reduce-scatter.4
  955.6 147.6 reduce-scatter.8
  1105.5 144.8 reduce-scatter.10

commit v2 on v1

v2 whole, which is shorter than its diff:
```python
import functools
import math

import jax
import jax.numpy as jnp
from jax import lax
from jax.experimental import pallas as pl
from jax.experimental.pallas import tpu as pltpu
from jax.sharding import PartitionSpec as P

HEAD_DIM = 64
SEQ = 577
STRIDE = 576
WINDOW = 592
EPSILON = 1e-06
LOG_SCALE = 0.125
bf16 = jnp.bfloat16
f32 = jnp.float32
NN = (((1,), (0,)), ((), ()))
NT = (((1,), (1,)), ((), ()))
TN = (((0,), (0,)), ((), ()))
VMEM_BYTES = 60 * 2**20
AXES = ("tensor", "dp")


def matmul(left, right, dims=NN):
    return lax.dot_general(left, right, dims, preferred_element_type=f32)


def norm_parts(values):
    center = values - jnp.mean(values, axis=-1, keepdims=True)
    second = jnp.mean(center * center, axis=-1, keepdims=True)
    inv = lax.rsqrt(second + EPSILON)
    return center * inv, inv


def gelu_and_slope(pre):
    phi = 0.5 + 0.5 * lax.erf(pre * 0.7071067811865476)
    bell = jnp.exp(pre * pre * -0.5)
    return pre * phi, phi + pre * (bell * 0.3989422804014327)


def full(shape):
    return pl.BlockSpec(shape, lambda *_: (0,) * len(shape), pipeline_mode=pl.Buffered(1))


def call(kernel, name, grid, in_specs, out_specs, out_shape, args, scratch=(), flops=0, prefetch=0, aliases={}, **params):
    moved = 0
    if flops:
        moved = sum(a.size * a.dtype.itemsize for a in args)
        moved += sum(math.prod(shape) * jnp.dtype(dtype).itemsize for shape, dtype in out_shape)
    return pl.pallas_call(
        kernel,
        grid_spec=pltpu.PrefetchScalarGridSpec(
            num_scalar_prefetch=prefetch,
            grid=grid,
            in_specs=in_specs,
            out_specs=out_specs,
            scratch_shapes=list(scratch),
        ),
        out_shape=[jax.ShapeDtypeStruct(shape, dtype) for shape, dtype in out_shape],
        input_output_aliases=aliases,
        compiler_params=pltpu.CompilerParams(vmem_limit_bytes=VMEM_BYTES, **params),
        cost_estimate=pl.CostEstimate(flops=2 * flops, bytes_accessed=moved, transcendentals=0),
        name=name,
    )(*args)


def before(ref, count):
    height = ref.shape[0]
    rows = pl.program_id(0) * height + lax.broadcasted_iota(jnp.int32, (height, 1), 0)
    return jnp.where(rows < count, ref[...].astype(f32), 0.0)


def qkv_kernel(part, count, x_ref, vec_ref, bias_ref, w_ref, normed_ref, triple_ref):
    hat, _ = norm_parts(before(x_ref, count))
    normed = (hat * vec_ref[0:1] + vec_ref[1:2]).astype(bf16)
    normed_ref[...] = normed
    tensor, dp = w_ref.shape[:2]
    width = w_ref.shape[3] // 3
    for s in range(3):
        for t in range(tensor):
            cols = slice(t * width, (t + 1) * width)
            w = w_ref[t, :, :part, s * width : (s + 1) * width].reshape(dp * part, width)
            out = matmul(normed, w)
            if s != 1:
                out = out + bias_ref[s // 2 : s // 2 + 1, cols]
            triple_ref[s, :, cols] = out.astype(bf16)


def window(image):
    start = pl.multiple_of(image * STRIDE, 16)
    return pl.ds(start, WINDOW)


def keep_before(image, ref, index, value):
    edge = pl.ds(pl.multiple_of(image * STRIDE, 16), 16)
    rest = pl.ds(pl.multiple_of(image * STRIDE + 16, 16), WINDOW - 16)
    rows = lax.broadcasted_iota(jnp.int32, (16, 1), 0)
    head = jnp.where(rows < image, ref[(*index[:-1], edge, index[-1])].astype(f32), value[:16])
    ref[(*index[:-1], edge, index[-1])] = head.astype(ref.dtype)
    ref[(*index[:-1], rest, index[-1])] = value[16:].astype(ref.dtype)


def attend_kernel(triple_ref, context_ref, stat_ref):
    image = pl.program_id(1)
    lanes = lax.broadcasted_iota(jnp.int32, (1, WINDOW), 1)
    mask = jnp.where((lanes >= image) & (lanes < image + SEQ), 0.0, -1e30)
    own = window(image)
    stats = []
    for h in range(triple_ref.shape[2] // HEAD_DIM):
        cols = slice(HEAD_DIM * h, HEAD_DIM * (h + 1))
        query = triple_ref[0, own, cols] * bf16(LOG_SCALE)
        scores = matmul(query, triple_ref[1, own, cols], NT) + mask
        top = jnp.max(scores, axis=1, keepdims=True)
        expo = jnp.exp(scores - top)
        total = jnp.sum(expo, axis=1, keepdims=True)
        context = matmul(expo.astype(bf16), triple_ref[2, own, cols]) * (1.0 / total)
        keep_before(image, context_ref, (cols,), context)
        stats.append(top + jnp.log(total))
    stat_ref[0] = jnp.concatenate(stats, axis=1).T


def attend_back_kernel(triple_ref, stat_ref, grad_ref, *refs):
    out_ref = refs[-1]
    image = pl.program_id(1)
    rows = lax.broadcasted_iota(jnp.int32, (WINDOW, 1), 0)
    mask = jnp.where((rows >= image) & (rows < image + SEQ), 0.0, -1e30)
    lanes = lax.broadcasted_iota(jnp.int32, (1, WINDOW), 1)
    real = (lanes >= image) & (lanes < image + SEQ)
    own = window(image)
    for h in range(triple_ref.shape[2] // HEAD_DIM):
        cols = slice(HEAD_DIM * h, HEAD_DIM * (h + 1))
        query = triple_ref[0, own, cols]
        keys = triple_ref[1, own, cols]
        grad = grad_ref[own, cols]
        scores = matmul(keys, query * bf16(LOG_SCALE), NT) + mask
        probs = jnp.exp(scores - jnp.where(real, stat_ref[0, h : h + 1, :], 1e30))
        grad_probs = matmul(triple_ref[2, own, cols], grad, NT)
        inner = jnp.sum(probs * grad_probs, axis=0, keepdims=True)
        grad_scores = (probs * (grad_probs - inner)).astype(bf16)
        keep_before(image, out_ref, (2, cols), matmul(probs.astype(bf16), grad))
        keep_before(image, out_ref, (1, cols), matmul(grad_scores, query) * LOG_SCALE)
        keep_before(image, out_ref, (0, cols), (matmul(keys.T, grad_scores) * LOG_SCALE).T)


def merge_kernel(count, ctx_ref, x_ref, vec_ref, w_ref, resid_ref, normed_ref):
    tensor, dp, rows, width = w_ref.shape
    total = before(x_ref, count) + vec_ref[2:3]
    for t in range(tensor):
        w = w_ref[t].reshape(dp * rows, width)
        total = total + matmul(ctx_ref[:, t * width : (t + 1) * width], w, NT)
    resid_ref[...] = total
    hat, _ = norm_parts(total)
    normed_ref[...] = (hat * vec_ref[3:4] + vec_ref[4:5]).astype(bf16)


def mlp_kernel(
    chunk, live_ref, normed_ref, resid_ref, ebias_ref, vec_ref, e_ref, r_ref, given_ref,
    out_ref, act_ref, slope_ref, grad_ref,
):
    grad_ref[...] = before(given_ref, live_ref[0]).astype(bf16)
    tensor, dp, rows, width = e_ref.shape
    normed = normed_ref[...]
    total = resid_ref[...] + vec_ref[5:6]
    for t in range(tensor):
        for c in range(width // chunk):
            local = slice(c * chunk, (c + 1) * chunk)
            cols = slice(t * width + c * chunk, t * width + (c + 1) * chunk)
            e = e_ref[t, :, :, local].reshape(dp * rows, chunk)
            active, slope = gelu_and_slope(matmul(normed, e) + ebias_ref[:, cols])
            active = active.astype(bf16)
            act_ref[:, cols] = active
            slope_ref[:, cols] = slope.astype(bf16)
            r = r_ref[t, :, :, local].reshape(dp * rows, chunk)
            total = total + matmul(active, r, NT)
    out_ref[...] = total.astype(bf16)


def accumulate(first, ref, value):
    @pl.when(first)
    def _():
        ref[...] = value

    @pl.when(jnp.logical_not(first))
    def _():
        ref[...] += value


def norm_back(values, gain, grad):
    hat, inv = norm_parts(values)
    scaled = grad * gain
    back = (
        scaled
        - jnp.mean(scaled, axis=-1, keepdims=True)
        - hat * jnp.mean(scaled * hat, axis=-1, keepdims=True)
    ) * inv
    return back, jnp.sum(grad * hat, axis=0, keepdims=True), jnp.sum(grad, axis=0, keepdims=True)


def mlp_back_kernel(
    chunk, grad_ref, slope_ref, resid_ref, vec_ref, e_ref, r_ref, m_ref,
    pre_ref, low_ref, ctx_ref, sums_ref, esum_ref,
):
    tensor, dp, rows, width = e_ref.shape
    first = pl.program_id(0) == 0
    grad = grad_ref[...]
    total = jnp.zeros(grad.shape, f32)
    parts = []
    for t in range(tensor):
        for c in range(width // chunk):
            local = slice(c * chunk, (c + 1) * chunk)
            cols = slice(t * width + c * chunk, t * width + (c + 1) * chunk)
            r = r_ref[t, :, :, local].reshape(dp * rows, chunk)
            pre = (matmul(grad, r) * slope_ref[:, cols].astype(f32)).astype(bf16)
            pre_ref[:, cols] = pre
            parts.append(jnp.sum(pre.astype(f32), axis=0, keepdims=True))
            e = e_ref[t, :, :, local].reshape(dp * rows, chunk)
            total = total + matmul(pre, e, NT)
    grad = grad.astype(f32)
    back, gain_sum, shift_sum = norm_back(resid_ref[...], vec_ref[3:4], total)
    resid_grad = grad + back
    low = resid_grad.astype(bf16)
    low_ref[...] = low
    wide = m_ref.shape[3]
    for t in range(tensor):
        m = m_ref[t].reshape(dp * rows, wide)
        ctx_ref[:, t * wide : (t + 1) * wide] = matmul(low, m).astype(bf16)
    sums = jnp.concatenate(
        [
            jnp.sum(grad, axis=0, keepdims=True),
            gain_sum,
            shift_sum,
            jnp.sum(resid_grad, axis=0, keepdims=True),
        ],
        axis=0,
    )
    accumulate(first, sums_ref, sums)
    parts = jnp.concatenate(parts, axis=1)
    lines = [parts[:, k * 128 : (k + 1) * 128] for k in range(esum_ref.shape[0])]
    accumulate(first, esum_ref, jnp.concatenate(lines, axis=0))


def qkv_back_kernel(part, count, x_ref, low_ref, vec_ref, grad_ref, w_ref, out_ref, sums_ref, bsum_ref):
    tensor, dp = w_ref.shape[:2]
    width = w_ref.shape[3] // 3
    first = pl.program_id(0) == 0
    total = jnp.zeros(x_ref.shape, f32)
    for s in range(3):
        for t in range(tensor):
            w = w_ref[t, :, :part, s * width : (s + 1) * width].reshape(dp * part, width)
            total = total + matmul(grad_ref[s, :, t * width : (t + 1) * width], w, NT)
    back, gain_sum, shift_sum = norm_back(before(x_ref, count), vec_ref[0:1], total)
    out_ref[...] = (low_ref[...].astype(f32) + back).astype(bf16)
    accumulate(first, sums_ref, jnp.concatenate([gain_sum, shift_sum], axis=0))
    bias = [jnp.sum(grad_ref[s].astype(f32), axis=0, keepdims=True) for s in (0, 2)]
    accumulate(first, bsum_ref, jnp.concatenate(bias, axis=0))


def weight_grad_kernel(starts, *refs):
    count = len(starts) - 1
    lefts, rights, out_ref, turned = refs[:count], refs[count : 2 * count], refs[-2], refs[-1]
    step = pl.program_id(0)
    for j in range(count):
        @pl.when((step >= starts[j]) & (step < starts[j + 1]))
        def _():
            @pl.when(step == starts[j])
            def _():
                turned[...] = lefts[j][...].T

            out = matmul(turned[...], rights[j][0])
            out_ref[...] = out.astype(bf16).reshape(out_ref.shape)


def weight_grads(name, pairs, tensor, dp, block):
    rows, deep = pairs[0][0].shape
    locals_ = [right.shape[1] // tensor for _, right in pairs]
    block = min([block] + locals_)
    pers = [local // block for local in locals_]
    starts = [0]
    for per in pers:
        starts.append(starts[-1] + tensor * per)

    def right_map(j, i):
        i = jnp.clip(i - starts[j], 0, tensor * pers[j] - 1)
        return (0, 0, i)

    def out_map(i):
        where, column, t = 0, 0, 0
        for j, per in enumerate(pers):
            inside = (i >= starts[j]) & (i < starts[j + 1])
            t = t + jnp.where(inside, (i - starts[j]) // per, 0)
            column = column + jnp.where(inside, where + (i - starts[j]) % per, 0)
            where += per
        return (t, 0, 0, column)

    return call(
        functools.partial(weight_grad_kernel, starts),
        name,
        (starts[-1],),
        [full((rows, deep))] * len(pairs)
        + [pl.BlockSpec((1, rows, block), functools.partial(right_map, j)) for j in range(len(pairs))],
        [pl.BlockSpec((1, dp, deep // dp, block), out_map)],
        [((tensor, dp, deep // dp, sum(locals_)), bf16)],
        [left for left, _ in pairs] + [right[None] for _, right in pairs],
        [pltpu.VMEM((deep, rows), bf16)],
        flops=rows * deep * tensor * sum(locals_),
    )[0]


def slot_grad_kernel(tensor, dp, starts, me_ref, *refs):
    count = len(starts) - 1
    lefts, rights = refs[:count], refs[count : 2 * count]
    keep_ref, send_ref, turned, total = refs[2 * count :]
    step, t = pl.program_id(0), pl.program_id(1)
    for j in range(count):
        @pl.when((step >= starts[j]) & (step < starts[j + 1]))
        def _():
            @pl.when((step == starts[j]) & (t == 0))
            def _():
                turned[...] = lefts[j][...].T

            total[...] = matmul(turned[...], rights[j][0])
    part = total.shape[0] // dp
    depth = dp // 4
    column = t ^ me_ref[1]
    for r in range(dp):
        owner = me_ref[0] ^ r
        slot = (((r >> 1) & 1) * tensor + column) * depth + (r >> 2)
        half = send_ref if r & 1 else keep_ref
        half[slot] = total[pl.ds(pl.multiple_of(owner * part, part), part), :].astype(bf16)


def slot_grads(name, pairs, tensor, dp, me, block):
    rows, deep = pairs[0][0].shape
    block = min([block] + [right.shape[2] // tensor for _, right in pairs])
    pers = [right.shape[2] // tensor // block for _, right in pairs]
    starts = [0]
    for (_, right), per in zip(pairs, pers):
        starts.append(starts[-1] + right.shape[0] * per)
    half = tensor * dp // 2

    def right_map(j, i, t, me):
        i = jnp.clip(i - starts[j], 0, starts[j + 1] - starts[j] - 1)
        return (i // pers[j], 0, t * pers[j] + i % pers[j])

    left_spec = pl.BlockSpec((rows, deep), lambda i, t, me: (0, 0), pipeline_mode=pl.Buffered(1))
    spec = pl.BlockSpec((half, deep // dp, block), lambda i, t, me: (0, 0, i))
    return call(
        functools.partial(slot_grad_kernel, tensor, dp, starts),
        name,
        (starts[-1], tensor),
        [left_spec] * len(pairs)
        + [pl.BlockSpec((1, rows, block), functools.partial(right_map, j)) for j in range(len(pairs))],
        [spec, spec],
        [((half, deep // dp, starts[-1] * block), bf16)] * 2,
        [me] + [left for left, _ in pairs] + [right for _, right in pairs],
        [pltpu.VMEM((deep, rows), bf16), pltpu.VMEM((deep, block), f32)],
        prefetch=1,
    )


def swap(values, d, t, tensor, dp):
    moves = []
    for p in range(dp):
        for q in range(tensor):
            moves.append((p * tensor + q, (p ^ d) * tensor + (q ^ t)))
    return lax.ppermute(values, ("dp", "tensor"), moves)


def sum_cores(keep, other, tensor, dp):
    depth = dp // 4
    parts = []
    for k in range(2 * tensor):
        own = slice(k * depth, (k + 1) * depth)
        parts.append((keep[own].astype(f32) + other[own].astype(f32)).astype(bf16))
    return parts


def send_plane(parts, tensor, dp):
    return [swap(parts[k], 2 * (k // tensor), k % tensor, tensor, dp) for k in range(1, 2 * tensor)]


def sum_plane(part, landed, dp):
    planes = []
    for z in range(dp // 4):
        total = part[z].astype(f32)
        for piece in landed:
            total = total + piece[z].astype(f32)
        planes.append(total.astype(bf16))
    return planes


def send_line(planes, tensor, dp):
    return [swap(planes[z], 4 * z, 0, tensor, dp) for z in range(1, dp // 4)]


def sum_line(plane, landed):
    total = plane.astype(f32)
    for piece in landed:
        total = total + piece.astype(f32)
    return total


def pack_kernel(
    heads_ref, merge_ref, expand_ref, reduce_ref, hb_ref, eb_ref, *refs
):
    small, (first_ref, later_ref) = refs[:-2], refs[-2:]
    _, part, own = heads_ref.shape
    for s in range(3):
        first_ref[:part, s * own : (s + 1) * own] = heads_ref[s]
    lines = [ref[...].astype(f32) for ref in small] + [jnp.zeros((8 - len(small), part), f32)]
    hb = hb_ref[...].astype(f32)
    hb = hb.reshape(hb.shape[0] * hb.shape[1], hb.shape[2])
    eb = eb_ref[...].astype(f32)
    pieces = []
    for piece in (jnp.concatenate(lines, axis=0), eb, hb):
        height, width = piece.shape
        if height < 8:
            piece = jnp.concatenate([piece, jnp.zeros((8 - height, width), f32)], axis=0)
        pieces.append(piece)
    used = sum(piece.shape[1] for piece in pieces)
    pieces.append(jnp.zeros((8, 128 - used), f32))
    first_ref[part:, :128] = jnp.concatenate(pieces, axis=1).astype(bf16)
    first_ref[part:, 128:] = jnp.zeros((8, 3 * own - 128), bf16)
    hidden = expand_ref.shape[1]
    later_ref[:, :hidden] = expand_ref[...]
    later_ref[:, hidden : 2 * hidden] = reduce_ref[...]
    later_ref[:, 2 * hidden :] = merge_ref[...]


def gather_kernel(in_ref, out_ref, own_sem, send_sem, recv_sem):
    d, y = lax.axis_index("dp"), lax.axis_index("tensor")
    z, x, c = lax.div(d, 4), lax.rem(lax.div(d, 2), 2), lax.rem(d, 2)
    far_x, far_y, far_c = 1 - x, 1 - y, 1 - c
    barrier = pltpu.get_barrier_semaphore()

    def index(place):
        pz, px, pc, py = place
        return (pz * 2 + px) * 2 + pc, py

    lines = [lax.rem(z + k, 4) for k in range(1, 4)]
    peers = [(other, x, c, y) for other in lines] + [(z, far_x, c, y), (z, x, c, far_y), (z, x, far_c, y)]
    to_x, to_y, to_c = peers[3:]
    for peer in peers:
        pl.semaphore_signal(barrier, inc=1, device_id=index(peer), device_id_type=pl.DeviceIdType.MESH)
    pl.semaphore_wait(barrier, len(peers))

    sent = []

    def copy(owner, peer, slot, source=None):
        p, q = index(owner)
        return pltpu.make_async_remote_copy(
            src_ref=out_ref.at[q, p] if source is None else source,
            dst_ref=out_ref.at[q, p],
            send_sem=send_sem.at[slot],
            recv_sem=recv_sem.at[p * 2 + q],
            device_id=index(peer),
            device_id_type=pl.DeviceIdType.MESH,
        )

    def send(owner, peer, source=None):
        out = copy(owner, peer, len(sent), source)
        out.start()
        sent.append(out)

    def arrive(owner):
        copy(owner, to_c, 0).wait_recv()

    own = (z, x, c, y)
    for peer in peers:
        send(own, peer, in_ref)
    keep = pltpu.make_async_copy(in_ref, out_ref.at[y, d], own_sem)
    keep.start()
    for other in lines:
        block = (other, x, c, y)
        arrive(block)
        for peer in (to_x, to_y, to_c):
            send(block, peer)
    for level in range(4):
        block = (level, far_x, c, y)
        arrive(block)
        if level % 2 == 0:
            send(block, to_y)
        send(block, to_c)
        block = (level, x, c, far_y)
        arrive(block)
        if level % 2 == 1:
            send(block, to_x)
        send(block, to_c)
    for level in range(4):
        block = (level, far_x, c, far_y)
        arrive(block)
        send(block, to_c)
    for level in range(4):
        for px in range(2):
            for py in range(2):
                arrive((level, px, far_c, py))
    for out in sent:
        out.wait_send()
    keep.wait()


def gather_first(shard, tensor, dp):
    shape = (tensor, dp) + shard.shape
    if (tensor, dp) != (2, 16):
        return lax.all_gather(shard, AXES, axis=0, tiled=True).reshape(shape)
    return call(
        gather_kernel,
        "gather",
        (),
        [pl.BlockSpec(memory_space=pltpu.VMEM)],
        [pl.BlockSpec(memory_space=pl.ANY)],
        [(shape, bf16)],
        (shard,),
        [pltpu.SemaphoreType.DMA, pltpu.SemaphoreType.DMA((31,)), pltpu.SemaphoreType.DMA((32,))],
        collective_id=1,
        has_side_effects=True,
    )[0]


def tail_kernel(dp, tensor, *refs):
    count, depth = dp * tensor, dp // 4
    own_ref, refs = refs[0], refs[1:]
    others, refs = refs[: 2 * tensor - 1], refs[2 * tensor - 1 :]
    one_ref, two_ref, hb_ref, eb_ref, out_ref, sums_ref = refs[:6]
    packed, landed, line, arrived, send_sem, recv_sem, line_send, line_recv = refs[6:]
    d, y = lax.axis_index("dp"), lax.axis_index("tensor")
    me = d * tensor + y
    part = own_ref.shape[1]
    barrier = pltpu.get_barrier_semaphore()

    def place(k):
        other = lax.rem(me + k, count)
        return other, (lax.div(other, tensor), lax.rem(other, tensor))

    def greet(k, carry):
        _, where = place(k)
        pl.semaphore_signal(barrier, inc=1, device_id=where, device_id_type=pl.DeviceIdType.MESH)
        return carry

    lax.fori_loop(1, count, greet, 0)

    def plane(z):
        total = own_ref[z].astype(f32)
        for ref in others:
            total = total + ref[z].astype(f32)
        return total

    for z in range(1, depth):
        line[z - 1] = plane(z).astype(bf16)
    heads = hb_ref.shape[1] // HEAD_DIM
    own_heads, hb_wide = heads // tensor, HEAD_DIM // dp
    eb_tall, eb_wide = eb_ref.shape[0] // tensor, eb_ref.shape[1] // dp
    hb = [
        hb_ref[k : k + 1, h * HEAD_DIM : (h + 1) * HEAD_DIM] for k in range(2) for h in range(heads)
    ]
    hb = jnp.concatenate(hb, axis=0).T
    eb = eb_ref[...].T
    sums = jnp.concatenate([one_ref[...], two_ref[3:4], two_ref[1:3], two_ref[0:1]], axis=0)
    for p in range(dp):
        piece = sums[:, p * part : (p + 1) * part]
        for q in range(tensor):
            packed[p * tensor + q, 0:6, 0:part] = piece
            lane = part
            packed[p * tensor + q, 0:eb_wide, lane : lane + eb_tall] = eb[
                p * eb_wide : (p + 1) * eb_wide, q * eb_tall : (q + 1) * eb_tall
            ]
            for k in range(2):
                lane = part + eb_tall + k * own_heads
                packed[p * tensor + q, 0:hb_wide, lane : lane + own_heads] = hb[
                    p * hb_wide : (p + 1) * hb_wide,
                    k * heads + q * own_heads : k * heads + (q + 1) * own_heads,
                ]
    pl.semaphore_wait(barrier, count - 1)

    copies = []
    for z in range(1, depth):
        far = d
        for bit in range(depth.bit_length() - 1):
            if (z >> bit) & 1:
                unit = 4 << bit
                far = far + unit - 2 * unit * lax.rem(lax.div(far, unit), 2)
        copies.append(pltpu.make_async_remote_copy(
            src_ref=line.at[z - 1],
            dst_ref=arrived.at[z - 1],
            send_sem=line_send.at[z - 1],
            recv_sem=line_recv.at[z - 1],
            device_id=(far, y),
            device_id_type=pl.DeviceIdType.MESH,
        ))

    def copy(k):
        other, where = place(k)
        return pltpu.make_async_remote_copy(
            src_ref=packed.at[other],
            dst_ref=landed.at[k],
            send_sem=send_sem.at[k],
            recv_sem=recv_sem.at[k],
            device_id=where,
            device_id_type=pl.DeviceIdType.MESH,
        )

    def start(k, carry):
        copy(k).start()
        return carry

    lax.fori_loop(1, count, start, 0)
    for item in copies:
        item.start()
    total = plane(0)

    def finish(k, sums):
        copy(k).wait()
        return sums + landed[k]

    sums = lax.fori_loop(1, count, finish, packed[me])
    sums_ref[...] = sums
    for item, z in zip(copies, range(1, depth)):
        item.wait()
        total = total + arrived[z - 1].astype(f32)
    own = out_ref.shape[2]
    for s in range(3):
        out_ref[s] = total[:, s * own : (s + 1) * own]


def tail(part_own, landed, sums, hb, eb, tensor, dp):
    depth, part, lanes = part_own.shape
    count = tensor * dp
    arrays = [part_own, *landed, *sums, hb, eb]
    vmem = pl.BlockSpec(memory_space=pltpu.VMEM)
    out = [((3, part, lanes // 3), f32), ((8, 128), f32)]
    return call(
        functools.partial(tail_kernel, dp, tensor),
        "tail",
        (),
        [vmem] * len(arrays),
        [vmem] * len(out),
        out,
        arrays,
        [
            pltpu.VMEM((count, 8, 128), f32), pltpu.VMEM((count, 8, 128), f32),
            pltpu.VMEM((depth - 1, part, lanes), bf16), pltpu.VMEM((depth - 1, part, lanes), bf16),
            pltpu.SemaphoreType.DMA((count,)), pltpu.SemaphoreType.DMA((count,)),
            pltpu.SemaphoreType.DMA((depth - 1,)), pltpu.SemaphoreType.DMA((depth - 1,)),
        ],
        collective_id=0,
        has_side_effects=True,
    )


def finish_kernel(sums_ref, heads_ref, out_ref, hb_ref, eb_ref, *vectors):
    out_ref[...] = heads_ref[...]
    part = vectors[0].shape[1]
    for r, ref in enumerate(vectors):
        ref[...] = sums_ref[r : r + 1, :part]
    wide, tall = eb_ref.shape
    eb_ref[...] = sums_ref[:wide, part : part + tall]
    wide, count = hb_ref.shape[1:]
    for k in range(2):
        lane = part + tall + k * count
        hb_ref[k] = sums_ref[:wide, lane : lane + count]


def shards(
    tensor,
    dp,
    activations,
    first_gain,
    first_shift,
    heads_weight,
    heads_bias,
    merge_weight,
    merge_bias,
    second_gain,
    second_shift,
    expand_weight,
    expand_bias,
    reduce_weight,
    reduce_bias,
    output_grad,
    real_images,
):
    rows, deep = activations.shape
    images = rows // SEQ
    part = deep // dp
    own = heads_weight.shape[2]
    hidden_own = expand_weight.shape[1]
    hidden = hidden_own * tensor
    heads = deep // HEAD_DIM
    least = (images - 1) * STRIDE + WINDOW
    blocks = -(-least // 512)
    block = -(-least // blocks // 16) * 16
    total_rows = block * blocks

    def gather(shard):
        out = lax.all_gather(shard, AXES, axis=0, tiled=True)
        return out.reshape(tensor, dp, *shard.shape)

    small = [first_gain, first_shift, merge_bias, second_gain, second_shift, reduce_bias]
    arrays = [
        heads_weight, merge_weight.T, expand_weight, reduce_weight.T,
        heads_bias.transpose(0, 2, 1), expand_bias.T,
    ] + [v.reshape(1, part) for v in small]
    vmem = pl.BlockSpec(memory_space=pltpu.VMEM)
    first, later = call(
        pack_kernel, "pack", (), [vmem] * len(arrays), [vmem] * 2,
        [((part + 8, 3 * own), bf16), ((part, 2 * hidden_own + own), bf16)], arrays,
    )
    wide = gather(later)
    wide_heads = gather_first(first, tensor, dp)

    hbs, ebs = heads_bias.shape, expand_bias.shape
    small = wide_heads[:, :, part:, :128].astype(f32)
    vectors = small[0, :, :6, :part].transpose(1, 0, 2).reshape(6, deep)
    eb = small[:, :, : ebs[1], part : part + ebs[0]].transpose(0, 3, 1, 2).reshape(1, hidden)
    hb = small[:, :, : 2 * hbs[2], part + ebs[0] : part + ebs[0] + hbs[1]]
    hb = hb.reshape(tensor, dp, 2, hbs[2], hbs[1]).transpose(2, 0, 4, 1, 3).reshape(2, deep)
    live = jnp.clip(real_images - lax.axis_index("tensor") * images, 0, images) * SEQ

    def by_rows(width):
        return pl.BlockSpec((block, width), lambda i, *_: (i, 0))

    def column(index, width):
        shape = (tensor, dp, part, width)
        return pl.BlockSpec(shape, lambda *_: (0, 0, 0, index), pipeline_mode=pl.Buffered(1))

    vec = full((6, deep))
    triple_spec = pl.BlockSpec((3, block, deep), lambda i: (0, i, 0))
    normed_one, triple = call(
        functools.partial(qkv_kernel, part, rows),
        "qkv",
        (blocks,),
        [by_rows(deep), vec, full((2, deep)), full(wide_heads.shape)],
        [by_rows(deep), triple_spec],
        [((total_rows, deep), bf16), ((3, total_rows, deep), bf16)],
        (activations, vectors, hb, wide_heads),
        flops=total_rows * deep * deep * 3,
    )

    group = 4
    groups = heads // group
    panel = group * HEAD_DIM
    head_spec = pl.BlockSpec((3, total_rows, panel), lambda g, i: (0, 0, g))
    ctx_spec = pl.BlockSpec((total_rows, panel), lambda g, i: (0, g))
    stat_spec = pl.BlockSpec((1, group, WINDOW), lambda g, i: (g * images + i, 0, 0))
    attend_flops = images * heads * WINDOW * 768 * 256 * 2
    context, stat = call(
        attend_kernel,
        "attend",
        (groups, images),
        [head_spec],
        [ctx_spec, stat_spec],
        [((total_rows, deep), bf16), ((images * groups, group, WINDOW), f32)],
        (triple,),
        flops=attend_flops,
    )

    merge_width, expand_width = merge_weight.shape[0], hidden_own
    expand_spec = column(0, expand_width)
    reduce_spec = column(1, expand_width)
    merge_spec = column(2 * expand_width // merge_width, merge_width)
    resid, normed_two = call(
        functools.partial(merge_kernel, rows),
        "merge",
        (blocks,),
        [by_rows(deep), by_rows(deep), vec, merge_spec],
        [by_rows(deep), by_rows(deep)],
        [((total_rows, deep), f32), ((total_rows, deep), bf16)],
        (context, activations, vectors, wide),
        flops=total_rows * deep * deep,
    )

    chunk = min(1024, hidden_own)
    output, active, slope, grad = call(
        functools.partial(mlp_kernel, chunk),
        "mlp",
        (blocks,),
        [
            by_rows(deep), by_rows(deep), full((1, hidden)), vec, expand_spec, reduce_spec, by_rows(deep),
        ],
        [by_rows(deep), by_rows(hidden), by_rows(hidden), by_rows(deep)],
        [
            ((rows, deep), bf16), ((total_rows, hidden), bf16), ((total_rows, hidden), bf16),
            ((total_rows, deep), bf16),
        ],
        (live, normed_two, resid, eb, vectors, wide, wide, output_grad),
        prefetch=1,
        flops=total_rows * deep * hidden * 2,
    )

    def scatter(grads):
        grads = grads.reshape(tensor * dp * part, grads.shape[3])
        return lax.psum_scatter(grads, AXES, scatter_dimension=0, tiled=True)

    grad_reduce = weight_grads("reduce_grad", [(grad, active)], tensor, dp, 512)
    grad, slope, grad_reduce = lax.optimization_barrier((grad, slope, grad_reduce))
    grad_reduce = scatter(grad_reduce)

    back_chunk = min(512, hidden_own)
    pre_grad, resid_low, grad_context, sums_two, esum = call(
        functools.partial(mlp_back_kernel, back_chunk),
        "mlp_back",
        (blocks,),
        [
            by_rows(deep), by_rows(hidden), by_rows(deep), vec,
            expand_spec, reduce_spec, merge_spec,
        ],
        [
            by_rows(hidden), by_rows(deep), by_rows(deep),
            pl.BlockSpec((4, deep), lambda i: (0, 0)), pl.BlockSpec((hidden // 128, 128), lambda i: (0, 0)),
        ],
        [
            ((total_rows, hidden), bf16), ((total_rows, deep), bf16), ((total_rows, deep), bf16),
            ((4, deep), f32), ((hidden // 128, 128), f32),
        ],
        (grad, slope, resid, vectors, wide, wide, wide),
    )
    me = jnp.stack([lax.axis_index("dp"), lax.axis_index("tensor")]).astype(jnp.int32)
    keep, send = slot_grads(
        "middle_grad", [(normed_two, pre_grad[None]), (resid_low, context[None])], tensor, dp, me, 512
    )
    grad_context, keep, send = lax.optimization_barrier((grad_context, keep, send))
    other = swap(send, 1, 0, tensor, dp)

    def attend_back(first, before, grad_context):
        count = groups // 2
        return call(
            attend_back_kernel,
            "attend_back",
            (count, images),
            [
                pl.BlockSpec((3, total_rows, panel), lambda g, i: (0, 0, first + g)),
                pl.BlockSpec((1, group, WINDOW), lambda g, i: ((first + g) * images + i, 0, 0)),
                pl.BlockSpec((total_rows, panel), lambda g, i: (0, first + g)),
            ] + [pl.BlockSpec(memory_space=pl.ANY)] * len(before),
            [pl.BlockSpec((3, total_rows, panel), lambda g, i: (0, 0, first + g))],
            [((3, total_rows, deep), bf16)],
            (triple, stat, grad_context) + before,
            aliases={3: 0} if before else {},
        )[0]

    grad_triple = attend_back(0, (), grad_context)
    keep, other, grad_triple = lax.optimization_barrier((keep, other, grad_triple))
    parts = sum_cores(keep, other, tensor, dp)
    *parts, grad_context = lax.optimization_barrier((*parts, grad_context))
    landed = send_plane(parts, tensor, dp)
    grad_triple = attend_back(groups // 2, (grad_triple,), grad_context)
    *landed, part_own, grad_triple = lax.optimization_barrier((*landed, parts[0], grad_triple))
    planes = sum_plane(part_own, landed, dp)
    *planes, grad_triple = lax.optimization_barrier((*planes, grad_triple))
    landed = send_line(planes, tensor, dp)
    keep, send = slot_grads("heads_grad", [(normed_one, grad_triple)], tensor, dp, me, 512)
    resid_low, keep, send, *landed = lax.optimization_barrier((resid_low, keep, send, *landed))
    grad_middle = sum_line(planes[0], landed)

    other = swap(send, 1, 0, tensor, dp)
    parts = sum_cores(keep, other, tensor, dp)
    *parts, resid_low = lax.optimization_barrier((*parts, resid_low))
    landed = send_plane(parts, tensor, dp)
    input_grad, sums_one, bsum = call(
        functools.partial(qkv_back_kernel, part, rows),
        "qkv_back",
        (blocks,),
        [by_rows(deep), by_rows(deep), vec, triple_spec, full(wide_heads.shape)],
        [by_rows(deep), pl.BlockSpec((2, deep), lambda i: (0, 0)), pl.BlockSpec((2, deep), lambda i: (0, 0))],
        [((rows, deep), bf16), ((2, deep), f32), ((2, deep), f32)],
        (activations, resid_low, vectors, grad_triple, wide_heads),
        flops=total_rows * deep * deep * 3,
    )

    heads_sum, sums = tail(parts[0], landed, (sums_one, sums_two), bsum, esum, tensor, dp)
    grad_heads, hb_grad, eb_grad, *vector = call(
        finish_kernel, "finish", (), [vmem] * 2, [vmem] * 9,
        [(heads_sum.shape, f32), ((2, hbs[2], hbs[1]), f32), (ebs[::-1], f32)] + [((1, part), f32)] * 6,
        (sums, heads_sum),
    )
    vector = [v.reshape(part) for v in vector]

    return (
        output,
        input_grad,
        vector[0],
        vector[1],
        grad_heads,
        hb_grad.transpose(0, 2, 1),
        grad_middle[:, expand_width:].T,
        vector[2],
        vector[3],
        vector[4],
        grad_middle[:, :expand_width],
        eb_grad.T,
        grad_reduce.astype(f32).T,
        vector[5],
    )


def solution(mesh):
    rows = P(("dp", "tensor"), None)
    specs = (
        P("dp"),
        P("dp"),
        P(None, "dp", "tensor"),
        P(None, "tensor", "dp"),
        P("tensor", "dp"),
        P("dp"),
        P("dp"),
        P("dp"),
        P("dp", "tensor"),
        P("tensor", "dp"),
        P("tensor", "dp"),
        P("dp"),
    )
    return jax.shard_map(
        functools.partial(shards, mesh.shape["tensor"], mesh.shape["dp"]),
        mesh=mesh,
        in_specs=(rows,) + specs + (rows, P("dp")),
        out_specs=(rows, rows) + specs,
        check_vma=False,
    )
```

time: 1260 us -> 610 us (0.48)
  waiting for transfers between devices: 677 us -> 33.9 us
  Pallas kernels: 450 us -> 513 us
  local copies, waits for them, and re-layouts: 62.2 us -> 4.56 us
  blocking collectives: 43 us -> 0 us
  starting transfers between devices: 0.36 us -> 21.6 us
    reduce_scatter x4 -> x1, waiting for transfers between devices: 545 us -> 0.01 us  [scatter(): return lax.psum_scatter(grads, AXES, scatter_dimension=0, tiled=True)]
    all_gather x4 -> x1, waiting for transfers between devices: 126 us -> 13.9 us  [gather(): out = lax.all_gather(shard, AXES, axis=0, tiled=True)]
    pallas_call x11 -> x15, Pallas kernels: 450 us -> 513 us  [call(): pl.pallas_call(kernel, grid_spec=pltpu.PrefetchScalarGridSpec(num_scalar_...]
    unnamed x1 -> x0, blocking collectives: 43 us -> none
    reshape x19 -> x4, local copies, waits for them, and re-layouts: 28.5 us -> 2.69 us  [the longest x2 1.22 us: shards(): hb.reshape(tensor, dp, 2, hbs[2], hbs[1]).transpose(2, 0, 4, 1, 3)]
    ppermute x0 -> x11, starting transfers between devices: none -> 21.5 us  [swap(): return lax.ppermute(values, ('dp', 'tensor'), moves)]
    ppermute x0 -> x11, waiting for transfers between devices: none -> 19.9 us  [swap(): return lax.ppermute(values, ('dp', 'tensor'), moves)]
  transfers between devices with their start and end apart: 9 -> 13, of which waited for: 7 -> 4; matrix products, arithmetic and copies ran while one was open for 5% -> 3% of each run, Pallas kernels for 14% -> 68%
where the time goes in v2:
time: 610 us; the launch traced here: 602 us
  Pallas kernels  513 us (84%)
  waiting for transfers between devices  33.9 us (6%)
  starting transfers between devices  21.6 us (4%)
  between operations  15.4 us (3%)
  other arithmetic  14.2 us (2%)
    pallas_call x15, Pallas kernels, call(): pl.pallas_call(kernel, grid_spec=pltpu.PrefetchScalarGridSpec(num_scalar_...  513 us
    ppermute x11, starting transfers between devices, swap(): return lax.ppermute(values, ('dp', 'tensor'), moves)  21.5 us
    ppermute x11, waiting for transfers between devices, swap(): return lax.ppermute(values, ('dp', 'tensor'), moves)  19.9 us
    all_gather x1, waiting for transfers between devices, gather(): out = lax.all_gather(shard, AXES, axis=0, tiled=True)  13.9 us
  transfers between devices with their start and end apart: 13, of which 4 were waited for; matrix products, arithmetic and copies ran while one was open for 3% of the time, Pallas kernels for 68%

profile of v2, /device:TPU:0, one launch (start us, length us, event | category | flops | bytes accessed | tf_op | source)
XLA Modules:
  0.0 602.4 jit_solution(6419169073424139663)
XLA Ops:
  7.2 2.2 pack.1
  10.1 55.1 %gather.1.w_ref = bf16[2,16,72,1536]{3,2,1,0:T(8,128)(2,1)} custom-call(bf16[72,1536]{1,0:T(8,128)(2,1)} %get-tuple-element.84.in_ref), custom_call_target="tpu_custom_call" | custom-call | tf_op jit(solution)/shard_map/gather/pallas_call | solution.py:52
  69.2 22.9 %qkv.1 = (bf16[2320,1024]{1,0:T(8,128)(2,1)}, bf16[3,2320,1024]{2,1,0:T(8,128)(2,1)}) custom-call(bf16[2308,1024]{1,0:T(8,128)(2,1)} %x_ref.5, f32[6,1024]{1,0:T(8,128)} %reshape.120.vec_ref, f32[2,1024]{1,0:T(2,128)} %reshape.122.bias_ref, bf16[2,16,72,1536]{3,2,1,0:T(8,128)(2,1)} %gather.1.w_ref), custom_call_target="tpu_custom_call" | custom-call | flops 14596177920 | bytes 30842880 | tf_op jit(solution)/shard_map/qkv/pallas_call | solution.py:52
  92.1 52.8 %attend.1 = (bf16[2320,1024]{1,0:T(8,128)(2,1)}, f32[16,4,592]{2,1,0:T(4,128)}) custom-call(bf16[3,2320,1024]{2,1,0:T(8,128)(2,1)} %get-tuple-element.85.triple_ref), custom_call_target="tpu_custom_call" | custom-call | flops 29796335616 | bytes 19156992 | tf_op jit(solution)/shard_map/attend/pallas_call | solution.py:52
  144.9 13.9 %all-gather.2.cloned.1.call-done = bf16[2048,4608]{1,0:T(8,128)(2,1)} async-done(((bf16[64,4608]{1,0:T(8,128)(2,1)}), bf16[2048,4608]{1,0:T(8,128)(2,1)}) %all-gather.2.cloned.1.call-update) | async-done | bytes 18874384 | tf_op jit(solution)/shard_map/all_gather | solution.py:697
  158.8 12.6 %merge.1 = (f32[2320,1024]{1,0:T(8,128)}, bf16[2320,1024]{1,0:T(8,128)(2,1)}) custom-call(bf16[2320,1024]{1,0:T(8,128)(2,1)} %get-tuple-element.86.ctx_ref, bf16[2308,1024]{1,0:T(8,128)(2,1)} %x_ref.5, f32[6,1024]{1,0:T(8,128)} %reshape.120.vec_ref, bf16[2,16,64,4608]{3,2,1,0:T(8,128)(2,1)} %bitcast.50), custom_call_target="tpu_custom_call" | custom-call | flops 4865392640 | bytes 42631168 | tf_op jit(solution)/shard_map/merge/pallas_call | solution.py:52
  171.4 58.5 %mlp.1 = (bf16[2308,1024]{1,0:T(8,128)(2,1)}, bf16[2320,4096]{1,0:T(8,128)(2,1)}, bf16[2320,4096]{1,0:T(8,128)(2,1)}, bf16[2320,1024]{1,0:T(8,128)(2,1)}) custom-call(s32[1]{0:T(128)S(6)} %mul.7.live_ref, bf16[2320,1024]{1,0:T(8,128)(2,1)} %get-tuple-element.88.normed_ref.refs_0_, f32[2320,1024]{1,0:T(8,128)} %get-tuple-element.89.resid_ref, ...), custom_call_target="tpu_custom_call" | custom-call | flops 38923141120 | bytes 104259584 | tf_op jit(solution)/shard_map/mlp/pallas_call | solution.py:52
  229.9 28.8 %reduce_grad.1 = bf16[2,16,64,2048]{3,2,1,0:T(8,128)(2,1)} custom-call(bf16[2320,1024]{1,0:T(8,128)(2,1)} %get-tuple-element.94.refs_0_.grad_ref, bf16[1,2320,4096]{2,1,0:T(8,128)(2,1)} %bitcast.79), custom_call_target="tpu_custom_call" | custom-call | flops 19461570560 | bytes 32145408 | tf_op jit(solution)/shard_map/reduce_grad/pallas_call | solution.py:52
  259.3 63.6 %mlp_back.1 = (bf16[2320,4096]{1,0:T(8,128)(2,1)}, bf16[2320,1024]{1,0:T(8,128)(2,1)}, bf16[2320,1024]{1,0:T(8,128)(2,1)}, f32[4,1024]{1,0:T(4,128)}, f32[32,128]{1,0:T(8,128)}) custom-call(bf16[2320,1024]{1,0:T(8,128)(2,1)} %get-tuple-element.94.refs_0_.grad_ref, bf16[2320,4096]{1,0:T(8,128)(2,1)} %get-tuple-element.95.slope_ref, ...), custom_call_target="tpu_custom_call" | custom-call | tf_op jit(solution)/shard_map/mlp_back/pallas_call | solution.py:52
  322.9 41.0 %middle_grad.1 = (bf16[16,64,2560]{2,1,0:T(8,128)(2,1)}, bf16[16,64,2560]{2,1,0:T(8,128)(2,1)}) custom-call(s32[2]{0:T(128)} %pad_add_fusion.me_ref, bf16[2320,1024]{1,0:T(8,128)(2,1)} %get-tuple-element.88.normed_ref.refs_0_, bf16[2320,1024]{1,0:T(8,128)(2,1)} %get-tuple-element.128.refs_1_.low_ref, bf16[1,2320,4096]{2,1,0:T(8,128)(2,1)} %bitcast.56, ...), custom_call_target="tpu_custom_call" | custom-call | tf_op jit(solution)/shard_map/middle_grad/pallas_call | solution.py:52
  364.2 47.3 %attend_back.2.refs_0_ = bf16[3,2320,1024]{2,1,0:T(8,128)(2,1)} custom-call(bf16[3,2320,1024]{2,1,0:T(8,128)(2,1)} %get-tuple-element.85.triple_ref, f32[16,4,592]{2,1,0:T(4,128)} %get-tuple-element.104.stat_ref, bf16[2320,1024]{1,0:T(8,128)(2,1)} %get-tuple-element.112.grad_ref), custom_call_target="tpu_custom_call" | custom-call | tf_op jit(solution)/shard_map/attend_back/pallas_call | solution.py:52
  411.5 6.5 %add_convert_fusion = (bf16[4,64,2560]{2,1,0:T(8,128)(2,1)}, bf16[4,64,2560]{2,1,0:T(8,128)(2,1)}, bf16[4,64,2560]{2,1,0:T(8,128)(2,1)}, bf16[4,64,2560]{2,1,0:T(8,128)(2,1)S(1)}) fusion(bf16[16,64,2560]{2,1,0:T(8,128)(2,1)} %collective-permute-done, bf16[16,64,2560]{2,1,0:T(8,128)(2,1)} %get-tuple-element.106), kind=kLoop, calls=%fused_computation | loop fusion | flops 10485760 | bytes 15728640 | tf_op jit(solution)/shard_map/convert_element_type | solution.py:376
  421.5 47.5 %attend_back.3.refs_1_.grad_ref = bf16[3,2320,1024]{2,1,0:T(8,128)(2,1)} custom-call(bf16[3,2320,1024]{2,1,0:T(8,128)(2,1)} %get-tuple-element.85.triple_ref, f32[16,4,592]{2,1,0:T(4,128)} %get-tuple-element.104.stat_ref, bf16[2320,1024]{1,0:T(8,128)(2,1)} %get-tuple-element.112.grad_ref, ...), custom_call_target="tpu_custom_call", output_to_operand_aliasing={{}: (3, {})} | custom-call | tf_op jit(solution)/shard_map/attend_back/pallas_call | solution.py:52
  469.0 9.5 %collective-permute-done.3 = bf16[4,64,2560]{2,1,0:T(8,128)(2,1)} collective-permute-done((bf16[4,64,2560]{2,1,0:T(8,128)(2,1)}, bf16[4,64,2560]{2,1,0:T(8,128)(2,1)}, u32[]{:S(2)}, u32[]{:S(2)}) %collective-permute-start.3) | collective-permute-done | bytes 1310752 | tf_op jit(solution)/shard_map/ppermute | solution.py:368
  478.5 2.3 fusion.3
  480.8 11.7 %collective-permute-start.4 = (bf16[64,2560]{1,0:T(8,128)(2,1)S(1)}, bf16[64,2560]{1,0:T(8,128)(2,1)S(1)}, u32[]{:S(2)}, u32[]{:S(2)}) collective-permute-start(bf16[64,2560]{1,0:T(8,128)(2,1)S(1)} %get-tuple-element.122), channel_id=1, source_target_pairs={{0,8},{1,9},{2,10},{3,11},{4,12},{5,13},{6,14},{7,15},{8,0},{9,1},... | collective-permute-start | bytes 983048 | tf_op jit(solution)/shard_map/ppermute | solution.py:368
  492.5 2.4 collective-permute-start.6
  495.0 24.5 %heads_grad.1 = (bf16[16,64,1536]{2,1,0:T(8,128)(2,1)}, bf16[16,64,1536]{2,1,0:T(8,128)(2,1)}) custom-call(s32[2]{0:T(128)} %pad_add_fusion.me_ref, bf16[2320,1024]{1,0:T(8,128)(2,1)} %get-tuple-element.97.refs_0_, bf16[3,2320,1024]{2,1,0:T(8,128)(2,1)} %attend_back.3.refs_1_.grad_ref), custom_call_target="tpu_custom_call" | custom-call | tf_op jit(solution)/shard_map/heads_grad/pallas_call | solution.py:52
  521.2 4.2 collective-permute-done.7
  525.4 2.0 add_convert_fusion.4
  530.9 28.0 %qkv_back.1 = (bf16[2308,1024]{1,0:T(8,128)(2,1)}, f32[2,1024]{1,0:T(2,128)}, f32[2,1024]{1,0:T(2,128)}) custom-call(bf16[2308,1024]{1,0:T(8,128)(2,1)} %x_ref.5, bf16[2320,1024]{1,0:T(8,128)(2,1)} %get-tuple-element.128.refs_1_.low_ref, f32[6,1024]{1,0:T(8,128)} %reshape.120.vec_ref, bf16[3,2320,1024]{2,1,0:T(8,128)(2,1)} %attend_back.3.refs_1_.grad_ref, ...), custom_call_target="tpu_custom_call" | custom-call | flops 14596177920 | bytes 35577856 | tf_op jit(solution)/shard_map/qkv_back/pallas_call | solution.py:52
  558.9 6.2 %collective-permute-done.10.refs_3_ = bf16[4,64,1536]{2,1,0:T(8,128)(2,1)} collective-permute-done((bf16[4,64,1536]{2,1,0:T(8,128)(2,1)S(1)}, bf16[4,64,1536]{2,1,0:T(8,128)(2,1)}, u32[]{:S(2)}, u32[]{:S(2)}) %collective-permute-start.10) | collective-permute-done | bytes 786464 | tf_op jit(solution)/shard_map/ppermute | solution.py:368
  565.1 26.3 %tail.1 = (f32[3,64,512]{2,1,0:T(8,128)}, f32[8,128]{1,0:T(8,128)}) custom-call(bf16[4,64,1536]{2,1,0:T(8,128)(2,1)} %get-tuple-element.130.refs_0_, bf16[4,64,1536]{2,1,0:T(8,128)(2,1)} %copy-done.1, bf16[4,64,1536]{2,1,0:T(8,128)(2,1)} %copy-done.2, bf16[4,64,1536]{2,1,0:T(8,128)(2,1)} %collective-permute-done.10.refs_3_, ...), custom_call_target="tpu_custom_call" | custom-call | tf_op jit(solution)/shard_map/tail/pallas_call | solution.py:52
  591.4 1.8 finish.1
  (43 shorter events, 15.4 us)
Async XLA Ops:
  7.2 151.6 %all-gather.2.cloned.1.call-start = ((), (), s32[]{:S(2)}) async-start(), calls=%async_computation.1 | async-start | bytes 19464192 | tf_op jit(solution)/shard_map/all_gather | solution.py:697
  9.4 583.8 %reduce-scatter.2.cloned.1.call-start = ((), (), s32[]{:S(2)}) async-start(), calls=%async_computation.2 | async-start | bytes 8650752 | tf_op jit(solution)/shard_map/reduce_scatter | solution.py:794
  363.9 47.6 %collective-permute-start = (bf16[16,64,2560]{2,1,0:T(8,128)(2,1)}, bf16[16,64,2560]{2,1,0:T(8,128)(2,1)}, u32[]{:S(2)}, u32[]{:S(2)}) collective-permute-start(bf16[16,64,2560]{2,1,0:T(8,128)(2,1)} %get-tuple-element.103), channel_id=1, source_target_pairs={{0,2},{1,3},{2,0},{3,1},{4,6},{5,7},{6,4},{7,5},{8,10},{9,11},{10,... | collective-permute-start | bytes 15728648 | tf_op jit(solution)/shard_map/ppermute | solution.py:368
  418.0 51.0 %collective-permute-start.1 = (bf16[4,64,2560]{2,1,0:T(8,128)(2,1)}, bf16[4,64,2560]{2,1,0:T(8,128)(2,1)S(1)}, u32[]{:S(2)}, u32[]{:S(2)}) collective-permute-start(bf16[4,64,2560]{2,1,0:T(8,128)(2,1)} %get-tuple-element.108), channel_id=1, source_target_pairs={{0,1},{1,0},{2,3},{3,2},{4,5},{5,4},{6,7},{7,6},{8,9},{9,8},{10,11... | collective-permute-start | bytes 3932168 | tf_op jit(solution)/shard_map/ppermute | solution.py:368
  419.4 49.6 %collective-permute-start.2 = (bf16[4,64,2560]{2,1,0:T(8,128)(2,1)}, bf16[4,64,2560]{2,1,0:T(8,128)(2,1)}, u32[]{:S(2)}, u32[]{:S(2)}) collective-permute-start(bf16[4,64,2560]{2,1,0:T(8,128)(2,1)} %get-tuple-element.109), channel_id=1, source_target_pairs={{0,4},{1,5},{2,6},{3,7},{4,0},{5,1},{6,2},{7,3},{8,12},{9,13},{10,... | collective-permute-start | bytes 3932168 | tf_op jit(solution)/shard_map/ppermute | solution.py:368
  419.8 58.7 %collective-permute-start.3 = (bf16[4,64,2560]{2,1,0:T(8,128)(2,1)}, bf16[4,64,2560]{2,1,0:T(8,128)(2,1)}, u32[]{:S(2)}, u32[]{:S(2)}) collective-permute-start(bf16[4,64,2560]{2,1,0:T(8,128)(2,1)} %get-tuple-element.110), channel_id=1, source_target_pairs={{0,5},{1,4},{2,7},{3,6},{4,1},{5,0},{6,3},{7,2},{8,13},{9,12},{10,... | collective-permute-start | bytes 3932168 | tf_op jit(solution)/shard_map/ppermute | solution.py:368
  480.8 38.6 %collective-permute-start.4 = (bf16[64,2560]{1,0:T(8,128)(2,1)S(1)}, bf16[64,2560]{1,0:T(8,128)(2,1)S(1)}, u32[]{:S(2)}, u32[]{:S(2)}) collective-permute-start(bf16[64,2560]{1,0:T(8,128)(2,1)S(1)} %get-tuple-element.122), channel_id=1, source_target_pairs={{0,8},{1,9},{2,10},{3,11},{4,12},{5,13},{6,14},{7,15},{8,0},{9,1},... | collective-permute-start | bytes 983048 | tf_op jit(solution)/shard_map/ppermute | solution.py:368
  492.5 26.9 %collective-permute-start.5 = (bf16[64,2560]{1,0:T(8,128)(2,1)S(1)}, bf16[64,2560]{1,0:T(8,128)(2,1)S(1)}, u32[]{:S(2)}, u32[]{:S(2)}) collective-permute-start(bf16[64,2560]{1,0:T(8,128)(2,1)S(1)} %get-tuple-element.123), channel_id=1, source_target_pairs={{0,16},{1,17},{2,18},{3,19},{4,20},{5,21},{6,22},{7,23},{8,24},{9,... | collective-permute-start | bytes 983048 | tf_op jit(solution)/shard_map/ppermute | solution.py:368
  492.5 26.9 %collective-permute-start.6 = (bf16[64,2560]{1,0:T(8,128)(2,1)S(1)}, bf16[64,2560]{1,0:T(8,128)(2,1)S(1)}, u32[]{:S(2)}, u32[]{:S(2)}) collective-permute-start(bf16[64,2560]{1,0:T(8,128)(2,1)S(1)} %get-tuple-element.124), channel_id=1, source_target_pairs={{0,24},{1,25},{2,26},{3,27},{4,28},{5,29},{6,30},{7,31},{8,16},{9,... | collective-permute-start | bytes 983048 | tf_op jit(solution)/shard_map/ppermute | solution.py:368
  519.5 6.0 copy-start
  519.5 5.9 collective-permute-start.7
  527.4 31.5 %collective-permute-start.8 = (bf16[4,64,1536]{2,1,0:T(8,128)(2,1)S(1)}, bf16[4,64,1536]{2,1,0:T(8,128)(2,1)S(1)}, u32[]{:S(2)}, u32[]{:S(2)}) collective-permute-start(bf16[4,64,1536]{2,1,0:T(8,128)(2,1)S(1)} %get-tuple-element.131), channel_id=1, source_target_pairs={{0,1},{1,0},{2,3},{3,2},{4,5},{5,4},{6,7},{7,6},{8,9},{9,8},{10,11... | collective-permute-start | bytes 2359304 | tf_op jit(solution)/shard_map/ppermute | solution.py:368
  529.1 29.8 %collective-permute-start.9 = (bf16[4,64,1536]{2,1,0:T(8,128)(2,1)S(1)}, bf16[4,64,1536]{2,1,0:T(8,128)(2,1)S(1)}, u32[]{:S(2)}, u32[]{:S(2)}) collective-permute-start(bf16[4,64,1536]{2,1,0:T(8,128)(2,1)S(1)} %get-tuple-element.132), channel_id=1, source_target_pairs={{0,4},{1,5},{2,6},{3,7},{4,0},{5,1},{6,2},{7,3},{8,12},{9,13},{10,... | collective-permute-start | bytes 2359304 | tf_op jit(solution)/shard_map/ppermute | solution.py:368
  529.4 35.8 %collective-permute-start.10 = (bf16[4,64,1536]{2,1,0:T(8,128)(2,1)S(1)}, bf16[4,64,1536]{2,1,0:T(8,128)(2,1)}, u32[]{:S(2)}, u32[]{:S(2)}) collective-permute-start(bf16[4,64,1536]{2,1,0:T(8,128)(2,1)S(1)} %get-tuple-element.133), channel_id=1, source_target_pairs={{0,5},{1,4},{2,7},{3,6},{4,1},{5,0},{6,3},{7,2},{8,13},{9,12},{10,... | collective-permute-start | bytes 2359304 | tf_op jit(solution)/shard_map/ppermute | solution.py:368
  558.9 6.2 %copy-start.1 = (bf16[4,64,1536]{2,1,0:T(8,128)(2,1)}, bf16[4,64,1536]{2,1,0:T(8,128)(2,1)S(1)}, u32[]{:S(2)}) copy-start(bf16[4,64,1536]{2,1,0:T(8,128)(2,1)S(1)} %collective-permute-done.8.refs_1_) | copy-start | bytes 2359300
  558.9 6.2 %copy-start.2 = (bf16[4,64,1536]{2,1,0:T(8,128)(2,1)}, bf16[4,64,1536]{2,1,0:T(8,128)(2,1)S(1)}, u32[]{:S(2)}) copy-start(bf16[4,64,1536]{2,1,0:T(8,128)(2,1)S(1)} %collective-permute-done.9.refs_2_) | copy-start | bytes 2359300
Sparse Core Ops, SparseCore 0:
  11.5 147.2 all-gather.1
  258.9 157.3 reduce-scatter.1

commit v3 on v2

--- a/solution.py
+++ b/solution.py
@@ -19,7 +19,7 @@
 NN = (((1,), (0,)), ((), ()))
 NT = (((1,), (1,)), ((), ()))
 TN = (((0,), (0,)), ((), ()))
-VMEM_BYTES = 60 * 2**20
+MIB = 2**20
 AXES = ("tensor", "dp")
 
 
@@ -44,7 +44,7 @@
     return pl.BlockSpec(shape, lambda *_: (0,) * len(shape), pipeline_mode=pl.Buffered(1))
 
 
-def call(kernel, name, grid, in_specs, out_specs, out_shape, args, scratch=(), flops=0, prefetch=0, aliases={}, **params):
+def call(kernel, name, grid, in_specs, out_specs, out_shape, args, scratch=(), flops=0, prefetch=0, vmem=40, **params):
     moved = 0
     if flops:
         moved = sum(a.size * a.dtype.itemsize for a in args)
@@ -59,8 +59,7 @@
             scratch_shapes=list(scratch),
         ),
         out_shape=[jax.ShapeDtypeStruct(shape, dtype) for shape, dtype in out_shape],
-        input_output_aliases=aliases,
-        compiler_params=pltpu.CompilerParams(vmem_limit_bytes=VMEM_BYTES, **params),
+        compiler_params=pltpu.CompilerParams(vmem_limit_bytes=vmem * MIB, **params),
         cost_estimate=pl.CostEstimate(flops=2 * flops, bytes_accessed=moved, transcendentals=0),
         name=name,
     )(*args)
@@ -77,7 +76,7 @@
     normed = (hat * vec_ref[0:1] + vec_ref[1:2]).astype(bf16)
     normed_ref[...] = normed
     tensor, dp = w_ref.shape[:2]
-    width = w_ref.shape[3] // 3
+    width = w_ref.shape[3] // 4
     for s in range(3):
         for t in range(tensor):
             cols = slice(t * width, (t + 1) * width)
@@ -121,8 +120,7 @@
     stat_ref[0] = jnp.concatenate(stats, axis=1).T
 
 
-def attend_back_kernel(triple_ref, stat_ref, grad_ref, *refs):
-    out_ref = refs[-1]
+def attend_back_kernel(triple_ref, stat_ref, grad_ref, out_ref):
     image = pl.program_id(1)
     rows = lax.broadcasted_iota(jnp.int32, (WINDOW, 1), 0)
     mask = jnp.where((rows >= image) & (rows < image + SEQ), 0.0, -1e30)
@@ -139,16 +137,23 @@
         grad_probs = matmul(triple_ref[2, own, cols], grad, NT)
         inner = jnp.sum(probs * grad_probs, axis=0, keepdims=True)
         grad_scores = (probs * (grad_probs - inner)).astype(bf16)
-        keep_before(image, out_ref, (2, cols), matmul(probs.astype(bf16), grad))
-        keep_before(image, out_ref, (1, cols), matmul(grad_scores, query) * LOG_SCALE)
+        blank = jnp.zeros_like(grad)
+        left = jnp.concatenate([probs.astype(bf16), grad_scores], axis=1)
+        right = jnp.concatenate(
+            [jnp.concatenate([grad, blank], axis=1), jnp.concatenate([blank, query], axis=1)], axis=0
+        )
+        pair = matmul(left, right)
+        keep_before(image, out_ref, (2, cols), pair[:, :HEAD_DIM])
+        keep_before(image, out_ref, (1, cols), pair[:, HEAD_DIM:] * LOG_SCALE)
         keep_before(image, out_ref, (0, cols), (matmul(keys.T, grad_scores) * LOG_SCALE).T)
 
 
-def merge_kernel(count, ctx_ref, x_ref, vec_ref, w_ref, resid_ref, normed_ref):
-    tensor, dp, rows, width = w_ref.shape
+def merge_kernel(part, count, ctx_ref, x_ref, vec_ref, w_ref, resid_ref, normed_ref):
+    tensor, dp = w_ref.shape[:2]
+    width = w_ref.shape[3] // 4
     total = before(x_ref, count) + vec_ref[2:3]
     for t in range(tensor):
-        w = w_ref[t].reshape(dp * rows, width)
+        w = w_ref[t, :, :part, 3 * width :].reshape(dp * part, width)
         total = total + matmul(ctx_ref[:, t * width : (t + 1) * width], w, NT)
     resid_ref[...] = total
     hat, _ = norm_parts(total)
@@ -156,23 +161,25 @@
 
 
 def mlp_kernel(
-    chunk, live_ref, normed_ref, resid_ref, ebias_ref, vec_ref, e_ref, r_ref, given_ref,
+    chunk, live_ref, normed_ref, resid_ref, ebias_ref, vec_ref, w_ref, given_ref,
     out_ref, act_ref, slope_ref, grad_ref,
 ):
     grad_ref[...] = before(given_ref, live_ref[0]).astype(bf16)
-    tensor, dp, rows, width = e_ref.shape
+    tensor, dp, rows, width = w_ref.shape
+    width = width // 2
     normed = normed_ref[...]
     total = resid_ref[...] + vec_ref[5:6]
     for t in range(tensor):
         for c in range(width // chunk):
             local = slice(c * chunk, (c + 1) * chunk)
+            other = slice(width + c * chunk, width + (c + 1) * chunk)
             cols = slice(t * width + c * chunk, t * width + (c + 1) * chunk)
-            e = e_ref[t, :, :, local].reshape(dp * rows, chunk)
+            e = w_ref[t, :, :, local].reshape(dp * rows, chunk)
             active, slope = gelu_and_slope(matmul(normed, e) + ebias_ref[:, cols])
             active = active.astype(bf16)
             act_ref[:, cols] = active
             slope_ref[:, cols] = slope.astype(bf16)
-            r = r_ref[t, :, :, local].reshape(dp * rows, chunk)
+            r = w_ref[t, :, :, other].reshape(dp * rows, chunk)
             total = total + matmul(active, r, NT)
     out_ref[...] = total.astype(bf16)
 
@@ -199,10 +206,11 @@
 
 
 def mlp_back_kernel(
-    chunk, grad_ref, slope_ref, resid_ref, vec_ref, e_ref, r_ref, m_ref,
+    part, chunk, grad_ref, slope_ref, resid_ref, vec_ref, w_ref, m_ref,
     pre_ref, low_ref, ctx_ref, sums_ref, esum_ref,
 ):
-    tensor, dp, rows, width = e_ref.shape
+    tensor, dp, rows, width = w_ref.shape
+    width = width // 2
     first = pl.program_id(0) == 0
     grad = grad_ref[...]
     total = jnp.zeros(grad.shape, f32)
@@ -210,31 +218,28 @@
     for t in range(tensor):
         for c in range(width // chunk):
             local = slice(c * chunk, (c + 1) * chunk)
+            other = slice(width + c * chunk, width + (c + 1) * chunk)
             cols = slice(t * width + c * chunk, t * width + (c + 1) * chunk)
-            r = r_ref[t, :, :, local].reshape(dp * rows, chunk)
+            r = w_ref[t, :, :, other].reshape(dp * rows, chunk)
             pre = (matmul(grad, r) * slope_ref[:, cols].astype(f32)).astype(bf16)
             pre_ref[:, cols] = pre
             parts.append(jnp.sum(pre.astype(f32), axis=0, keepdims=True))
-            e = e_ref[t, :, :, local].reshape(dp * rows, chunk)
+            e = w_ref[t, :, :, local].reshape(dp * rows, chunk)
             total = total + matmul(pre, e, NT)
-    grad = grad.astype(f32)
-    back, gain_sum, shift_sum = norm_back(resid_ref[...], vec_ref[3:4], total)
-    resid_grad = grad + back
-    low = resid_grad.astype(bf16)
-    low_ref[...] = low
+    sums = 0
+    half = grad.shape[0] // 2
+    for rows_half in (slice(0, half), slice(half, 2 * half)):
+        own = grad_ref[rows_half].astype(f32)
+        back, gain_sum, shift_sum = norm_back(resid_ref[rows_half], vec_ref[3:4], total[rows_half])
+        resid_grad = own + back
+        low_ref[rows_half] = resid_grad.astype(bf16)
+        lines = [jnp.sum(own, axis=0, keepdims=True), gain_sum, shift_sum]
+        sums = sums + jnp.concatenate(lines + [jnp.sum(resid_grad, axis=0, keepdims=True)], axis=0)
+    low = low_ref[...]
     wide = m_ref.shape[3]
     for t in range(tensor):
-        m = m_ref[t].reshape(dp * rows, wide)
+        m = m_ref[t, :, :part].reshape(dp * part, wide)
         ctx_ref[:, t * wide : (t + 1) * wide] = matmul(low, m).astype(bf16)
-    sums = jnp.concatenate(
-        [
-            jnp.sum(grad, axis=0, keepdims=True),
-            gain_sum,
-            shift_sum,
-            jnp.sum(resid_grad, axis=0, keepdims=True),
-        ],
-        axis=0,
-    )
     accumulate(first, sums_ref, sums)
     parts = jnp.concatenate(parts, axis=1)
     lines = [parts[:, k * 128 : (k + 1) * 128] for k in range(esum_ref.shape[0])]
@@ -243,7 +248,7 @@
 
 def qkv_back_kernel(part, count, x_ref, low_ref, vec_ref, grad_ref, w_ref, out_ref, sums_ref, bsum_ref):
     tensor, dp = w_ref.shape[:2]
-    width = w_ref.shape[3] // 3
+    width = w_ref.shape[3] // 4
     first = pl.program_id(0) == 0
     total = jnp.zeros(x_ref.shape, f32)
     for s in range(3):
@@ -259,16 +264,12 @@
 
 def weight_grad_kernel(starts, *refs):
     count = len(starts) - 1
-    lefts, rights, out_ref, turned = refs[:count], refs[count : 2 * count], refs[-2], refs[-1]
+    lefts, rights, out_ref = refs[:count], refs[count : 2 * count], refs[-1]
     step = pl.program_id(0)
     for j in range(count):
         @pl.when((step >= starts[j]) & (step < starts[j + 1]))
         def _():
-            @pl.when(step == starts[j])
-            def _():
-                turned[...] = lefts[j][...].T
-
-            out = matmul(turned[...], rights[j][0])
+            out = matmul(lefts[j][...], rights[j][0], TN)
             out_ref[...] = out.astype(bf16).reshape(out_ref.shape)
 
 
@@ -303,60 +304,116 @@
         [pl.BlockSpec((1, dp, deep // dp, block), out_map)],
         [((tensor, dp, deep // dp, sum(locals_)), bf16)],
         [left for left, _ in pairs] + [right[None] for _, right in pairs],
-        [pltpu.VMEM((deep, rows), bf16)],
         flops=rows * deep * tensor * sum(locals_),
     )[0]
 
 
-def slot_grad_kernel(tensor, dp, starts, me_ref, *refs):
-    count = len(starts) - 1
-    lefts, rights = refs[:count], refs[count : 2 * count]
-    keep_ref, send_ref, turned, total = refs[2 * count :]
+def flip(value, mask):
+    unit = 1
+    while unit <= mask:
+        if mask & unit:
+            value = value + unit - 2 * unit * lax.rem(lax.div(value, unit), 2)
+        unit *= 2
+    return value
+
+
+def differ(left, right, size):
+    total, unit = 0, 1
+    while unit < size:
+        p, q = lax.rem(lax.div(left, unit), 2), lax.rem(lax.div(right, unit), 2)
+        total = total + unit * (p + q - 2 * p * q)
+        unit *= 2
+    return total
+
+
+def slot_grad_kernel(tensor, dp, starts, *refs):
+    count, steps, depth = len(starts) - 1, starts[-1], dp // 4
+    lefts, rights, outs = refs[:count], refs[count : 2 * count], refs[2 * count : 2 * count + 2 * tensor]
+    total, keep, send, landed, send_sem, recv_sem = refs[2 * count + 2 * tensor :]
     step, t = pl.program_id(0), pl.program_id(1)
+    d, y = lax.axis_index("dp"), lax.axis_index("tensor")
+    part, block = total.shape[0] // dp, total.shape[1]
+    column = differ(t, y, tensor)
+    slots = pl.ds(column * (2 * depth), 2 * depth)
+
+    def copy(step):
+        cols = pl.ds(pl.multiple_of(step * block, block), block)
+        return pltpu.make_async_remote_copy(
+            src_ref=send.at[slots, :, cols],
+            dst_ref=landed.at[slots, :, cols],
+            send_sem=send_sem.at[step * tensor + t],
+            recv_sem=recv_sem.at[step * tensor + t],
+            device_id=(flip(d, 1), y),
+            device_id_type=pl.DeviceIdType.MESH,
+        )
+
+    @pl.when((step == 0) & (t == 0))
+    def _():
+        barrier = pltpu.get_barrier_semaphore()
+        pl.semaphore_signal(
+            barrier, inc=1, device_id=(flip(d, 1), y), device_id_type=pl.DeviceIdType.MESH
+        )
+        pl.semaphore_wait(barrier, 1)
+
     for j in range(count):
         @pl.when((step >= starts[j]) & (step < starts[j + 1]))
         def _():
-            @pl.when((step == starts[j]) & (t == 0))
+            total[...] = matmul(lefts[j][...], rights[j][0], TN)
+
+    @pl.when(step < steps)
+    def _():
+        cols = pl.ds(pl.multiple_of(step * block, block), block)
+        for r in range(dp):
+            owner = pl.multiple_of(flip(d, r) * part, part)
+            half = send if r & 1 else keep
+            slot = column * (2 * depth) + ((r >> 1) & 1) * depth + (r >> 2)
+            half[slot, :, cols] = total[pl.ds(owner, part), :].astype(bf16)
+        copy(step).start()
+
+    @pl.when(step > 0)
+    def _():
+        copy(step - 1).wait()
+        cols = pl.ds(pl.multiple_of((step - 1) * block, block), block)
+        for k in range(2 * tensor):
+            @pl.when(column == k // 2)
             def _():
-                turned[...] = lefts[j][...].T
-
-            total[...] = matmul(turned[...], rights[j][0])
-    part = total.shape[0] // dp
-    depth = dp // 4
-    column = t ^ me_ref[1]
-    for r in range(dp):
-        owner = me_ref[0] ^ r
-        slot = (((r >> 1) & 1) * tensor + column) * depth + (r >> 2)
-        half = send_ref if r & 1 else keep_ref
-        half[slot] = total[pl.ds(pl.multiple_of(owner * part, part), part), :].astype(bf16)
-
-
-def slot_grads(name, pairs, tensor, dp, me, block):
+                own = pl.ds(k * depth, depth)
+                both = keep[own, :, cols].astype(f32) + landed[own, :, cols].astype(f32)
+                outs[k][...] = both.astype(bf16)
+
+
+def slot_grads(name, pairs, tensor, dp, block, collective_id):
     rows, deep = pairs[0][0].shape
+    part, depth = deep // dp, dp // 4
     block = min([block] + [right.shape[2] // tensor for _, right in pairs])
     pers = [right.shape[2] // tensor // block for _, right in pairs]
     starts = [0]
     for (_, right), per in zip(pairs, pers):
         starts.append(starts[-1] + right.shape[0] * per)
+    wide = starts[-1] * block
     half = tensor * dp // 2
 
-    def right_map(j, i, t, me):
+    def right_map(j, i, t):
+        t = jnp.where(i < starts[j], 0, jnp.where(i >= starts[j + 1], tensor - 1, t))
         i = jnp.clip(i - starts[j], 0, starts[j + 1] - starts[j] - 1)
         return (i // pers[j], 0, t * pers[j] + i % pers[j])
 
-    left_spec = pl.BlockSpec((rows, deep), lambda i, t, me: (0, 0), pipeline_mode=pl.Buffered(1))
-    spec = pl.BlockSpec((half, deep // dp, block), lambda i, t, me: (0, 0, i))
+    spec = pl.BlockSpec((depth, part, block), lambda i, t: (0, 0, jnp.maximum(i - 1, 0)))
     return call(
         functools.partial(slot_grad_kernel, tensor, dp, starts),
         name,
-        (starts[-1], tensor),
-        [left_spec] * len(pairs)
+        (starts[-1] + 1, tensor),
+        [full((rows, deep))] * len(pairs)
         + [pl.BlockSpec((1, rows, block), functools.partial(right_map, j)) for j in range(len(pairs))],
-        [spec, spec],
-        [((half, deep // dp, starts[-1] * block), bf16)] * 2,
-        [me] + [left for left, _ in pairs] + [right for _, right in pairs],
-        [pltpu.VMEM((deep, rows), bf16), pltpu.VMEM((deep, block), f32)],
-        prefetch=1,
+        [spec] * (2 * tensor),
+        [((depth, part, wide), bf16)] * (2 * tensor),
+        [left for left, _ in pairs] + [right for _, right in pairs],
+        [pltpu.VMEM((deep, block), f32)]
+        + [pltpu.VMEM((half, part, wide), bf16)] * 3
+        + [pltpu.SemaphoreType.DMA((starts[-1] * tensor,))] * 2,
+        vmem=56,
+        collective_id=collective_id,
+        has_side_effects=True,
     )
 
 
@@ -368,17 +425,8 @@
     return lax.ppermute(values, ("dp", "tensor"), moves)
 
 
-def sum_cores(keep, other, tensor, dp):
-    depth = dp // 4
-    parts = []
-    for k in range(2 * tensor):
-        own = slice(k * depth, (k + 1) * depth)
-        parts.append((keep[own].astype(f32) + other[own].astype(f32)).astype(bf16))
-    return parts
-
-
 def send_plane(parts, tensor, dp):
-    return [swap(parts[k], 2 * (k // tensor), k % tensor, tensor, dp) for k in range(1, 2 * tensor)]
+    return [swap(parts[k], 2 * (k % 2), k // 2, tensor, dp) for k in range(1, 2 * tensor)]
 
 
 def sum_plane(part, landed, dp):
@@ -422,11 +470,11 @@
     used = sum(piece.shape[1] for piece in pieces)
     pieces.append(jnp.zeros((8, 128 - used), f32))
     first_ref[part:, :128] = jnp.concatenate(pieces, axis=1).astype(bf16)
-    first_ref[part:, 128:] = jnp.zeros((8, 3 * own - 128), bf16)
+    first_ref[:part, 3 * own :] = merge_ref[...]
+    first_ref[part:, 128:] = jnp.zeros((8, 4 * own - 128), bf16)
     hidden = expand_ref.shape[1]
     later_ref[:, :hidden] = expand_ref[...]
-    later_ref[:, hidden : 2 * hidden] = reduce_ref[...]
-    later_ref[:, 2 * hidden :] = merge_ref[...]
+    later_ref[:, hidden:] = reduce_ref[...]
 
 
 def gather_kernel(in_ref, out_ref, own_sem, send_sem, recv_sem):
@@ -439,12 +487,17 @@
         pz, px, pc, py = place
         return (pz * 2 + px) * 2 + pc, py
 
-    lines = [lax.rem(z + k, 4) for k in range(1, 4)]
-    peers = [(other, x, c, y) for other in lines] + [(z, far_x, c, y), (z, x, c, far_y), (z, x, far_c, y)]
-    to_x, to_y, to_c = peers[3:]
-    for peer in peers:
+    lower, upper = (z - 1, x, c, y), (z + 1, x, c, y)
+    to_x, to_y, to_c = (z, far_x, c, y), (z, x, c, far_y), (z, x, far_c, y)
+
+    def greet(peer):
         pl.semaphore_signal(barrier, inc=1, device_id=index(peer), device_id_type=pl.DeviceIdType.MESH)
-    pl.semaphore_wait(barrier, len(peers))
+
+    for peer in (to_x, to_y, to_c):
+        greet(peer)
+    pl.when(z > 0)(lambda: greet(lower))
+    pl.when(z < 3)(lambda: greet(upper))
+    pl.semaphore_wait(barrier, 4 + lax.rem(lax.div(z + 1, 2), 2))
 
     sent = []
 
@@ -459,45 +512,61 @@
             device_id_type=pl.DeviceIdType.MESH,
         )
 
-    def send(owner, peer, source=None):
-        out = copy(owner, peer, len(sent), source)
-        out.start()
-        sent.append(out)
-
-    def arrive(owner):
-        copy(owner, to_c, 0).wait_recv()
+    def send(owner, peer, there, source=None):
+        slot = len(sent)
+        sent.append((owner, peer, slot, there))
+
+        @pl.when(there)
+        def _():
+            copy(owner, peer, slot, source).start()
+
+    def arrive(owner, there):
+        @pl.when(there)
+        def _():
+            copy(owner, to_c, 0).wait_recv()
 
     own = (z, x, c, y)
-    for peer in peers:
-        send(own, peer, in_ref)
     keep = pltpu.make_async_copy(in_ref, out_ref.at[y, d], own_sem)
+    send(own, upper, z < 3, in_ref)
+    send(own, lower, z > 0, in_ref)
+    for peer in (to_x, to_y, to_c):
+        send(own, peer, z >= 0, in_ref)
     keep.start()
-    for other in lines:
-        block = (other, x, c, y)
-        arrive(block)
-        for peer in (to_x, to_y, to_c):
-            send(block, peer)
-    for level in range(4):
-        block = (level, far_x, c, y)
-        arrive(block)
-        if level % 2 == 0:
-            send(block, to_y)
-        send(block, to_c)
-        block = (level, x, c, far_y)
-        arrive(block)
-        if level % 2 == 1:
-            send(block, to_x)
-        send(block, to_c)
-    for level in range(4):
-        block = (level, far_x, c, far_y)
-        arrive(block)
-        send(block, to_c)
+    for far in range(1, 4):
+        for sign, after, onward in ((-1, upper, z < 3), (1, lower, z > 0)):
+            level = z + sign * far
+            there = (level >= 0) & (level <= 3)
+            block = (level, x, c, y)
+            arrive(block, there)
+            send(block, after, there & onward)
+            for peer in (to_x, to_y, to_c):
+                send(block, peer, there)
+    for far in range(4):
+        for sign in (-1, 1) if far else (1,):
+            level = z + sign * far
+            there = (level >= 0) & (level <= 3)
+            odd = lax.rem(level + 4, 2)
+            block = (level, far_x, c, y)
+            arrive(block, there)
+            send(block, to_y, there & (odd == 0))
+            send(block, to_c, there)
+            block = (level, x, c, far_y)
+            arrive(block, there)
+            send(block, to_x, there & (odd == 1))
+            send(block, to_c, there)
+    for far in range(4):
+        for sign in (-1, 1) if far else (1,):
+            level = z + sign * far
+            there = (level >= 0) & (level <= 3)
+            block = (level, far_x, c, far_y)
+            arrive(block, there)
+            send(block, to_c, there)
     for level in range(4):
         for px in range(2):
             for py in range(2):
-                arrive((level, px, far_c, py))
-    for out in sent:
-        out.wait_send()
+                arrive((level, px, far_c, py), z >= 0)
+    for owner, peer, slot, there in sent:
+        pl.when(there)(lambda: copy(owner, peer, slot).wait_send())
     keep.wait()
 
 
@@ -513,7 +582,7 @@
         [pl.BlockSpec(memory_space=pl.ANY)],
         [(shape, bf16)],
         (shard,),
-        [pltpu.SemaphoreType.DMA, pltpu.SemaphoreType.DMA((31,)), pltpu.SemaphoreType.DMA((32,))],
+        [pltpu.SemaphoreType.DMA, pltpu.SemaphoreType.DMA((64,)), pltpu.SemaphoreType.DMA((32,))],
         collective_id=1,
         has_side_effects=True,
     )[0]
@@ -705,7 +774,7 @@
     vmem = pl.BlockSpec(memory_space=pltpu.VMEM)
     first, later = call(
         pack_kernel, "pack", (), [vmem] * len(arrays), [vmem] * 2,
-        [((part + 8, 3 * own), bf16), ((part, 2 * hidden_own + own), bf16)], arrays,
+        [((part + 8, 4 * own), bf16), ((part, 2 * hidden_own), bf16)], arrays,
     )
     wide = gather(later)
     wide_heads = gather_first(first, tensor, dp)
@@ -721,17 +790,13 @@
     def by_rows(width):
         return pl.BlockSpec((block, width), lambda i, *_: (i, 0))
 
-    def column(index, width):
-        shape = (tensor, dp, part, width)
-        return pl.BlockSpec(shape, lambda *_: (0, 0, 0, index), pipeline_mode=pl.Buffered(1))
-
     vec = full((6, deep))
     triple_spec = pl.BlockSpec((3, block, deep), lambda i: (0, i, 0))
     normed_one, triple = call(
         functools.partial(qkv_kernel, part, rows),
         "qkv",
         (blocks,),
-        [by_rows(deep), vec, full((2, deep)), full(wide_heads.shape)],
+        [by_rows(deep), vec, full((2, deep)), vmem],
         [by_rows(deep), triple_spec],
         [((total_rows, deep), bf16), ((3, total_rows, deep), bf16)],
         (activations, vectors, hb, wide_heads),
@@ -756,18 +821,14 @@
         flops=attend_flops,
     )
 
-    merge_width, expand_width = merge_weight.shape[0], hidden_own
-    expand_spec = column(0, expand_width)
-    reduce_spec = column(1, expand_width)
-    merge_spec = column(2 * expand_width // merge_width, merge_width)
     resid, normed_two = call(
-        functools.partial(merge_kernel, rows),
+        functools.partial(merge_kernel, part, rows),
         "merge",
         (blocks,),
-        [by_rows(deep), by_rows(deep), vec, merge_spec],
+        [by_rows(deep), by_rows(deep), vec, vmem],
         [by_rows(deep), by_rows(deep)],
         [((total_rows, deep), f32), ((total_rows, deep), bf16)],
-        (context, activations, vectors, wide),
+        (context, activations, vectors, wide_heads),
         flops=total_rows * deep * deep,
     )
 
@@ -777,16 +838,17 @@
         "mlp",
         (blocks,),
         [
-            by_rows(deep), by_rows(deep), full((1, hidden)), vec, expand_spec, reduce_spec, by_rows(deep),
+            by_rows(deep), by_rows(deep), full((1, hidden)), vec, vmem, by_rows(deep),
         ],
         [by_rows(deep), by_rows(hidden), by_rows(hidden), by_rows(deep)],
         [
             ((rows, deep), bf16), ((total_rows, hidden), bf16), ((total_rows, hidden), bf16),
             ((total_rows, deep), bf16),
         ],
-        (live, normed_two, resid, eb, vectors, wide, wide, output_grad),
+        (live, normed_two, resid, eb, vectors, wide, output_grad),
         prefetch=1,
         flops=total_rows * deep * hidden * 2,
+        vmem=44,
     )
 
     def scatter(grads):
@@ -799,12 +861,15 @@
 
     back_chunk = min(512, hidden_own)
     pre_grad, resid_low, grad_context, sums_two, esum = call(
-        functools.partial(mlp_back_kernel, back_chunk),
+        functools.partial(mlp_back_kernel, part, back_chunk),
         "mlp_back",
         (blocks,),
         [
             by_rows(deep), by_rows(hidden), by_rows(deep), vec,
-            expand_spec, reduce_spec, merge_spec,
+            vmem,
+            pl.BlockSpec(
+                (tensor, dp, part + 8, own), lambda i: (0, 0, 0, 3), pipeline_mode=pl.Buffered(1)
+            ),
         ],
         [
             by_rows(hidden), by_rows(deep), by_rows(deep),
@@ -814,62 +879,44 @@
             ((total_rows, hidden), bf16), ((total_rows, deep), bf16), ((total_rows, deep), bf16),
             ((4, deep), f32), ((hidden // 128, 128), f32),
         ],
-        (grad, slope, resid, vectors, wide, wide, wide),
-    )
-    me = jnp.stack([lax.axis_index("dp"), lax.axis_index("tensor")]).astype(jnp.int32)
-    keep, send = slot_grads(
-        "middle_grad", [(normed_two, pre_grad[None]), (resid_low, context[None])], tensor, dp, me, 512
-    )
-    grad_context, keep, send = lax.optimization_barrier((grad_context, keep, send))
-    other = swap(send, 1, 0, tensor, dp)
-
-    def attend_back(first, before, grad_context):
-        count = groups // 2
-        return call(
-            attend_back_kernel,
-            "attend_back",
-            (count, images),
-            [
-                pl.BlockSpec((3, total_rows, panel), lambda g, i: (0, 0, first + g)),
-                pl.BlockSpec((1, group, WINDOW), lambda g, i: ((first + g) * images + i, 0, 0)),
-                pl.BlockSpec((total_rows, panel), lambda g, i: (0, first + g)),
-            ] + [pl.BlockSpec(memory_space=pl.ANY)] * len(before),
-            [pl.BlockSpec((3, total_rows, panel), lambda g, i: (0, 0, first + g))],
-            [((3, total_rows, deep), bf16)],
-            (triple, stat, grad_context) + before,
-            aliases={3: 0} if before else {},
-        )[0]
-
-    grad_triple = attend_back(0, (), grad_context)
-    keep, other, grad_triple = lax.optimization_barrier((keep, other, grad_triple))
-    parts = sum_cores(keep, other, tensor, dp)
+        (grad, slope, resid, vectors, wide, wide_heads),
+        vmem=44,
+    )
+    parts = slot_grads(
+        "middle_grad", [(normed_two, pre_grad[None]), (resid_low, context[None])], tensor, dp, 512, 2
+    )
     *parts, grad_context = lax.optimization_barrier((*parts, grad_context))
     landed = send_plane(parts, tensor, dp)
-    grad_triple = attend_back(groups // 2, (grad_triple,), grad_context)
+    grad_triple = call(
+        attend_back_kernel,
+        "attend_back",
+        (groups, images),
+        [head_spec, stat_spec, ctx_spec],
+        [head_spec],
+        [((3, total_rows, deep), bf16)],
+        (triple, stat, grad_context),
+    )[0]
     *landed, part_own, grad_triple = lax.optimization_barrier((*landed, parts[0], grad_triple))
     planes = sum_plane(part_own, landed, dp)
     *planes, grad_triple = lax.optimization_barrier((*planes, grad_triple))
     landed = send_line(planes, tensor, dp)
-    keep, send = slot_grads("heads_grad", [(normed_one, grad_triple)], tensor, dp, me, 512)
-    resid_low, keep, send, *landed = lax.optimization_barrier((resid_low, keep, send, *landed))
-    grad_middle = sum_line(planes[0], landed)
-
-    other = swap(send, 1, 0, tensor, dp)
-    parts = sum_cores(keep, other, tensor, dp)
-    *parts, resid_low = lax.optimization_barrier((*parts, resid_low))
-    landed = send_plane(parts, tensor, dp)
+    parts = slot_grads("heads_grad", [(normed_one, grad_triple)], tensor, dp, 512, 3)
+    held = (tuple(parts), tuple(landed), planes[0], resid_low)
+    parts, landed, plane_own, resid_low = lax.optimization_barrier(held)
+    last = send_plane(parts, tensor, dp)
+    grad_middle = sum_line(plane_own, landed)
     input_grad, sums_one, bsum = call(
         functools.partial(qkv_back_kernel, part, rows),
         "qkv_back",
         (blocks,),
-        [by_rows(deep), by_rows(deep), vec, triple_spec, full(wide_heads.shape)],
+        [by_rows(deep), by_rows(deep), vec, triple_spec, vmem],
         [by_rows(deep), pl.BlockSpec((2, deep), lambda i: (0, 0)), pl.BlockSpec((2, deep), lambda i: (0, 0))],
         [((rows, deep), bf16), ((2, deep), f32), ((2, deep), f32)],
         (activations, resid_low, vectors, grad_triple, wide_heads),
         flops=total_rows * deep * deep * 3,
     )
 
-    heads_sum, sums = tail(parts[0], landed, (sums_one, sums_two), bsum, esum, tensor, dp)
+    heads_sum, sums = tail(parts[0], last, (sums_one, sums_two), bsum, esum, tensor, dp)
     grad_heads, hb_grad, eb_grad, *vector = call(
         finish_kernel, "finish", (), [vmem] * 2, [vmem] * 9,
         [(heads_sum.shape, f32), ((2, hbs[2], hbs[1]), f32), (ebs[::-1], f32)] + [((1, part), f32)] * 6,
@@ -884,11 +931,11 @@
         vector[1],
         grad_heads,
         hb_grad.transpose(0, 2, 1),
-        grad_middle[:, expand_width:].T,
+        grad_middle[:, hidden_own:].T,
         vector[2],
         vector[3],
         vector[4],
-        grad_middle[:, :expand_width],
+        grad_middle[:, :hidden_own],
         eb_grad.T,
         grad_reduce.astype(f32).T,
         vector[5],

time: 610 us -> 599 us (0.982)
  waiting for transfers between devices: 33.9 us -> 2.3 us
  local copies, waits for them, and re-layouts: 4.56 us -> 34.1 us
  other arithmetic: 14.2 us -> 2.59 us
  Pallas kernels: 513 us -> 524 us
  starting transfers between devices: 21.6 us -> 11.6 us
    unnamed x6 -> x56, local copies, waits for them, and re-layouts: 0.01 us -> 31.4 us
    ppermute x11 -> x9, waiting for transfers between devices: 19.9 us -> 2.27 us  [swap(): return lax.ppermute(values, ('dp', 'tensor'), moves)]
    all_gather x1, waiting for transfers between devices: 13.9 us -> 0.01 us  [gather(): out = lax.all_gather(shard, AXES, axis=0, tiled=True)]
    pallas_call x15 -> x14, Pallas kernels: 513 us -> 524 us  [call(): pl.pallas_call(kernel, grid_spec=pltpu.PrefetchScalarGridSpec(num_scalar_...]
    ppermute x11 -> x9, starting transfers between devices: 21.5 us -> 11.6 us  [swap(): return lax.ppermute(values, ('dp', 'tensor'), moves)]
    convert_element_type x2 -> x0, other arithmetic: 8.49 us -> none  [sum_cores(): parts.append((keep[own].astype(f32) + other[own].astype(f32)).astype(bf16))]
  transfers between devices with their start and end apart: 13 -> 11, of which waited for: 4 -> 2; matrix products, arithmetic and copies ran while one was open for 3% -> 1% of each run, Pallas kernels for 68% -> 74%
where the time goes in v3:
time: 599 us; the launch traced here: 590 us
  Pallas kernels  524 us (87%)
  local copies, waits for them, and re-layouts  34.1 us (6%)
  between operations  15.4 us (3%)
  starting transfers between devices  11.6 us (2%)
    pallas_call x14, Pallas kernels, call(): pl.pallas_call(kernel, grid_spec=pltpu.PrefetchScalarGridSpec(num_scalar_...  524 us
    unnamed x56, local copies, waits for them, and re-layouts  31.4 us
  transfers between devices with their start and end apart: 11, of which 2 were waited for; matrix products, arithmetic and copies ran while one was open for 1% of the time, Pallas kernels for 74%

profile of v3, /device:TPU:0, one launch (start us, length us, event | category | flops | bytes accessed | tf_op | source)
XLA Modules:
  0.0 590.1 jit_solution(2544607044720286595)
XLA Ops:
  17.8 72.1 %gather.1.w_ref.m_ref = bf16[2,16,72,2048]{3,2,1,0:T(8,128)(2,1)S(1)} custom-call(bf16[72,2048]{1,0:T(8,128)(2,1)S(1)} %get-tuple-element.80.in_ref), custom_call_target="tpu_custom_call" | custom-call | tf_op jit(solution)/shard_map/gather/pallas_call | solution.py:52
  89.9 3.5 copy-done
  94.8 2.3 copy-done.7
  97.1 23.4 %qkv.1 = (bf16[2320,1024]{1,0:T(8,128)(2,1)S(1)}, bf16[3,2320,1024]{2,1,0:T(8,128)(2,1)}) custom-call(bf16[2308,1024]{1,0:T(8,128)(2,1)S(1)} %copy-done.7, f32[6,1024]{1,0:T(8,128)S(1)} %reshape.120.vec_ref, f32[2,1024]{1,0:T(2,128)S(1)} %reshape.122.bias_ref, bf16[2,16,72,2048]{3,2,1,0:T(8,128)(2,1)} %copy-done), custom_call_target="tpu_custom_call" | custom-call | flops 14596177920 | bytes 33202176 | tf_op jit(solution)/shard_map/qkv/pallas_call | solution.py:52
  120.5 2.1 copy-done.4
  122.6 52.6 %attend.1 = (bf16[2320,1024]{1,0:T(8,128)(2,1)S(1)}, f32[16,4,592]{2,1,0:T(4,128)S(1)}) custom-call(bf16[3,2320,1024]{2,1,0:T(8,128)(2,1)} %get-tuple-element.81.triple_ref), custom_call_target="tpu_custom_call" | custom-call | flops 29796335616 | bytes 19156992 | tf_op jit(solution)/shard_map/attend/pallas_call | solution.py:52
  175.3 13.4 %merge.1 = (f32[2320,1024]{1,0:T(8,128)}, bf16[2320,1024]{1,0:T(8,128)(2,1)S(1)}) custom-call(bf16[2320,1024]{1,0:T(8,128)(2,1)S(1)} %get-tuple-element.82.ctx_ref, bf16[2308,1024]{1,0:T(8,128)(2,1)S(1)} %bitcast.53, f32[6,1024]{1,0:T(8,128)S(1)} %reshape.120.vec_ref, bf16[2,16,72,2048]{3,2,1,0:T(8,128)(2,1)} %copy-done), custom_call_target="tpu_custom_call" | custom-call | flops 4865392640 | bytes 33193984 | tf_op jit(solution)/shard_map/merge/pallas_call | solution.py:52
  188.7 2.1 copy-done.1
  190.9 2.1 copy-done.6
  193.0 2.3 copy-done.22
  195.3 58.1 %mlp.1 = (bf16[2308,1024]{1,0:T(8,128)(2,1)}, bf16[2320,4096]{1,0:T(8,128)(2,1)}, bf16[2320,4096]{1,0:T(8,128)(2,1)}, bf16[2320,1024]{1,0:T(8,128)(2,1)S(1)}) custom-call(s32[1]{0:T(128)S(6)} %mul.7.live_ref, bf16[2320,1024]{1,0:T(8,128)(2,1)} %copy-done.6, f32[2320,1024]{1,0:T(8,128)} %get-tuple-element.84.resid_ref, f32[1,4096]{1,0:T(1,128)S(1)} %reshape.123.ebias_ref, ...), custom_call_target="tpu_custom_call" | custom-call | flops 38923141120 | bytes 83288064 | tf_op jit(solution)/shard_map/mlp/pallas_call | solution.py:52
  253.4 27.8 %reduce_grad.1 = bf16[2,16,64,2048]{3,2,1,0:T(8,128)(2,1)S(1)} custom-call(bf16[2320,1024]{1,0:T(8,128)(2,1)S(1)} %get-tuple-element.91.refs_0_.grad_ref, bf16[1,2320,4096]{2,1,0:T(8,128)(2,1)} %bitcast.77), custom_call_target="tpu_custom_call" | custom-call | flops 19461570560 | bytes 32145408 | tf_op jit(solution)/shard_map/reduce_grad/pallas_call | solution.py:52
  281.3 3.3 copy-done.2
  284.6 65.3 %mlp_back.1 = (bf16[2320,4096]{1,0:T(8,128)(2,1)}, bf16[2320,1024]{1,0:T(8,128)(2,1)S(1)}, bf16[2320,1024]{1,0:T(8,128)(2,1)S(1)}, f32[4,1024]{1,0:T(4,128)S(1)}, f32[32,128]{1,0:T(8,128)S(1)}) custom-call(bf16[2320,1024]{1,0:T(8,128)(2,1)} %copy-done.3, bf16[2320,4096]{1,0:T(8,128)(2,1)} %get-tuple-element.92.slope_ref, ...), custom_call_target="tpu_custom_call" | custom-call | tf_op jit(solution)/shard_map/mlp_back/pallas_call | solution.py:52
  349.8 2.2 copy-done.5
  352.0 41.1 %middle_grad.1 = (bf16[4,64,2560]{2,1,0:T(8,128)(2,1)}, bf16[4,64,2560]{2,1,0:T(8,128)(2,1)}, bf16[4,64,2560]{2,1,0:T(8,128)(2,1)}, bf16[4,64,2560]{2,1,0:T(8,128)(2,1)}) custom-call(bf16[2320,1024]{1,0:T(8,128)(2,1)} %copy-done.6, bf16[2320,1024]{1,0:T(8,128)(2,1)} %copy-done.5, bf16[1,2320,4096]{2,1,0:T(8,128)(2,1)} %bitcast.64, ...), custom_call_target="tpu_custom_call" | custom-call | tf_op jit(solution)/shard_map/middle_grad/pallas_call | solution.py:52
  393.7 1.7 collective-permute-start.1
  396.7 92.6 %attend_back.1.refs_1_.grad_ref = bf16[3,2320,1024]{2,1,0:T(8,128)(2,1)} custom-call(bf16[3,2320,1024]{2,1,0:T(8,128)(2,1)} %get-tuple-element.81.triple_ref, f32[16,4,592]{2,1,0:T(4,128)S(1)} %get-tuple-element.104.stat_ref, bf16[2320,1024]{1,0:T(8,128)(2,1)S(1)} %get-tuple-element.105.grad_ref), custom_call_target="tpu_custom_call" | custom-call | tf_op jit(solution)/shard_map/attend_back/pallas_call | solution.py:52
  490.1 3.8 collective-permute-start.4
  494.4 25.3 %heads_grad.1 = (bf16[4,64,1536]{2,1,0:T(8,128)(2,1)}, bf16[4,64,1536]{2,1,0:T(8,128)(2,1)}, bf16[4,64,1536]{2,1,0:T(8,128)(2,1)}, bf16[4,64,1536]{2,1,0:T(8,128)(2,1)}) custom-call(bf16[2320,1024]{1,0:T(8,128)(2,1)} %copy-done.4, bf16[3,2320,1024]{2,1,0:T(8,128)(2,1)} %attend_back.1.refs_1_.grad_ref), custom_call_target="tpu_custom_call" | custom-call | tf_op jit(solution)/shard_map/heads_grad/pallas_call | solution.py:52
  523.3 2.3 copy-done.8
  525.7 27.9 %qkv_back.1 = (bf16[2308,1024]{1,0:T(8,128)(2,1)}, f32[2,1024]{1,0:T(2,128)S(1)}, f32[2,1024]{1,0:T(2,128)S(1)}) custom-call(bf16[2308,1024]{1,0:T(8,128)(2,1)S(1)} %copy-done.8, bf16[2320,1024]{1,0:T(8,128)(2,1)S(1)} %bitcast.51, f32[6,1024]{1,0:T(8,128)S(1)} %reshape.120.vec_ref, bf16[3,2320,1024]{2,1,0:T(8,128)(2,1)} %attend_back.1.refs_1_.grad_ref, ...), custom_call_target="tpu_custom_call" | custom-call | flops 14596177920 | bytes 37937152 | tf_op jit(solution)/shard_map/qkv_back/pallas_call | solution.py:52
  557.4 22.8 %tail.1 = (f32[3,64,512]{2,1,0:T(8,128)S(1)}, f32[8,128]{1,0:T(8,128)S(1)}) custom-call(bf16[4,64,1536]{2,1,0:T(8,128)(2,1)S(1)} %copy-done.9, bf16[4,64,1536]{2,1,0:T(8,128)(2,1)S(1)} %collective-permute-done.6.refs_1_, bf16[4,64,1536]{2,1,0:T(8,128)(2,1)S(1)} %collective-permute-done.7.refs_2_, bf16[4,64,1536]{2,1,0:T(8,128)(2,1)S(1)} %collective-permute-done.8.refs_3_, ...), custom_call_target="tpu_custom_call" | custom-call | tf_op jit(solution)/shard_map/tail/pallas_call | solution.py:52
  581.1 1.8 convert_bitcast_fusion
  (87 shorter events, 22.6 us)
Async XLA Ops:
  7.2 185.8 %all-gather.2.cloned.1.call-start = ((), (), s32[]{:S(2)}) async-start(), calls=%async_computation.1 | async-start | bytes 17301504 | tf_op jit(solution)/shard_map/all_gather | solution.py:766
  17.1 564.0 %reduce-scatter.2.cloned.1.call-start = ((), (), s32[]{:S(2)}) async-start(), calls=%async_computation.2 | async-start | bytes 8650752 | tf_op jit(solution)/shard_map/reduce_scatter | solution.py:856
  89.9 3.6 copy-start
  94.8 2.3 copy-start.7
  97.1 78.2 %slice-start.2 = ((s8[4734976]{0:T(1024)(128)(4,1)}), s8[540672]{0:T(1024)(128)(4,1)S(1)}, s32[]{:S(2)}) async-start(s8[4734976]{0:T(1024)(128)(4,1)} %bitcast.52), calls=%async_computation.5 | async-start | bytes 1081344
  122.6 52.7 %slice-start.3 = ((s8[4734976]{0:T(1024)(128)(4,1)}), s8[4194304]{0:T(1024)(128)(4,1)S(1)}, s32[]{:S(2)}) async-start(s8[4734976]{0:T(1024)(128)(4,1)} %bitcast.52), calls=%async_computation.6 | async-start | bytes 8388608
  193.0 2.3 copy-start.22
  253.4 27.8 %copy-start.3 = (bf16[2320,1024]{1,0:T(8,128)(2,1)}, bf16[2320,1024]{1,0:T(8,128)(2,1)S(1)}, u32[]{:S(2)}) copy-start(bf16[2320,1024]{1,0:T(8,128)(2,1)S(1)} %get-tuple-element.91.refs_0_.grad_ref) | copy-start | bytes 14254084
  281.2 3.3 copy-start.2
  349.8 2.2 copy-start.5
  393.1 96.2 %collective-permute-start = (bf16[4,64,2560]{2,1,0:T(8,128)(2,1)}, bf16[4,64,2560]{2,1,0:T(8,128)(2,1)S(1)}, u32[]{:S(2)}, u32[]{:S(2)}) collective-permute-start(bf16[4,64,2560]{2,1,0:T(8,128)(2,1)} %get-tuple-element.100), channel_id=1, source_target_pairs={{0,4},{1,5},{2,6},{3,7},{4,0},{5,1},{6,2},{7,3},{8,12},{9,13},{10,... | collective-permute-start | bytes 3932168 | tf_op jit(solution)/shard_map/ppermute | solution.py:425
  393.7 95.6 %collective-permute-start.1 = (bf16[4,64,2560]{2,1,0:T(8,128)(2,1)}, bf16[4,64,2560]{2,1,0:T(8,128)(2,1)S(1)}, u32[]{:S(2)}, u32[]{:S(2)}) collective-permute-start(bf16[4,64,2560]{2,1,0:T(8,128)(2,1)} %get-tuple-element.101), channel_id=1, source_target_pairs={{0,1},{1,0},{2,3},{3,2},{4,5},{5,4},{6,7},{7,6},{8,9},{9,8},{10,11... | collective-permute-start | bytes 3932168 | tf_op jit(solution)/shard_map/ppermute | solution.py:425
  395.4 93.9 %collective-permute-start.2 = (bf16[4,64,2560]{2,1,0:T(8,128)(2,1)}, bf16[4,64,2560]{2,1,0:T(8,128)(2,1)S(1)}, u32[]{:S(2)}, u32[]{:S(2)}) collective-permute-start(bf16[4,64,2560]{2,1,0:T(8,128)(2,1)} %get-tuple-element.102), channel_id=1, source_target_pairs={{0,5},{1,4},{2,7},{3,6},{4,1},{5,0},{6,3},{7,2},{8,13},{9,12},{10,... | collective-permute-start | bytes 3932168 | tf_op jit(solution)/shard_map/ppermute | solution.py:425
  396.7 92.6 %copy-start.23 = (bf16[4,64,2560]{2,1,0:T(8,128)(2,1)S(1)}, bf16[4,64,2560]{2,1,0:T(8,128)(2,1)}, u32[]{:S(2)}) copy-start(bf16[4,64,2560]{2,1,0:T(8,128)(2,1)} %get-tuple-element.106) | copy-start | bytes 3932164
  489.3 34.0 %slice-start = ((s8[4751360]{0:T(1024)(128)(4,1)}), s8[4194304]{0:T(1024)(128)(4,1)S(1)}, s32[]{:S(2)}) async-start(s8[4751360]{0:T(1024)(128)(4,1)} %bitcast.50), calls=%async_computation.3 | async-start | bytes 8388608
  490.0 29.8 %collective-permute-start.3 = (bf16[64,2560]{1,0:T(8,128)(2,1)S(1)}, bf16[64,2560]{1,0:T(8,128)(2,1)S(1)}, u32[]{:S(2)}, u32[]{:S(2)}) collective-permute-start(bf16[64,2560]{1,0:T(8,128)(2,1)S(1)} %get-tuple-element.116), channel_id=1, source_target_pairs={{0,8},{1,9},{2,10},{3,11},{4,12},{5,13},{6,14},{7,15},{8,0},{9,1},... | collective-permute-start | bytes 983048 | tf_op jit(solution)/shard_map/ppermute | solution.py:425
  490.1 29.7 %collective-permute-start.4 = (bf16[64,2560]{1,0:T(8,128)(2,1)S(1)}, bf16[64,2560]{1,0:T(8,128)(2,1)S(1)}, u32[]{:S(2)}, u32[]{:S(2)}) collective-permute-start(bf16[64,2560]{1,0:T(8,128)(2,1)S(1)} %get-tuple-element.117), channel_id=1, source_target_pairs={{0,16},{1,17},{2,18},{3,19},{4,20},{5,21},{6,22},{7,23},{8,24},{9,... | collective-permute-start | bytes 983048 | tf_op jit(solution)/shard_map/ppermute | solution.py:425
  493.9 25.9 %collective-permute-start.5 = (bf16[64,2560]{1,0:T(8,128)(2,1)S(1)}, bf16[64,2560]{1,0:T(8,128)(2,1)S(1)}, u32[]{:S(2)}, u32[]{:S(2)}) collective-permute-start(bf16[64,2560]{1,0:T(8,128)(2,1)S(1)} %get-tuple-element.118), channel_id=1, source_target_pairs={{0,24},{1,25},{2,26},{3,27},{4,28},{5,29},{6,30},{7,31},{8,16},{9,... | collective-permute-start | bytes 983048 | tf_op jit(solution)/shard_map/ppermute | solution.py:425
  494.4 28.9 %slice-start.1 = ((s8[4751360]{0:T(1024)(128)(4,1)}), s8[557056]{0:T(1024)(128)(4,1)S(1)}, s32[]{:S(2)}) async-start(s8[4751360]{0:T(1024)(128)(4,1)} %bitcast.50), calls=%async_computation.4 | async-start | bytes 1114112
  519.8 35.4 %collective-permute-start.6 = (bf16[4,64,1536]{2,1,0:T(8,128)(2,1)}, bf16[4,64,1536]{2,1,0:T(8,128)(2,1)S(1)}, u32[]{:S(2)}, u32[]{:S(2)}) collective-permute-start(bf16[4,64,1536]{2,1,0:T(8,128)(2,1)} %get-tuple-element.123), channel_id=1, source_target_pairs={{0,4},{1,5},{2,6},{3,7},{4,0},{5,1},{6,2},{7,3},{8,12},{9,13},{10,... | collective-permute-start | bytes 2359304 | tf_op jit(solution)/shard_map/ppermute | solution.py:425
  520.3 35.7 %collective-permute-start.7 = (bf16[4,64,1536]{2,1,0:T(8,128)(2,1)}, bf16[4,64,1536]{2,1,0:T(8,128)(2,1)S(1)}, u32[]{:S(2)}, u32[]{:S(2)}) collective-permute-start(bf16[4,64,1536]{2,1,0:T(8,128)(2,1)} %get-tuple-element.124), channel_id=1, source_target_pairs={{0,1},{1,0},{2,3},{3,2},{4,5},{5,4},{6,7},{7,6},{8,9},{9,8},{10,11... | collective-permute-start | bytes 2359304 | tf_op jit(solution)/shard_map/ppermute | solution.py:425
  522.0 35.4 %collective-permute-start.8 = (bf16[4,64,1536]{2,1,0:T(8,128)(2,1)}, bf16[4,64,1536]{2,1,0:T(8,128)(2,1)S(1)}, u32[]{:S(2)}, u32[]{:S(2)}) collective-permute-start(bf16[4,64,1536]{2,1,0:T(8,128)(2,1)} %get-tuple-element.125), channel_id=1, source_target_pairs={{0,5},{1,4},{2,7},{3,6},{4,1},{5,0},{6,3},{7,2},{8,13},{9,12},{10,... | collective-permute-start | bytes 2359304 | tf_op jit(solution)/shard_map/ppermute | solution.py:425
  523.3 2.3 copy-start.8
  525.7 31.8 %copy-start.9 = (bf16[4,64,1536]{2,1,0:T(8,128)(2,1)S(1)}, bf16[4,64,1536]{2,1,0:T(8,128)(2,1)}, u32[]{:S(2)}) copy-start(bf16[4,64,1536]{2,1,0:T(8,128)(2,1)} %get-tuple-element.122.refs_0_) | copy-start | bytes 2359300
  (15 other events, 15.3 us)
Sparse Core Ops, SparseCore 0:
  17.2 137.3 all-gather.1
  284.7 151.6 reduce-scatter.1

commit v4 on v3

--- a/solution.py
+++ b/solution.py
@@ -12,6 +12,7 @@
 SEQ = 577
 STRIDE = 576
 WINDOW = 592
+LANES = 640
 EPSILON = 1e-06
 LOG_SCALE = 0.125
 bf16 = jnp.bfloat16
@@ -19,7 +20,6 @@
 NN = (((1,), (0,)), ((), ()))
 NT = (((1,), (1,)), ((), ()))
 TN = (((0,), (0,)), ((), ()))
-MIB = 2**20
 AXES = ("tensor", "dp")
 
 
@@ -44,7 +44,7 @@
     return pl.BlockSpec(shape, lambda *_: (0,) * len(shape), pipeline_mode=pl.Buffered(1))
 
 
-def call(kernel, name, grid, in_specs, out_specs, out_shape, args, scratch=(), flops=0, prefetch=0, vmem=40, **params):
+def call(kernel, name, grid, in_specs, out_specs, out_shape, args, scratch=(), flops=0, prefetch=0, **params):
     moved = 0
     if flops:
         moved = sum(a.size * a.dtype.itemsize for a in args)
@@ -59,7 +59,7 @@
             scratch_shapes=list(scratch),
         ),
         out_shape=[jax.ShapeDtypeStruct(shape, dtype) for shape, dtype in out_shape],
-        compiler_params=pltpu.CompilerParams(vmem_limit_bytes=vmem * MIB, **params),
+        compiler_params=pltpu.CompilerParams(vmem_limit_bytes=60 * 2**20, **params),
         cost_estimate=pl.CostEstimate(flops=2 * flops, bytes_accessed=moved, transcendentals=0),
         name=name,
     )(*args)
@@ -101,22 +101,47 @@
     ref[(*index[:-1], rest, index[-1])] = value[16:].astype(ref.dtype)
 
 
+def two_heads(first, second):
+    blank, below = jnp.zeros_like(first), jnp.zeros((LANES - WINDOW, 2 * HEAD_DIM), first.dtype)
+    return jnp.concatenate(
+        [
+            jnp.concatenate([first, blank], axis=1), below,
+            jnp.concatenate([blank, second], axis=1), below,
+        ],
+        axis=0,
+    )
+
+
+def head_columns(h):
+    return (
+        slice(HEAD_DIM * h, HEAD_DIM * (h + 2)),
+        (slice(HEAD_DIM * h, HEAD_DIM * (h + 1)), slice(HEAD_DIM * (h + 1), HEAD_DIM * (h + 2))),
+    )
+
+
 def attend_kernel(triple_ref, context_ref, stat_ref):
     image = pl.program_id(1)
-    lanes = lax.broadcasted_iota(jnp.int32, (1, WINDOW), 1)
+    lanes = lax.broadcasted_iota(jnp.int32, (1, LANES), 1)
     mask = jnp.where((lanes >= image) & (lanes < image + SEQ), 0.0, -1e30)
     own = window(image)
+    left = lax.broadcasted_iota(jnp.int32, (1, 2 * HEAD_DIM), 1) < HEAD_DIM
     stats = []
-    for h in range(triple_ref.shape[2] // HEAD_DIM):
-        cols = slice(HEAD_DIM * h, HEAD_DIM * (h + 1))
-        query = triple_ref[0, own, cols] * bf16(LOG_SCALE)
-        scores = matmul(query, triple_ref[1, own, cols], NT) + mask
-        top = jnp.max(scores, axis=1, keepdims=True)
-        expo = jnp.exp(scores - top)
-        total = jnp.sum(expo, axis=1, keepdims=True)
-        context = matmul(expo.astype(bf16), triple_ref[2, own, cols]) * (1.0 / total)
-        keep_before(image, context_ref, (cols,), context)
-        stats.append(top + jnp.log(total))
+    for h in range(0, triple_ref.shape[2] // HEAD_DIM, 2):
+        pair, single = head_columns(h)
+        keys = two_heads(*(triple_ref[1, own, cols] for cols in single))
+        both = matmul(triple_ref[0, own, pair] * bf16(LOG_SCALE), keys, NT)
+        probs, scale = [], []
+        for u in range(2):
+            scores = both[:, u * LANES : (u + 1) * LANES] + mask
+            top = jnp.max(scores, axis=1, keepdims=True)
+            expo = jnp.exp(scores - top)
+            total = jnp.sum(expo, axis=1, keepdims=True)
+            probs.append(expo.astype(bf16))
+            scale.append(1.0 / total)
+            stats.append(top + jnp.log(total))
+        values = two_heads(*(triple_ref[2, own, cols] for cols in single))
+        context = matmul(jnp.concatenate(probs, axis=1), values)
+        keep_before(image, context_ref, (pair,), context * jnp.where(left, *scale))
     stat_ref[0] = jnp.concatenate(stats, axis=1).T
 
 
@@ -124,36 +149,45 @@
     image = pl.program_id(1)
     rows = lax.broadcasted_iota(jnp.int32, (WINDOW, 1), 0)
     mask = jnp.where((rows >= image) & (rows < image + SEQ), 0.0, -1e30)
-    lanes = lax.broadcasted_iota(jnp.int32, (1, WINDOW), 1)
+    lanes = lax.broadcasted_iota(jnp.int32, (1, LANES), 1)
     real = (lanes >= image) & (lanes < image + SEQ)
     own = window(image)
-    for h in range(triple_ref.shape[2] // HEAD_DIM):
-        cols = slice(HEAD_DIM * h, HEAD_DIM * (h + 1))
-        query = triple_ref[0, own, cols]
-        keys = triple_ref[1, own, cols]
-        grad = grad_ref[own, cols]
-        scores = matmul(keys, query * bf16(LOG_SCALE), NT) + mask
-        probs = jnp.exp(scores - jnp.where(real, stat_ref[0, h : h + 1, :], 1e30))
-        grad_probs = matmul(triple_ref[2, own, cols], grad, NT)
-        inner = jnp.sum(probs * grad_probs, axis=0, keepdims=True)
-        grad_scores = (probs * (grad_probs - inner)).astype(bf16)
-        blank = jnp.zeros_like(grad)
-        left = jnp.concatenate([probs.astype(bf16), grad_scores], axis=1)
-        right = jnp.concatenate(
-            [jnp.concatenate([grad, blank], axis=1), jnp.concatenate([blank, query], axis=1)], axis=0
-        )
-        pair = matmul(left, right)
-        keep_before(image, out_ref, (2, cols), pair[:, :HEAD_DIM])
-        keep_before(image, out_ref, (1, cols), pair[:, HEAD_DIM:] * LOG_SCALE)
-        keep_before(image, out_ref, (0, cols), (matmul(keys.T, grad_scores) * LOG_SCALE).T)
+    for h in range(0, triple_ref.shape[2] // HEAD_DIM, 2):
+        pair, single = head_columns(h)
+        keys = triple_ref[1, own, pair]
+        queries = [triple_ref[0, own, cols] for cols in single]
+        grads = [grad_ref[own, cols] for cols in single]
+        both = matmul(keys, two_heads(*queries) * bf16(LOG_SCALE), NT)
+        both_grad = matmul(triple_ref[2, own, pair], two_heads(*grads), NT)
+        turned = keys.T
+        value_grad, key_grad, query_grad = [], [], []
+        for u in range(2):
+            side = slice(u * LANES, (u + 1) * LANES)
+            stat = jnp.concatenate(
+                [stat_ref[0, h + u : h + u + 1, :], jnp.zeros((1, LANES - WINDOW), f32)], axis=1
+            )
+            probs = jnp.exp(both[:, side] + mask - jnp.where(real, stat, 1e30))
+            grad_probs = both_grad[:, side]
+            inner = jnp.sum(probs * grad_probs, axis=0, keepdims=True)
+            grad_scores = (probs * (grad_probs - inner)).astype(bf16)
+            out = matmul(
+                jnp.concatenate([probs.astype(bf16), grad_scores], axis=1),
+                two_heads(grads[u], queries[u]),
+            )
+            value_grad.append(out[:, :HEAD_DIM])
+            key_grad.append(out[:, HEAD_DIM:])
+            query_grad.append(matmul(turned[u * HEAD_DIM : (u + 1) * HEAD_DIM], grad_scores))
+        keep_before(image, out_ref, (2, pair), jnp.concatenate(value_grad, axis=1))
+        keep_before(image, out_ref, (1, pair), jnp.concatenate(key_grad, axis=1) * LOG_SCALE)
+        query_grad = jnp.concatenate(query_grad, axis=0).T[:WINDOW]
+        keep_before(image, out_ref, (0, pair), query_grad * LOG_SCALE)
 
 
 def merge_kernel(part, count, ctx_ref, x_ref, vec_ref, w_ref, resid_ref, normed_ref):
-    tensor, dp = w_ref.shape[:2]
-    width = w_ref.shape[3] // 4
+    tensor, dp, _, width = w_ref.shape
     total = before(x_ref, count) + vec_ref[2:3]
     for t in range(tensor):
-        w = w_ref[t, :, :part, 3 * width :].reshape(dp * part, width)
+        w = w_ref[t, :, :part].reshape(dp * part, width)
         total = total + matmul(ctx_ref[:, t * width : (t + 1) * width], w, NT)
     resid_ref[...] = total
     hat, _ = norm_parts(total)
@@ -161,25 +195,23 @@
 
 
 def mlp_kernel(
-    chunk, live_ref, normed_ref, resid_ref, ebias_ref, vec_ref, w_ref, given_ref,
+    chunk, live_ref, normed_ref, resid_ref, ebias_ref, vec_ref, e_ref, r_ref, given_ref,
     out_ref, act_ref, slope_ref, grad_ref,
 ):
     grad_ref[...] = before(given_ref, live_ref[0]).astype(bf16)
-    tensor, dp, rows, width = w_ref.shape
-    width = width // 2
+    tensor, dp, rows, width = e_ref.shape
     normed = normed_ref[...]
     total = resid_ref[...] + vec_ref[5:6]
     for t in range(tensor):
         for c in range(width // chunk):
             local = slice(c * chunk, (c + 1) * chunk)
-            other = slice(width + c * chunk, width + (c + 1) * chunk)
             cols = slice(t * width + c * chunk, t * width + (c + 1) * chunk)
-            e = w_ref[t, :, :, local].reshape(dp * rows, chunk)
+            e = e_ref[t, :, :, local].reshape(dp * rows, chunk)
             active, slope = gelu_and_slope(matmul(normed, e) + ebias_ref[:, cols])
             active = active.astype(bf16)
             act_ref[:, cols] = active
             slope_ref[:, cols] = slope.astype(bf16)
-            r = w_ref[t, :, :, other].reshape(dp * rows, chunk)
+            r = r_ref[t, :, :, local].reshape(dp * rows, chunk)
             total = total + matmul(active, r, NT)
     out_ref[...] = total.astype(bf16)
 
@@ -206,11 +238,10 @@
 
 
 def mlp_back_kernel(
-    part, chunk, grad_ref, slope_ref, resid_ref, vec_ref, w_ref, m_ref,
+    part, chunk, grad_ref, slope_ref, resid_ref, vec_ref, e_ref, r_ref, m_ref,
     pre_ref, low_ref, ctx_ref, sums_ref, esum_ref,
 ):
-    tensor, dp, rows, width = w_ref.shape
-    width = width // 2
+    tensor, dp, rows, width = e_ref.shape
     first = pl.program_id(0) == 0
     grad = grad_ref[...]
     total = jnp.zeros(grad.shape, f32)
@@ -218,13 +249,12 @@
     for t in range(tensor):
         for c in range(width // chunk):
             local = slice(c * chunk, (c + 1) * chunk)
-            other = slice(width + c * chunk, width + (c + 1) * chunk)
             cols = slice(t * width + c * chunk, t * width + (c + 1) * chunk)
-            r = w_ref[t, :, :, other].reshape(dp * rows, chunk)
+            r = r_ref[t, :, :, local].reshape(dp * rows, chunk)
             pre = (matmul(grad, r) * slope_ref[:, cols].astype(f32)).astype(bf16)
             pre_ref[:, cols] = pre
             parts.append(jnp.sum(pre.astype(f32), axis=0, keepdims=True))
-            e = w_ref[t, :, :, local].reshape(dp * rows, chunk)
+            e = e_ref[t, :, :, local].reshape(dp * rows, chunk)
             total = total + matmul(pre, e, NT)
     sums = 0
     half = grad.shape[0] // 2
@@ -411,7 +441,6 @@
         [pltpu.VMEM((deep, block), f32)]
         + [pltpu.VMEM((half, part, wide), bf16)] * 3
         + [pltpu.SemaphoreType.DMA((starts[-1] * tensor,))] * 2,
-        vmem=56,
         collective_id=collective_id,
         has_side_effects=True,
     )
@@ -790,13 +819,19 @@
     def by_rows(width):
         return pl.BlockSpec((block, width), lambda i, *_: (i, 0))
 
+    def columns(array, index, width):
+        shape = array.shape[:3] + (width,)
+        return pl.BlockSpec(shape, lambda *_: (0, 0, 0, index), pipeline_mode=pl.Buffered(1))
+
     vec = full((6, deep))
+    expand_spec, reduce_spec = columns(wide, 0, hidden_own), columns(wide, 1, hidden_own)
+    merge_spec = columns(wide_heads, 3, own)
     triple_spec = pl.BlockSpec((3, block, deep), lambda i: (0, i, 0))
     normed_one, triple = call(
         functools.partial(qkv_kernel, part, rows),
         "qkv",
         (blocks,),
-        [by_rows(deep), vec, full((2, deep)), vmem],
+        [by_rows(deep), vec, full((2, deep)), full(wide_heads.shape)],
         [by_rows(deep), triple_spec],
         [((total_rows, deep), bf16), ((3, total_rows, deep), bf16)],
         (activations, vectors, hb, wide_heads),
@@ -825,7 +860,7 @@
         functools.partial(merge_kernel, part, rows),
         "merge",
         (blocks,),
-        [by_rows(deep), by_rows(deep), vec, vmem],
+        [by_rows(deep), by_rows(deep), vec, merge_spec],
         [by_rows(deep), by_rows(deep)],
         [((total_rows, deep), f32), ((total_rows, deep), bf16)],
         (context, activations, vectors, wide_heads),
@@ -838,17 +873,16 @@
         "mlp",
         (blocks,),
         [
-            by_rows(deep), by_rows(deep), full((1, hidden)), vec, vmem, by_rows(deep),
+            by_rows(deep), by_rows(deep), full((1, hidden)), vec, expand_spec, reduce_spec, by_rows(deep),
         ],
         [by_rows(deep), by_rows(hidden), by_rows(hidden), by_rows(deep)],
         [
             ((rows, deep), bf16), ((total_rows, hidden), bf16), ((total_rows, hidden), bf16),
             ((total_rows, deep), bf16),
         ],
-        (live, normed_two, resid, eb, vectors, wide, output_grad),
+        (live, normed_two, resid, eb, vectors, wide, wide, output_grad),
         prefetch=1,
         flops=total_rows * deep * hidden * 2,
-        vmem=44,
     )
 
     def scatter(grads):
@@ -866,10 +900,7 @@
         (blocks,),
         [
             by_rows(deep), by_rows(hidden), by_rows(deep), vec,
-            vmem,
-            pl.BlockSpec(
-                (tensor, dp, part + 8, own), lambda i: (0, 0, 0, 3), pipeline_mode=pl.Buffered(1)
-            ),
+            expand_spec, reduce_spec, merge_spec,
         ],
         [
             by_rows(hidden), by_rows(deep), by_rows(deep),
@@ -879,8 +910,7 @@
             ((total_rows, hidden), bf16), ((total_rows, deep), bf16), ((total_rows, deep), bf16),
             ((4, deep), f32), ((hidden // 128, 128), f32),
         ],
-        (grad, slope, resid, vectors, wide, wide_heads),
-        vmem=44,
+        (grad, slope, resid, vectors, wide, wide, wide_heads),
     )
     parts = slot_grads(
         "middle_grad", [(normed_two, pre_grad[None]), (resid_low, context[None])], tensor, dp, 512, 2
@@ -909,7 +939,7 @@
         functools.partial(qkv_back_kernel, part, rows),
         "qkv_back",
         (blocks,),
-        [by_rows(deep), by_rows(deep), vec, triple_spec, vmem],
+        [by_rows(deep), by_rows(deep), vec, triple_spec, full(wide_heads.shape)],
         [by_rows(deep), pl.BlockSpec((2, deep), lambda i: (0, 0)), pl.BlockSpec((2, deep), lambda i: (0, 0))],
         [((rows, deep), bf16), ((2, deep), f32), ((2, deep), f32)],
         (activations, resid_low, vectors, grad_triple, wide_heads),

time: 599 us -> 559 us (0.933)
  local copies, waits for them, and re-layouts: 34.1 us -> 6.36 us
  Pallas kernels: 524 us -> 506 us
    unnamed x56 -> x20, local copies, waits for them, and re-layouts: 31.4 us -> 1.82 us
    pallas_call x14, Pallas kernels: 524 us -> 506 us  [call(): pl.pallas_call(kernel, grid_spec=pltpu.PrefetchScalarGridSpec(num_scalar_...]
  transfers between devices with their start and end apart: 11 -> 11, of which waited for: 2 -> 2; matrix products, arithmetic and copies ran while one was open for 1% -> 1% of each run, Pallas kernels for 74% -> 76%
where the time goes in v4:
time: 559 us; the launch traced here: 551 us
  Pallas kernels  506 us (91%)
  between operations  15.4 us (3%)
  starting transfers between devices  11.6 us (2%)
  waiting for transfers between devices  7.05 us (1%)
  local copies, waits for them, and re-layouts  6.36 us (1%)
    pallas_call x14, Pallas kernels, call(): pl.pallas_call(kernel, grid_spec=pltpu.PrefetchScalarGridSpec(num_scalar_...  506 us
    ppermute x9, starting transfers between devices, swap(): return lax.ppermute(values, ('dp', 'tensor'), moves)  11.5 us
  transfers between devices with their start and end apart: 11, of which 2 were waited for; matrix products, arithmetic and copies ran while one was open for 1% of the time, Pallas kernels for 76%

profile of v4, /device:TPU:0, one launch (start us, length us, event | category | flops | bytes accessed | tf_op | source)
XLA Modules:
  0.0 551.0 jit_solution(2119686633175827818)
XLA Ops:
  7.2 2.2 pack.1
  10.1 74.0 %gather.1.w_ref.m_ref = bf16[2,16,72,2048]{3,2,1,0:T(8,128)(2,1)} custom-call(bf16[72,2048]{1,0:T(8,128)(2,1)} %get-tuple-element.80.in_ref), custom_call_target="tpu_custom_call" | custom-call | tf_op jit(solution)/shard_map/gather/pallas_call | solution.py:52
  88.0 23.7 %qkv.1 = (bf16[2320,1024]{1,0:T(8,128)(2,1)}, bf16[3,2320,1024]{2,1,0:T(8,128)(2,1)}) custom-call(bf16[2308,1024]{1,0:T(8,128)(2,1)} %x_ref.5, f32[6,1024]{1,0:T(8,128)} %reshape.120.vec_ref, f32[2,1024]{1,0:T(2,128)} %reshape.122.bias_ref, bf16[2,16,72,2048]{3,2,1,0:T(8,128)(2,1)} %gather.1.w_ref.m_ref), custom_call_target="tpu_custom_call" | custom-call | flops 14596177920 | bytes 33202176 | tf_op jit(solution)/shard_map/qkv/pallas_call | solution.py:52
  111.7 43.9 %attend.1 = (bf16[2320,1024]{1,0:T(8,128)(2,1)}, f32[16,4,592]{2,1,0:T(4,128)}) custom-call(bf16[3,2320,1024]{2,1,0:T(8,128)(2,1)} %get-tuple-element.81.triple_ref), custom_call_target="tpu_custom_call" | custom-call | flops 29796335616 | bytes 19156992 | tf_op jit(solution)/shard_map/attend/pallas_call | solution.py:52
  155.6 12.6 %merge.1 = (f32[2320,1024]{1,0:T(8,128)}, bf16[2320,1024]{1,0:T(8,128)(2,1)}) custom-call(bf16[2320,1024]{1,0:T(8,128)(2,1)} %get-tuple-element.82.ctx_ref, bf16[2308,1024]{1,0:T(8,128)(2,1)} %x_ref.5, f32[6,1024]{1,0:T(8,128)} %reshape.120.vec_ref, bf16[2,16,72,2048]{3,2,1,0:T(8,128)(2,1)} %gather.1.w_ref.m_ref), custom_call_target="tpu_custom_call" | custom-call | flops 4865392640 | bytes 33193984 | tf_op jit(solution)/shard_map/merge/pallas_call | solution.py:52
  168.2 58.4 %mlp.1 = (bf16[2308,1024]{1,0:T(8,128)(2,1)}, bf16[2320,4096]{1,0:T(8,128)(2,1)}, bf16[2320,4096]{1,0:T(8,128)(2,1)}, bf16[2320,1024]{1,0:T(8,128)(2,1)}) custom-call(s32[1]{0:T(128)S(6)} %mul.7.live_ref, bf16[2320,1024]{1,0:T(8,128)(2,1)} %get-tuple-element.83.normed_ref.refs_0_, f32[2320,1024]{1,0:T(8,128)} %get-tuple-element.84.resid_ref, ...), custom_call_target="tpu_custom_call" | custom-call | flops 38923141120 | bytes 100065280 | tf_op jit(solution)/shard_map/mlp/pallas_call | solution.py:52
  226.6 27.7 %reduce_grad.1 = bf16[2,16,64,2048]{3,2,1,0:T(8,128)(2,1)} custom-call(bf16[2320,1024]{1,0:T(8,128)(2,1)} %get-tuple-element.91.refs_0_.grad_ref, bf16[1,2320,4096]{2,1,0:T(8,128)(2,1)} %bitcast.75), custom_call_target="tpu_custom_call" | custom-call | flops 19461570560 | bytes 32145408 | tf_op jit(solution)/shard_map/reduce_grad/pallas_call | solution.py:52
  254.4 65.9 %mlp_back.1 = (bf16[2320,4096]{1,0:T(8,128)(2,1)}, bf16[2320,1024]{1,0:T(8,128)(2,1)}, bf16[2320,1024]{1,0:T(8,128)(2,1)}, f32[4,1024]{1,0:T(4,128)}, f32[32,128]{1,0:T(8,128)}) custom-call(bf16[2320,1024]{1,0:T(8,128)(2,1)} %get-tuple-element.91.refs_0_.grad_ref, bf16[2320,4096]{1,0:T(8,128)(2,1)} %get-tuple-element.92.slope_ref, ...), custom_call_target="tpu_custom_call" | custom-call | tf_op jit(solution)/shard_map/mlp_back/pallas_call | solution.py:52
  320.3 41.3 %middle_grad.1 = (bf16[4,64,2560]{2,1,0:T(8,128)(2,1)}, bf16[4,64,2560]{2,1,0:T(8,128)(2,1)}, bf16[4,64,2560]{2,1,0:T(8,128)(2,1)}, bf16[4,64,2560]{2,1,0:T(8,128)(2,1)}) custom-call(bf16[2320,1024]{1,0:T(8,128)(2,1)} %get-tuple-element.83.normed_ref.refs_0_, bf16[2320,1024]{1,0:T(8,128)(2,1)} %get-tuple-element.120.refs_1_.low_ref, ...), custom_call_target="tpu_custom_call" | custom-call | tf_op jit(solution)/shard_map/middle_grad/pallas_call | solution.py:52
  362.5 1.2 collective-permute-start.1
  363.7 1.5 collective-permute-start.2
  365.2 75.6 %attend_back.1.refs_1_.grad_ref = bf16[3,2320,1024]{2,1,0:T(8,128)(2,1)} custom-call(bf16[3,2320,1024]{2,1,0:T(8,128)(2,1)} %get-tuple-element.81.triple_ref, f32[16,4,592]{2,1,0:T(4,128)} %get-tuple-element.104.stat_ref, bf16[2320,1024]{1,0:T(8,128)(2,1)} %get-tuple-element.105.grad_ref), custom_call_target="tpu_custom_call" | custom-call | tf_op jit(solution)/shard_map/attend_back/pallas_call | solution.py:52
  440.8 3.6 collective-permute-done.2
  444.5 2.3 fusion.3
  447.3 3.9 collective-permute-start.5
  451.2 25.3 %heads_grad.1 = (bf16[4,64,1536]{2,1,0:T(8,128)(2,1)}, bf16[4,64,1536]{2,1,0:T(8,128)(2,1)}, bf16[4,64,1536]{2,1,0:T(8,128)(2,1)}, bf16[4,64,1536]{2,1,0:T(8,128)(2,1)}) custom-call(bf16[2320,1024]{1,0:T(8,128)(2,1)} %get-tuple-element.87.refs_0_, bf16[3,2320,1024]{2,1,0:T(8,128)(2,1)} %attend_back.1.refs_1_.grad_ref), custom_call_target="tpu_custom_call" | custom-call | tf_op jit(solution)/shard_map/heads_grad/pallas_call | solution.py:52
  477.5 1.0 collective-permute-start.7
  478.5 2.5 collective-permute-start.8
  481.0 28.5 %qkv_back.1 = (bf16[2308,1024]{1,0:T(8,128)(2,1)}, f32[2,1024]{1,0:T(2,128)}, f32[2,1024]{1,0:T(2,128)}) custom-call(bf16[2308,1024]{1,0:T(8,128)(2,1)} %x_ref.5, bf16[2320,1024]{1,0:T(8,128)(2,1)} %get-tuple-element.120.refs_1_.low_ref, f32[6,1024]{1,0:T(8,128)} %reshape.120.vec_ref, bf16[3,2320,1024]{2,1,0:T(8,128)(2,1)} %attend_back.1.refs_1_.grad_ref, ...), custom_call_target="tpu_custom_call" | custom-call | flops 14596177920 | bytes 37937152 | tf_op jit(solution)/shard_map/qkv_back/pallas_call | solution.py:52
  511.2 3.3 collective-permute-done.8.refs_3_
  514.5 0.9 copy-done.3
  515.4 24.7 %tail.1 = (f32[3,64,512]{2,1,0:T(8,128)}, f32[8,128]{1,0:T(8,128)}) custom-call(bf16[4,64,1536]{2,1,0:T(8,128)(2,1)} %get-tuple-element.122.refs_0_, bf16[4,64,1536]{2,1,0:T(8,128)(2,1)} %copy-done.1, bf16[4,64,1536]{2,1,0:T(8,128)(2,1)} %copy-done.2, bf16[4,64,1536]{2,1,0:T(8,128)(2,1)} %copy-done.3, f32[2,1024]{1,0:T(2,128)} %get-tuple-element.126.refs_4_, ...), custom_call_target="tpu_custom_call" | custom-call | tf_op jit(solution)/shard_map/tail/pallas_call | solution.py:52
  540.1 1.8 finish.1
  541.9 1.8 convert_bitcast_fusion
  (49 shorter events, 8.0 us)
Async XLA Ops:
  7.2 161.0 %all-gather.2.cloned.1.call-start = ((), (), s32[]{:S(2)}) async-start(), calls=%async_computation.1 | async-start | bytes 17301504 | tf_op jit(solution)/shard_map/all_gather | solution.py:795
  9.4 532.5 %reduce-scatter.2.cloned.1.call-start = ((), (), s32[]{:S(2)}) async-start(), calls=%async_computation.2 | async-start | bytes 8650752 | tf_op jit(solution)/shard_map/reduce_scatter | solution.py:890
  361.6 79.2 %collective-permute-start = (bf16[4,64,2560]{2,1,0:T(8,128)(2,1)}, bf16[4,64,2560]{2,1,0:T(8,128)(2,1)S(1)}, u32[]{:S(2)}, u32[]{:S(2)}) collective-permute-start(bf16[4,64,2560]{2,1,0:T(8,128)(2,1)} %get-tuple-element.100), channel_id=1, source_target_pairs={{0,4},{1,5},{2,6},{3,7},{4,0},{5,1},{6,2},{7,3},{8,12},{9,13},{10,... | collective-permute-start | bytes 3932168 | tf_op jit(solution)/shard_map/ppermute | solution.py:454
  362.5 78.3 %collective-permute-start.1 = (bf16[4,64,2560]{2,1,0:T(8,128)(2,1)}, bf16[4,64,2560]{2,1,0:T(8,128)(2,1)}, u32[]{:S(2)}, u32[]{:S(2)}) collective-permute-start(bf16[4,64,2560]{2,1,0:T(8,128)(2,1)} %get-tuple-element.101), channel_id=1, source_target_pairs={{0,1},{1,0},{2,3},{3,2},{4,5},{5,4},{6,7},{7,6},{8,9},{9,8},{10,11... | collective-permute-start | bytes 3932168 | tf_op jit(solution)/shard_map/ppermute | solution.py:454
  363.7 80.7 %collective-permute-start.2 = (bf16[4,64,2560]{2,1,0:T(8,128)(2,1)}, bf16[4,64,2560]{2,1,0:T(8,128)(2,1)}, u32[]{:S(2)}, u32[]{:S(2)}) collective-permute-start(bf16[4,64,2560]{2,1,0:T(8,128)(2,1)} %get-tuple-element.102), channel_id=1, source_target_pairs={{0,5},{1,4},{2,7},{3,6},{4,1},{5,0},{6,3},{7,2},{8,13},{9,12},{10,... | collective-permute-start | bytes 3932168 | tf_op jit(solution)/shard_map/ppermute | solution.py:454
  365.2 79.3 %copy-start = (bf16[4,64,2560]{2,1,0:T(8,128)(2,1)S(1)}, bf16[4,64,2560]{2,1,0:T(8,128)(2,1)}, u32[]{:S(2)}) copy-start(bf16[4,64,2560]{2,1,0:T(8,128)(2,1)} %get-tuple-element.106) | copy-start | bytes 3932164
  446.8 29.7 %collective-permute-start.3 = (bf16[64,2560]{1,0:T(8,128)(2,1)S(1)}, bf16[64,2560]{1,0:T(8,128)(2,1)S(1)}, u32[]{:S(2)}, u32[]{:S(2)}) collective-permute-start(bf16[64,2560]{1,0:T(8,128)(2,1)S(1)} %get-tuple-element.116), channel_id=1, source_target_pairs={{0,8},{1,9},{2,10},{3,11},{4,12},{5,13},{6,14},{7,15},{8,0},{9,1},... | collective-permute-start | bytes 983048 | tf_op jit(solution)/shard_map/ppermute | solution.py:454
  446.9 29.7 %collective-permute-start.4 = (bf16[64,2560]{1,0:T(8,128)(2,1)S(1)}, bf16[64,2560]{1,0:T(8,128)(2,1)S(1)}, u32[]{:S(2)}, u32[]{:S(2)}) collective-permute-start(bf16[64,2560]{1,0:T(8,128)(2,1)S(1)} %get-tuple-element.117), channel_id=1, source_target_pairs={{0,16},{1,17},{2,18},{3,19},{4,20},{5,21},{6,22},{7,23},{8,24},{9,... | collective-permute-start | bytes 983048 | tf_op jit(solution)/shard_map/ppermute | solution.py:454
  447.3 29.2 %collective-permute-start.5 = (bf16[64,2560]{1,0:T(8,128)(2,1)S(1)}, bf16[64,2560]{1,0:T(8,128)(2,1)S(1)}, u32[]{:S(2)}, u32[]{:S(2)}) collective-permute-start(bf16[64,2560]{1,0:T(8,128)(2,1)S(1)} %get-tuple-element.118), channel_id=1, source_target_pairs={{0,24},{1,25},{2,26},{3,27},{4,28},{5,29},{6,30},{7,31},{8,16},{9,... | collective-permute-start | bytes 983048 | tf_op jit(solution)/shard_map/ppermute | solution.py:454
  476.5 0.7 copy-start.4
  476.5 0.8 copy-start.6
  476.6 0.9 copy-start.8
  477.5 32.0 %copy-start.5 = (bf16[64,2560]{1,0:T(8,128)(2,1)S(1)}, bf16[64,2560]{1,0:T(8,128)(2,1)}, u32[]{:S(2)}) copy-start(bf16[64,2560]{1,0:T(8,128)(2,1)} %copy-done.4) | copy-start | bytes 983044
  477.5 32.0 %copy-start.7 = (bf16[64,2560]{1,0:T(8,128)(2,1)S(1)}, bf16[64,2560]{1,0:T(8,128)(2,1)}, u32[]{:S(2)}) copy-start(bf16[64,2560]{1,0:T(8,128)(2,1)} %copy-done.6) | copy-start | bytes 983044
  477.5 32.0 %copy-start.9 = (bf16[64,2560]{1,0:T(8,128)(2,1)S(1)}, bf16[64,2560]{1,0:T(8,128)(2,1)}, u32[]{:S(2)}) copy-start(bf16[64,2560]{1,0:T(8,128)(2,1)} %copy-done.8) | copy-start | bytes 983044
  477.5 33.7 %collective-permute-start.6 = (bf16[4,64,1536]{2,1,0:T(8,128)(2,1)}, bf16[4,64,1536]{2,1,0:T(8,128)(2,1)S(1)}, u32[]{:S(2)}, u32[]{:S(2)}) collective-permute-start(bf16[4,64,1536]{2,1,0:T(8,128)(2,1)} %get-tuple-element.123), channel_id=1, source_target_pairs={{0,4},{1,5},{2,6},{3,7},{4,0},{5,1},{6,2},{7,3},{8,12},{9,13},{10,... | collective-permute-start | bytes 2359304 | tf_op jit(solution)/shard_map/ppermute | solution.py:454
  477.5 33.7 %collective-permute-start.7 = (bf16[4,64,1536]{2,1,0:T(8,128)(2,1)}, bf16[4,64,1536]{2,1,0:T(8,128)(2,1)S(1)}, u32[]{:S(2)}, u32[]{:S(2)}) collective-permute-start(bf16[4,64,1536]{2,1,0:T(8,128)(2,1)} %get-tuple-element.124), channel_id=1, source_target_pairs={{0,1},{1,0},{2,3},{3,2},{4,5},{5,4},{6,7},{7,6},{8,9},{9,8},{10,11... | collective-permute-start | bytes 2359304 | tf_op jit(solution)/shard_map/ppermute | solution.py:454
  478.5 36.0 %collective-permute-start.8 = (bf16[4,64,1536]{2,1,0:T(8,128)(2,1)}, bf16[4,64,1536]{2,1,0:T(8,128)(2,1)S(1)}, u32[]{:S(2)}, u32[]{:S(2)}) collective-permute-start(bf16[4,64,1536]{2,1,0:T(8,128)(2,1)} %get-tuple-element.125), channel_id=1, source_target_pairs={{0,5},{1,4},{2,7},{3,6},{4,1},{5,0},{6,3},{7,2},{8,13},{9,12},{10,... | collective-permute-start | bytes 2359304 | tf_op jit(solution)/shard_map/ppermute | solution.py:454
  511.2 3.4 copy-start.1
  511.2 3.4 copy-start.2
  514.5 0.9 copy-start.3
Sparse Core Ops, SparseCore 0:
  11.4 137.0 all-gather.1
  254.5 152.5 reduce-scatter.1

commit v5 on v4

--- a/solution.py
+++ b/solution.py
@@ -76,7 +76,7 @@
     normed = (hat * vec_ref[0:1] + vec_ref[1:2]).astype(bf16)
     normed_ref[...] = normed
     tensor, dp = w_ref.shape[:2]
-    width = w_ref.shape[3] // 4
+    width = w_ref.shape[3] // 3
     for s in range(3):
         for t in range(tensor):
             cols = slice(t * width, (t + 1) * width)
@@ -183,37 +183,26 @@
         keep_before(image, out_ref, (0, pair), query_grad * LOG_SCALE)
 
 
-def merge_kernel(part, count, ctx_ref, x_ref, vec_ref, w_ref, resid_ref, normed_ref):
-    tensor, dp, _, width = w_ref.shape
+def merge_kernel(count, live_ref, ctx_ref, x_ref, vec_ref, w_ref, given_ref, resid_ref, normed_ref, grad_ref):
+    grad_ref[...] = before(given_ref, live_ref[0]).astype(bf16)
+    tensor, dp, part, width = w_ref.shape
     total = before(x_ref, count) + vec_ref[2:3]
     for t in range(tensor):
-        w = w_ref[t, :, :part].reshape(dp * part, width)
+        w = w_ref[t].reshape(dp * part, width)
         total = total + matmul(ctx_ref[:, t * width : (t + 1) * width], w, NT)
     resid_ref[...] = total
     hat, _ = norm_parts(total)
     normed_ref[...] = (hat * vec_ref[3:4] + vec_ref[4:5]).astype(bf16)
 
 
-def mlp_kernel(
-    chunk, live_ref, normed_ref, resid_ref, ebias_ref, vec_ref, e_ref, r_ref, given_ref,
-    out_ref, act_ref, slope_ref, grad_ref,
-):
-    grad_ref[...] = before(given_ref, live_ref[0]).astype(bf16)
-    tensor, dp, rows, width = e_ref.shape
-    normed = normed_ref[...]
-    total = resid_ref[...] + vec_ref[5:6]
-    for t in range(tensor):
-        for c in range(width // chunk):
-            local = slice(c * chunk, (c + 1) * chunk)
-            cols = slice(t * width + c * chunk, t * width + (c + 1) * chunk)
-            e = e_ref[t, :, :, local].reshape(dp * rows, chunk)
-            active, slope = gelu_and_slope(matmul(normed, e) + ebias_ref[:, cols])
-            active = active.astype(bf16)
-            act_ref[:, cols] = active
-            slope_ref[:, cols] = slope.astype(bf16)
-            r = r_ref[t, :, :, local].reshape(dp * rows, chunk)
-            total = total + matmul(active, r, NT)
-    out_ref[...] = total.astype(bf16)
+def expand_kernel(normed_ref, grad_ref, bias_ref, w_ref, act_ref, slope_ref, out_ref):
+    _, dp, part, width = w_ref.shape
+    w = w_ref[0].reshape(dp * part, width)
+    active, slope = gelu_and_slope(matmul(normed_ref[...], w) + bias_ref[...])
+    active = active.astype(bf16)
+    act_ref[...] = active
+    slope_ref[...] = slope.astype(bf16)
+    out_ref[...] = matmul(grad_ref[...], active, TN).astype(bf16).reshape(out_ref.shape)
 
 
 def accumulate(first, ref, value):
@@ -238,7 +227,7 @@
 
 
 def mlp_back_kernel(
-    part, chunk, grad_ref, slope_ref, resid_ref, vec_ref, e_ref, r_ref, m_ref,
+    chunk, grad_ref, slope_ref, resid_ref, vec_ref, e_ref, r_ref, m_ref,
     pre_ref, low_ref, ctx_ref, sums_ref, esum_ref,
 ):
     tensor, dp, rows, width = e_ref.shape
@@ -268,7 +257,7 @@
     low = low_ref[...]
     wide = m_ref.shape[3]
     for t in range(tensor):
-        m = m_ref[t, :, :part].reshape(dp * part, wide)
+        m = m_ref[t].reshape(dp * rows, wide)
         ctx_ref[:, t * wide : (t + 1) * wide] = matmul(low, m).astype(bf16)
     accumulate(first, sums_ref, sums)
     parts = jnp.concatenate(parts, axis=1)
@@ -276,9 +265,22 @@
     accumulate(first, esum_ref, jnp.concatenate(lines, axis=0))
 
 
-def qkv_back_kernel(part, count, x_ref, low_ref, vec_ref, grad_ref, w_ref, out_ref, sums_ref, bsum_ref):
+def qkv_back_kernel(part, count, depth, x_ref, low_ref, vec_ref, grad_ref, w_ref, *refs):
+    reduce_ref, planes, refs = refs[0], refs[1 : depth + 1], refs[depth + 1 :]
+    out_ref, sums_ref, bsum_ref, expand_out_ref, merge_out_ref, reduce_out_ref = refs
+
+    @pl.when(pl.program_id(0) == 0)
+    def _():
+        total = planes[0][...].astype(f32)
+        for ref in planes[1:]:
+            total = total + ref[...].astype(f32)
+        hidden = expand_out_ref.shape[1]
+        expand_out_ref[...] = total[:, :hidden]
+        merge_out_ref[...] = total[:, hidden:]
+        reduce_out_ref[...] = reduce_ref[...].astype(f32)
+
     tensor, dp = w_ref.shape[:2]
-    width = w_ref.shape[3] // 4
+    width = w_ref.shape[3] // 3
     first = pl.program_id(0) == 0
     total = jnp.zeros(x_ref.shape, f32)
     for s in range(3):
@@ -290,52 +292,6 @@
     accumulate(first, sums_ref, jnp.concatenate([gain_sum, shift_sum], axis=0))
     bias = [jnp.sum(grad_ref[s].astype(f32), axis=0, keepdims=True) for s in (0, 2)]
     accumulate(first, bsum_ref, jnp.concatenate(bias, axis=0))
-
-
-def weight_grad_kernel(starts, *refs):
-    count = len(starts) - 1
-    lefts, rights, out_ref = refs[:count], refs[count : 2 * count], refs[-1]
-    step = pl.program_id(0)
-    for j in range(count):
-        @pl.when((step >= starts[j]) & (step < starts[j + 1]))
-        def _():
-            out = matmul(lefts[j][...], rights[j][0], TN)
-            out_ref[...] = out.astype(bf16).reshape(out_ref.shape)
-
-
-def weight_grads(name, pairs, tensor, dp, block):
-    rows, deep = pairs[0][0].shape
-    locals_ = [right.shape[1] // tensor for _, right in pairs]
-    block = min([block] + locals_)
-    pers = [local // block for local in locals_]
-    starts = [0]
-    for per in pers:
-        starts.append(starts[-1] + tensor * per)
-
-    def right_map(j, i):
-        i = jnp.clip(i - starts[j], 0, tensor * pers[j] - 1)
-        return (0, 0, i)
-
-    def out_map(i):
-        where, column, t = 0, 0, 0
-        for j, per in enumerate(pers):
-            inside = (i >= starts[j]) & (i < starts[j + 1])
-            t = t + jnp.where(inside, (i - starts[j]) // per, 0)
-            column = column + jnp.where(inside, where + (i - starts[j]) % per, 0)
-            where += per
-        return (t, 0, 0, column)
-
-    return call(
-        functools.partial(weight_grad_kernel, starts),
-        name,
-        (starts[-1],),
-        [full((rows, deep))] * len(pairs)
-        + [pl.BlockSpec((1, rows, block), functools.partial(right_map, j)) for j in range(len(pairs))],
-        [pl.BlockSpec((1, dp, deep // dp, block), out_map)],
-        [((tensor, dp, deep // dp, sum(locals_)), bf16)],
-        [left for left, _ in pairs] + [right[None] for _, right in pairs],
-        flops=rows * deep * tensor * sum(locals_),
-    )[0]
 
 
 def flip(value, mask):
@@ -472,15 +428,8 @@
     return [swap(planes[z], 4 * z, 0, tensor, dp) for z in range(1, dp // 4)]
 
 
-def sum_line(plane, landed):
-    total = plane.astype(f32)
-    for piece in landed:
-        total = total + piece.astype(f32)
-    return total
-
-
 def pack_kernel(
-    heads_ref, merge_ref, expand_ref, reduce_ref, hb_ref, eb_ref, *refs
+    heads_ref, merge_ref, expand_ref, hb_ref, eb_ref, *refs
 ):
     small, (first_ref, later_ref) = refs[:-2], refs[-2:]
     _, part, own = heads_ref.shape
@@ -499,11 +448,10 @@
     used = sum(piece.shape[1] for piece in pieces)
     pieces.append(jnp.zeros((8, 128 - used), f32))
     first_ref[part:, :128] = jnp.concatenate(pieces, axis=1).astype(bf16)
-    first_ref[:part, 3 * own :] = merge_ref[...]
-    first_ref[part:, 128:] = jnp.zeros((8, 4 * own - 128), bf16)
+    first_ref[part:, 128:] = jnp.zeros((8, 3 * own - 128), bf16)
     hidden = expand_ref.shape[1]
     later_ref[:, :hidden] = expand_ref[...]
-    later_ref[:, hidden:] = reduce_ref[...]
+    later_ref[:, hidden:] = merge_ref[...]
 
 
 def gather_kernel(in_ref, out_ref, own_sem, send_sem, recv_sem):
@@ -617,12 +565,12 @@
     )[0]
 
 
-def tail_kernel(dp, tensor, *refs):
+def last_kernel(dp, tensor, act_ref, resid_ref, vec_ref, w_ref, *refs):
     count, depth = dp * tensor, dp // 4
-    own_ref, refs = refs[0], refs[1:]
-    others, refs = refs[: 2 * tensor - 1], refs[2 * tensor - 1 :]
-    one_ref, two_ref, hb_ref, eb_ref, out_ref, sums_ref = refs[:6]
-    packed, landed, line, arrived, send_sem, recv_sem, line_send, line_recv = refs[6:]
+    own_ref, others, refs = refs[0], refs[1 : 2 * tensor], refs[2 * tensor :]
+    one_ref, two_ref, hb_ref, eb_ref, out_ref, heads_ref, sums_ref = refs[:7]
+    packed, landed, line, arrived, send_sem, recv_sem, line_send, line_recv = refs[7:]
+    step = pl.program_id(0)
     d, y = lax.axis_index("dp"), lax.axis_index("tensor")
     me = d * tensor + y
     part = own_ref.shape[1]
@@ -636,8 +584,6 @@
         _, where = place(k)
         pl.semaphore_signal(barrier, inc=1, device_id=where, device_id_type=pl.DeviceIdType.MESH)
         return carry
-
-    lax.fori_loop(1, count, greet, 0)
 
     def plane(z):
         total = own_ref[z].astype(f32)
@@ -645,48 +591,45 @@
             total = total + ref[z].astype(f32)
         return total
 
-    for z in range(1, depth):
-        line[z - 1] = plane(z).astype(bf16)
-    heads = hb_ref.shape[1] // HEAD_DIM
-    own_heads, hb_wide = heads // tensor, HEAD_DIM // dp
-    eb_tall, eb_wide = eb_ref.shape[0] // tensor, eb_ref.shape[1] // dp
-    hb = [
-        hb_ref[k : k + 1, h * HEAD_DIM : (h + 1) * HEAD_DIM] for k in range(2) for h in range(heads)
-    ]
-    hb = jnp.concatenate(hb, axis=0).T
-    eb = eb_ref[...].T
-    sums = jnp.concatenate([one_ref[...], two_ref[3:4], two_ref[1:3], two_ref[0:1]], axis=0)
-    for p in range(dp):
-        piece = sums[:, p * part : (p + 1) * part]
-        for q in range(tensor):
-            packed[p * tensor + q, 0:6, 0:part] = piece
-            lane = part
-            packed[p * tensor + q, 0:eb_wide, lane : lane + eb_tall] = eb[
-                p * eb_wide : (p + 1) * eb_wide, q * eb_tall : (q + 1) * eb_tall
-            ]
-            for k in range(2):
-                lane = part + eb_tall + k * own_heads
-                packed[p * tensor + q, 0:hb_wide, lane : lane + own_heads] = hb[
-                    p * hb_wide : (p + 1) * hb_wide,
-                    k * heads + q * own_heads : k * heads + (q + 1) * own_heads,
+    @pl.when(step == 0)
+    def _():
+        lax.fori_loop(1, count, greet, 0)
+        for z in range(1, depth):
+            line[z - 1] = plane(z).astype(bf16)
+        heads = hb_ref.shape[1] // HEAD_DIM
+        own_heads, hb_wide = heads // tensor, HEAD_DIM // dp
+        eb_tall, eb_wide = eb_ref.shape[0] // tensor, eb_ref.shape[1] // dp
+        hb = [
+            hb_ref[k : k + 1, h * HEAD_DIM : (h + 1) * HEAD_DIM] for k in range(2) for h in range(heads)
+        ]
+        hb = jnp.concatenate(hb, axis=0).T
+        eb = eb_ref[...].T
+        sums = jnp.concatenate([one_ref[...], two_ref[3:4], two_ref[1:3], two_ref[0:1]], axis=0)
+        for p in range(dp):
+            piece = sums[:, p * part : (p + 1) * part]
+            for q in range(tensor):
+                packed[p * tensor + q, 0:6, 0:part] = piece
+                packed[p * tensor + q, 0:eb_wide, part : part + eb_tall] = eb[
+                    p * eb_wide : (p + 1) * eb_wide, q * eb_tall : (q + 1) * eb_tall
                 ]
-    pl.semaphore_wait(barrier, count - 1)
-
-    copies = []
-    for z in range(1, depth):
-        far = d
-        for bit in range(depth.bit_length() - 1):
-            if (z >> bit) & 1:
-                unit = 4 << bit
-                far = far + unit - 2 * unit * lax.rem(lax.div(far, unit), 2)
-        copies.append(pltpu.make_async_remote_copy(
+                for k in range(2):
+                    lane = part + eb_tall + k * own_heads
+                    packed[p * tensor + q, 0:hb_wide, lane : lane + own_heads] = hb[
+                        p * hb_wide : (p + 1) * hb_wide,
+                        k * heads + q * own_heads : k * heads + (q + 1) * own_heads,
+                    ]
+
+    copies = [
+        pltpu.make_async_remote_copy(
             src_ref=line.at[z - 1],
             dst_ref=arrived.at[z - 1],
             send_sem=line_send.at[z - 1],
             recv_sem=line_recv.at[z - 1],
-            device_id=(far, y),
+            device_id=(flip(d, 4 * z), y),
             device_id_type=pl.DeviceIdType.MESH,
-        ))
+        )
+        for z in range(1, depth)
+    ]
 
     def copy(k):
         other, where = place(k)
@@ -703,48 +646,34 @@
         copy(k).start()
         return carry
 
-    lax.fori_loop(1, count, start, 0)
-    for item in copies:
-        item.start()
-    total = plane(0)
+    @pl.when(step == 1)
+    def _():
+        pl.semaphore_wait(barrier, count - 1)
+        lax.fori_loop(1, count, start, 0)
+        for item in copies:
+            item.start()
+
+    total = resid_ref[...] + vec_ref[5:6]
+    width = w_ref.shape[3]
+    for t in range(tensor):
+        w = w_ref[t].reshape(dp * part, width)
+        total = total + matmul(act_ref[:, t * width : (t + 1) * width], w, NT)
+    out_ref[...] = total.astype(bf16)
 
     def finish(k, sums):
         copy(k).wait()
         return sums + landed[k]
 
-    sums = lax.fori_loop(1, count, finish, packed[me])
-    sums_ref[...] = sums
-    for item, z in zip(copies, range(1, depth)):
-        item.wait()
-        total = total + arrived[z - 1].astype(f32)
-    own = out_ref.shape[2]
-    for s in range(3):
-        out_ref[s] = total[:, s * own : (s + 1) * own]
-
-
-def tail(part_own, landed, sums, hb, eb, tensor, dp):
-    depth, part, lanes = part_own.shape
-    count = tensor * dp
-    arrays = [part_own, *landed, *sums, hb, eb]
-    vmem = pl.BlockSpec(memory_space=pltpu.VMEM)
-    out = [((3, part, lanes // 3), f32), ((8, 128), f32)]
-    return call(
-        functools.partial(tail_kernel, dp, tensor),
-        "tail",
-        (),
-        [vmem] * len(arrays),
-        [vmem] * len(out),
-        out,
-        arrays,
-        [
-            pltpu.VMEM((count, 8, 128), f32), pltpu.VMEM((count, 8, 128), f32),
-            pltpu.VMEM((depth - 1, part, lanes), bf16), pltpu.VMEM((depth - 1, part, lanes), bf16),
-            pltpu.SemaphoreType.DMA((count,)), pltpu.SemaphoreType.DMA((count,)),
-            pltpu.SemaphoreType.DMA((depth - 1,)), pltpu.SemaphoreType.DMA((depth - 1,)),
-        ],
-        collective_id=0,
-        has_side_effects=True,
-    )
+    @pl.when(step == pl.num_programs(0) - 1)
+    def _():
+        sums_ref[...] = lax.fori_loop(1, count, finish, packed[me])
+        total = plane(0)
+        for item, z in zip(copies, range(1, depth)):
+            item.wait()
+            total = total + arrived[z - 1].astype(f32)
+        own = heads_ref.shape[2]
+        for s in range(3):
+            heads_ref[s] = total[:, s * own : (s + 1) * own]
 
 
 def finish_kernel(sums_ref, heads_ref, out_ref, hb_ref, eb_ref, *vectors):
@@ -797,16 +726,18 @@
 
     small = [first_gain, first_shift, merge_bias, second_gain, second_shift, reduce_bias]
     arrays = [
-        heads_weight, merge_weight.T, expand_weight, reduce_weight.T,
+        heads_weight, merge_weight.T, expand_weight,
         heads_bias.transpose(0, 2, 1), expand_bias.T,
     ] + [v.reshape(1, part) for v in small]
     vmem = pl.BlockSpec(memory_space=pltpu.VMEM)
     first, later = call(
         pack_kernel, "pack", (), [vmem] * len(arrays), [vmem] * 2,
-        [((part + 8, 4 * own), bf16), ((part, 2 * hidden_own), bf16)], arrays,
+        [((part + 8, 3 * own), bf16), ((part, hidden_own + own), bf16)], arrays,
     )
     wide = gather(later)
     wide_heads = gather_first(first, tensor, dp)
+    wide_heads, turned = lax.optimization_barrier((wide_heads, reduce_weight.T))
+    wide_reduce = gather(turned)
 
     hbs, ebs = heads_bias.shape, expand_bias.shape
     small = wide_heads[:, :, part:, :128].astype(f32)
@@ -824,8 +755,7 @@
         return pl.BlockSpec(shape, lambda *_: (0, 0, 0, index), pipeline_mode=pl.Buffered(1))
 
     vec = full((6, deep))
-    expand_spec, reduce_spec = columns(wide, 0, hidden_own), columns(wide, 1, hidden_own)
-    merge_spec = columns(wide_heads, 3, own)
+    expand_spec, merge_spec = columns(wide, 0, hidden_own), columns(wide, hidden_own // own, own)
     triple_spec = pl.BlockSpec((3, block, deep), lambda i: (0, i, 0))
     normed_one, triple = call(
         functools.partial(qkv_kernel, part, rows),
@@ -856,51 +786,49 @@
         flops=attend_flops,
     )
 
-    resid, normed_two = call(
-        functools.partial(merge_kernel, part, rows),
+    resid, normed_two, grad = call(
+        functools.partial(merge_kernel, rows),
         "merge",
         (blocks,),
-        [by_rows(deep), by_rows(deep), vec, merge_spec],
-        [by_rows(deep), by_rows(deep)],
-        [((total_rows, deep), f32), ((total_rows, deep), bf16)],
-        (context, activations, vectors, wide_heads),
+        [by_rows(deep), by_rows(deep), vec, merge_spec, by_rows(deep)],
+        [by_rows(deep), by_rows(deep), by_rows(deep)],
+        [((total_rows, deep), f32), ((total_rows, deep), bf16), ((total_rows, deep), bf16)],
+        (live, context, activations, vectors, wide, output_grad),
         flops=total_rows * deep * deep,
-    )
-
-    chunk = min(1024, hidden_own)
-    output, active, slope, grad = call(
-        functools.partial(mlp_kernel, chunk),
-        "mlp",
-        (blocks,),
+        prefetch=1,
+    )
+
+    chunk = min(512, hidden_own)
+    per = hidden_own // chunk
+    chunk_spec = pl.BlockSpec((total_rows, chunk), lambda c: (0, c))
+    shard_spec = pl.BlockSpec((1, dp, part, chunk), lambda c: (c // per, 0, 0, c % per))
+    active, slope, grad_reduce = call(
+        expand_kernel,
+        "expand",
+        (hidden // chunk,),
         [
-            by_rows(deep), by_rows(deep), full((1, hidden)), vec, expand_spec, reduce_spec, by_rows(deep),
+            full((total_rows, deep)), full((total_rows, deep)),
+            pl.BlockSpec((1, chunk), lambda c: (0, c)), shard_spec,
         ],
-        [by_rows(deep), by_rows(hidden), by_rows(hidden), by_rows(deep)],
+        [chunk_spec, chunk_spec, shard_spec],
         [
-            ((rows, deep), bf16), ((total_rows, hidden), bf16), ((total_rows, hidden), bf16),
-            ((total_rows, deep), bf16),
+            ((total_rows, hidden), bf16), ((total_rows, hidden), bf16),
+            ((tensor, dp, part, hidden_own), bf16),
         ],
-        (live, normed_two, resid, eb, vectors, wide, wide, output_grad),
-        prefetch=1,
+        (normed_two, grad, eb, wide),
         flops=total_rows * deep * hidden * 2,
     )
-
-    def scatter(grads):
-        grads = grads.reshape(tensor * dp * part, grads.shape[3])
-        return lax.psum_scatter(grads, AXES, scatter_dimension=0, tiled=True)
-
-    grad_reduce = weight_grads("reduce_grad", [(grad, active)], tensor, dp, 512)
-    grad, slope, grad_reduce = lax.optimization_barrier((grad, slope, grad_reduce))
-    grad_reduce = scatter(grad_reduce)
+    grad_reduce = grad_reduce.reshape(tensor * dp * part, hidden_own)
+    grad_reduce = lax.psum_scatter(grad_reduce, AXES, scatter_dimension=0, tiled=True)
 
     back_chunk = min(512, hidden_own)
     pre_grad, resid_low, grad_context, sums_two, esum = call(
-        functools.partial(mlp_back_kernel, part, back_chunk),
+        functools.partial(mlp_back_kernel, back_chunk),
         "mlp_back",
         (blocks,),
         [
             by_rows(deep), by_rows(hidden), by_rows(deep), vec,
-            expand_spec, reduce_spec, merge_spec,
+            expand_spec, full(wide_reduce.shape), merge_spec,
         ],
         [
             by_rows(hidden), by_rows(deep), by_rows(deep),
@@ -910,7 +838,7 @@
             ((total_rows, hidden), bf16), ((total_rows, deep), bf16), ((total_rows, deep), bf16),
             ((4, deep), f32), ((hidden // 128, 128), f32),
         ],
-        (grad, slope, resid, vectors, wide, wide, wide_heads),
+        (grad, slope, resid, vectors, wide, wide_reduce, wide),
     )
     parts = slot_grads(
         "middle_grad", [(normed_two, pre_grad[None]), (resid_low, context[None])], tensor, dp, 512, 2
@@ -934,19 +862,43 @@
     held = (tuple(parts), tuple(landed), planes[0], resid_low)
     parts, landed, plane_own, resid_low = lax.optimization_barrier(held)
     last = send_plane(parts, tensor, dp)
-    grad_middle = sum_line(plane_own, landed)
-    input_grad, sums_one, bsum = call(
-        functools.partial(qkv_back_kernel, part, rows),
+    def whole(shape):
+        return pl.BlockSpec(shape, lambda *_: (0,) * len(shape))
+
+    shapes = [(2, deep), (2, deep), (part, hidden_own), (part, own), (part, hidden_own)]
+    input_grad, sums_one, bsum, grad_expand, grad_merge, grad_reduce = call(
+        functools.partial(qkv_back_kernel, part, rows, dp // 4),
         "qkv_back",
         (blocks,),
-        [by_rows(deep), by_rows(deep), vec, triple_spec, full(wide_heads.shape)],
-        [by_rows(deep), pl.BlockSpec((2, deep), lambda i: (0, 0)), pl.BlockSpec((2, deep), lambda i: (0, 0))],
-        [((rows, deep), bf16), ((2, deep), f32), ((2, deep), f32)],
-        (activations, resid_low, vectors, grad_triple, wide_heads),
+        [by_rows(deep), by_rows(deep), vec, triple_spec, full(wide_heads.shape), full(grad_reduce.shape)]
+        + [full(plane_own.shape)] * (dp // 4),
+        [by_rows(deep)] + [whole(shape) for shape in shapes],
+        [((rows, deep), bf16)] + [(shape, f32) for shape in shapes],
+        (activations, resid_low, vectors, grad_triple, wide_heads, grad_reduce, plane_own, *landed),
         flops=total_rows * deep * deep * 3,
     )
 
-    heads_sum, sums = tail(parts[0], last, (sums_one, sums_two), bsum, esum, tensor, dp)
+    hbs, ebs = heads_bias.shape, expand_bias.shape
+    depth = dp // 4
+    arrays = [parts[0], *last, sums_one, sums_two, bsum, esum]
+    output, heads_sum, sums = call(
+        functools.partial(last_kernel, dp, tensor),
+        "reduce",
+        (blocks,),
+        [by_rows(hidden), by_rows(deep), vec, full(wide_reduce.shape)] + [full(v.shape) for v in arrays],
+        [by_rows(deep), whole((3, part, own)), whole((8, 128))],
+        [((rows, deep), bf16), ((3, part, own), f32), ((8, 128), f32)],
+        (active, resid, vectors, wide_reduce, *arrays),
+        [
+            pltpu.VMEM((tensor * dp, 8, 128), f32), pltpu.VMEM((tensor * dp, 8, 128), f32),
+            pltpu.VMEM((depth - 1, part, 3 * own), bf16), pltpu.VMEM((depth - 1, part, 3 * own), bf16),
+            pltpu.SemaphoreType.DMA((tensor * dp,)), pltpu.SemaphoreType.DMA((tensor * dp,)),
+            pltpu.SemaphoreType.DMA((depth - 1,)), pltpu.SemaphoreType.DMA((depth - 1,)),
+        ],
+        flops=total_rows * deep * hidden,
+        collective_id=0,
+        has_side_effects=True,
+    )
     grad_heads, hb_grad, eb_grad, *vector = call(
         finish_kernel, "finish", (), [vmem] * 2, [vmem] * 9,
         [(heads_sum.shape, f32), ((2, hbs[2], hbs[1]), f32), (ebs[::-1], f32)] + [((1, part), f32)] * 6,
@@ -961,13 +913,13 @@
         vector[1],
         grad_heads,
         hb_grad.transpose(0, 2, 1),
-        grad_middle[:, hidden_own:].T,
+        grad_merge.T,
         vector[2],
         vector[3],
         vector[4],
-        grad_middle[:, :hidden_own],
+        grad_expand,
         eb_grad.T,
-        grad_reduce.astype(f32).T,
+        grad_reduce.T,
         vector[5],
     )
 

time: 559 us -> 522 us (0.934)
  Pallas kernels: 506 us -> 462 us
    pallas_call x14 -> x13, Pallas kernels: 506 us -> 462 us  [call(): pl.pallas_call(kernel, grid_spec=pltpu.PrefetchScalarGridSpec(num_scalar_...]
  transfers between devices with their start and end apart: 11 -> 12, of which waited for: 2 -> 2; matrix products, arithmetic and copies ran while one was open for 1% -> 1% of each run, Pallas kernels for 76% -> 84%
where the time goes in v5:
time: 522 us; the launch traced here: 512 us
  Pallas kernels  462 us (89%)
  between operations  15 us (3%)
  starting transfers between devices  14.1 us (3%)
  local copies, waits for them, and re-layouts  9.35 us (2%)
  waiting for transfers between devices  7.37 us (1%)
    pallas_call x13, Pallas kernels, call(): pl.pallas_call(kernel, grid_spec=pltpu.PrefetchScalarGridSpec(num_scalar_...  462 us
    ppermute x9, starting transfers between devices, swap(): return lax.ppermute(values, ('dp', 'tensor'), moves)  14 us
  transfers between devices with their start and end apart: 12, of which 2 were waited for; matrix products, arithmetic and copies ran while one was open for 1% of the time, Pallas kernels for 84%

profile of v5, /device:TPU:0, one launch (start us, length us, event | category | flops | bytes accessed | tf_op | source)
XLA Modules:
  0.0 511.9 jit_solution(13038204188967353396)
XLA Ops:
  7.2 2.0 pack.1
  9.3 52.6 %gather.1.w_ref = bf16[2,16,72,1536]{3,2,1,0:T(8,128)(2,1)} custom-call(bf16[72,1536]{1,0:T(8,128)(2,1)} %get-tuple-element.83.in_ref), custom_call_target="tpu_custom_call" | custom-call | tf_op jit(solution)/shard_map/gather/pallas_call | solution.py:52
  62.6 0.9 slice_convert_fusion
  65.8 0.8 reshape.127.bias_ref
  66.5 22.9 %qkv.1 = (bf16[2320,1024]{1,0:T(8,128)(2,1)}, bf16[3,2320,1024]{2,1,0:T(8,128)(2,1)}) custom-call(bf16[2308,1024]{1,0:T(8,128)(2,1)} %x_ref.5, f32[6,1024]{1,0:T(8,128)} %reshape.123.vec_ref, f32[2,1024]{1,0:T(2,128)} %reshape.125.bias_ref, bf16[2,16,72,1536]{3,2,1,0:T(8,128)(2,1)} %gather.1.w_ref), custom_call_target="tpu_custom_call" | custom-call | flops 14596177920 | bytes 30842880 | tf_op jit(solution)/shard_map/qkv/pallas_call | solution.py:52
  89.4 43.9 %attend.1 = (bf16[2320,1024]{1,0:T(8,128)(2,1)}, f32[16,4,592]{2,1,0:T(4,128)}) custom-call(bf16[3,2320,1024]{2,1,0:T(8,128)(2,1)} %get-tuple-element.85.triple_ref), custom_call_target="tpu_custom_call" | custom-call | flops 29796335616 | bytes 19156992 | tf_op jit(solution)/shard_map/attend/pallas_call | solution.py:52
  133.3 16.8 %merge.1 = (f32[2320,1024]{1,0:T(8,128)}, bf16[2320,1024]{1,0:T(8,128)(2,1)}, bf16[2320,1024]{1,0:T(8,128)(2,1)}) custom-call(s32[1]{0:T(128)S(6)} %mul.7.live_ref, bf16[2320,1024]{1,0:T(8,128)(2,1)} %get-tuple-element.86.ctx_ref, bf16[2308,1024]{1,0:T(8,128)(2,1)} %x_ref.5, f32[6,1024]{1,0:T(8,128)} %reshape.123.vec_ref, ...), custom_call_target="tpu_custom_call" | custom-call | flops 4865392640 | bytes 43720708 | tf_op jit(solution)/shard_map/merge/pallas_call | solution.py:52
  150.0 55.2 %expand.1 = (bf16[2320,4096]{1,0:T(8,128)(2,1)}, bf16[2320,4096]{1,0:T(8,128)(2,1)}, bf16[2,16,64,2048]{3,2,1,0:T(8,128)(2,1)}) custom-call(bf16[2320,1024]{1,0:T(8,128)(2,1)} %get-tuple-element.88.normed_ref.refs_0_, bf16[2320,1024]{1,0:T(8,128)(2,1)} %get-tuple-element.89.grad_ref, f32[1,4096]{1,0:T(1,128)} %reshape.127.bias_ref, ...), custom_call_target="tpu_custom_call" | custom-call | flops 38923141120 | bytes 66404352 | tf_op jit(solution)/shard_map/expand/pallas_call | solution.py:52
  205.2 66.1 %mlp_back.1 = (bf16[2320,4096]{1,0:T(8,128)(2,1)}, bf16[2320,1024]{1,0:T(8,128)(2,1)}, bf16[2320,1024]{1,0:T(8,128)(2,1)}, f32[4,1024]{1,0:T(4,128)}, f32[32,128]{1,0:T(8,128)}) custom-call(bf16[2320,1024]{1,0:T(8,128)(2,1)} %get-tuple-element.89.grad_ref, bf16[2320,4096]{1,0:T(8,128)(2,1)} %get-tuple-element.94.slope_ref, ...), custom_call_target="tpu_custom_call" | custom-call | tf_op jit(solution)/shard_map/mlp_back/pallas_call | solution.py:52
  271.3 40.9 %middle_grad.1 = (bf16[4,64,2560]{2,1,0:T(8,128)(2,1)}, bf16[4,64,2560]{2,1,0:T(8,128)(2,1)}, bf16[4,64,2560]{2,1,0:T(8,128)(2,1)}, bf16[4,64,2560]{2,1,0:T(8,128)(2,1)}) custom-call(bf16[2320,1024]{1,0:T(8,128)(2,1)} %get-tuple-element.88.normed_ref.refs_0_, bf16[2320,1024]{1,0:T(8,128)(2,1)} %get-tuple-element.126.refs_1_.low_ref, ...), custom_call_target="tpu_custom_call" | custom-call | tf_op jit(solution)/shard_map/middle_grad/pallas_call | solution.py:52
  312.6 4.3 collective-permute-start.1
  316.9 1.4 collective-permute-start.2
  318.3 75.7 %attend_back.1.refs_1_.grad_ref = bf16[3,2320,1024]{2,1,0:T(8,128)(2,1)} custom-call(bf16[3,2320,1024]{2,1,0:T(8,128)(2,1)} %get-tuple-element.85.triple_ref, f32[16,4,592]{2,1,0:T(4,128)} %get-tuple-element.106.stat_ref, bf16[2320,1024]{1,0:T(8,128)(2,1)} %get-tuple-element.107.grad_ref), custom_call_target="tpu_custom_call" | custom-call | tf_op jit(solution)/shard_map/attend_back/pallas_call | solution.py:52
  394.0 2.8 collective-permute-done.2
  396.8 2.8 fusion.3
  399.8 4.2 collective-permute-start.5
  404.0 25.3 %heads_grad.1 = (bf16[4,64,1536]{2,1,0:T(8,128)(2,1)}, bf16[4,64,1536]{2,1,0:T(8,128)(2,1)}, bf16[4,64,1536]{2,1,0:T(8,128)(2,1)}, bf16[4,64,1536]{2,1,0:T(8,128)(2,1)}) custom-call(bf16[2320,1024]{1,0:T(8,128)(2,1)} %get-tuple-element.93.refs_0_, bf16[3,2320,1024]{2,1,0:T(8,128)(2,1)} %attend_back.1.refs_1_.grad_ref), custom_call_target="tpu_custom_call" | custom-call | tf_op jit(solution)/shard_map/heads_grad/pallas_call | solution.py:52
  429.7 3.3 collective-permute-start.8
  433.0 28.7 %qkv_back.1 = (bf16[2308,1024]{1,0:T(8,128)(2,1)}, f32[2,1024]{1,0:T(2,128)}, f32[2,1024]{1,0:T(2,128)}, f32[64,2048]{1,0:T(8,128)}, f32[64,512]{1,0:T(8,128)}, /*index=5*/f32[64,2048]{1,0:T(8,128)}) custom-call(bf16[2308,1024]{1,0:T(8,128)(2,1)} %x_ref.5, bf16[2320,1024]{1,0:T(8,128)(2,1)} %get-tuple-element.126.refs_1_.low_ref, ...), custom_call_target="tpu_custom_call" | custom-call | flops 14596177920 | bytes 38330368 | tf_op jit(solution)/shard_map/qkv_back/pallas_call | solution.py:52
  461.8 4.5 collective-permute-done.7.refs_2_
  466.2 0.9 copy-done.2
  467.5 30.6 %reduce.1 = (bf16[2308,1024]{1,0:T(8,128)(2,1)}, f32[3,64,512]{2,1,0:T(8,128)}, f32[8,128]{1,0:T(8,128)}) custom-call(bf16[2320,4096]{1,0:T(8,128)(2,1)} %get-tuple-element.90.act_ref, f32[2320,1024]{1,0:T(8,128)} %get-tuple-element.91.resid_ref, f32[6,1024]{1,0:T(8,128)} %reshape.123.vec_ref, bf16[2,16,64,2048]{3,2,1,0:T(8,128)(2,1)} %bitcast.54, ...), custom_call_target="tpu_custom_call" | custom-call | flops 19461570560 | bytes 45240320 | tf_op jit(solution)/shard_map/reduce/pallas_call | solution.py:52
  498.1 1.8 finish.1
  499.9 5.0 copy.37
  (42 shorter events, 3.7 us)
Async XLA Ops:
  7.2 126.1 %all-gather.3.cloned.1.call-start = ((), (), s32[]{:S(2)}) async-start(), calls=%async_computation.1 | async-start | bytes 10813440 | tf_op jit(solution)/shard_map/all_gather | solution.py:724
  9.2 196.0 %all-gather.5.cloned.1.call-start = ((), (), s32[]{:S(2)}) async-start(), calls=%async_computation.2 | async-start | bytes 8650752 | tf_op jit(solution)/shard_map/all_gather | solution.py:724
  61.9 371.1 %reduce-scatter.2.cloned.1.call-start = ((), (), s32[]{:S(2)}) async-start(), calls=%async_computation.3 | async-start | bytes 8650752 | tf_op jit(solution)/shard_map/reduce_scatter | solution.py:822
  312.2 81.8 %collective-permute-start = (bf16[4,64,2560]{2,1,0:T(8,128)(2,1)}, bf16[4,64,2560]{2,1,0:T(8,128)(2,1)S(1)}, u32[]{:S(2)}, u32[]{:S(2)}) collective-permute-start(bf16[4,64,2560]{2,1,0:T(8,128)(2,1)} %get-tuple-element.102), channel_id=1, source_target_pairs={{0,4},{1,5},{2,6},{3,7},{4,0},{5,1},{6,2},{7,3},{8,12},{9,13},{10,... | collective-permute-start | bytes 3932168 | tf_op jit(solution)/shard_map/ppermute | solution.py:410
  312.6 81.4 %collective-permute-start.1 = (bf16[4,64,2560]{2,1,0:T(8,128)(2,1)}, bf16[4,64,2560]{2,1,0:T(8,128)(2,1)S(1)}, u32[]{:S(2)}, u32[]{:S(2)}) collective-permute-start(bf16[4,64,2560]{2,1,0:T(8,128)(2,1)} %get-tuple-element.103), channel_id=1, source_target_pairs={{0,1},{1,0},{2,3},{3,2},{4,5},{5,4},{6,7},{7,6},{8,9},{9,8},{10,11... | collective-permute-start | bytes 3932168 | tf_op jit(solution)/shard_map/ppermute | solution.py:410
  316.9 79.9 %collective-permute-start.2 = (bf16[4,64,2560]{2,1,0:T(8,128)(2,1)}, bf16[4,64,2560]{2,1,0:T(8,128)(2,1)}, u32[]{:S(2)}, u32[]{:S(2)}) collective-permute-start(bf16[4,64,2560]{2,1,0:T(8,128)(2,1)} %get-tuple-element.104), channel_id=1, source_target_pairs={{0,5},{1,4},{2,7},{3,6},{4,1},{5,0},{6,3},{7,2},{8,13},{9,12},{10,... | collective-permute-start | bytes 3932168 | tf_op jit(solution)/shard_map/ppermute | solution.py:410
  318.3 78.5 %copy-start = (bf16[4,64,2560]{2,1,0:T(8,128)(2,1)S(1)}, bf16[4,64,2560]{2,1,0:T(8,128)(2,1)}, u32[]{:S(2)}) copy-start(bf16[4,64,2560]{2,1,0:T(8,128)(2,1)} %get-tuple-element.108) | copy-start | bytes 3932164
  399.6 29.7 %collective-permute-start.3 = (bf16[64,2560]{1,0:T(8,128)(2,1)}, bf16[64,2560]{1,0:T(8,128)(2,1)S(1)}, u32[]{:S(2)}, u32[]{:S(2)}) collective-permute-start(bf16[64,2560]{1,0:T(8,128)(2,1)} %get-tuple-element.118), channel_id=1, source_target_pairs={{0,8},{1,9},{2,10},{3,11},{4,12},{5,13},{6,14},{7,15},{8,0},{9,1},... | collective-permute-start | bytes 983048 | tf_op jit(solution)/shard_map/ppermute | solution.py:410
  399.6 29.8 %collective-permute-start.4 = (bf16[64,2560]{1,0:T(8,128)(2,1)}, bf16[64,2560]{1,0:T(8,128)(2,1)S(1)}, u32[]{:S(2)}, u32[]{:S(2)}) collective-permute-start(bf16[64,2560]{1,0:T(8,128)(2,1)} %get-tuple-element.119), channel_id=1, source_target_pairs={{0,16},{1,17},{2,18},{3,19},{4,20},{5,21},{6,22},{7,23},{8,24},{9,... | collective-permute-start | bytes 983048 | tf_op jit(solution)/shard_map/ppermute | solution.py:410
  399.8 29.6 %collective-permute-start.5 = (bf16[64,2560]{1,0:T(8,128)(2,1)}, bf16[64,2560]{1,0:T(8,128)(2,1)S(1)}, u32[]{:S(2)}, u32[]{:S(2)}) collective-permute-start(bf16[64,2560]{1,0:T(8,128)(2,1)} %get-tuple-element.120), channel_id=1, source_target_pairs={{0,24},{1,25},{2,26},{3,27},{4,28},{5,29},{6,30},{7,31},{8,16},{9,... | collective-permute-start | bytes 983048 | tf_op jit(solution)/shard_map/ppermute | solution.py:410
  429.4 3.6 copy-start.4
  429.4 3.6 copy-start.5
  429.4 3.6 copy-start.6
  429.4 32.3 %collective-permute-start.6 = (bf16[4,64,1536]{2,1,0:T(8,128)(2,1)}, bf16[4,64,1536]{2,1,0:T(8,128)(2,1)S(1)}, u32[]{:S(2)}, u32[]{:S(2)}) collective-permute-start(bf16[4,64,1536]{2,1,0:T(8,128)(2,1)} %get-tuple-element.123), channel_id=1, source_target_pairs={{0,4},{1,5},{2,6},{3,7},{4,0},{5,1},{6,2},{7,3},{8,12},{9,13},{10,... | collective-permute-start | bytes 2359304 | tf_op jit(solution)/shard_map/ppermute | solution.py:410
  429.5 36.7 %collective-permute-start.7 = (bf16[4,64,1536]{2,1,0:T(8,128)(2,1)}, bf16[4,64,1536]{2,1,0:T(8,128)(2,1)S(1)}, u32[]{:S(2)}, u32[]{:S(2)}) collective-permute-start(bf16[4,64,1536]{2,1,0:T(8,128)(2,1)} %get-tuple-element.124), channel_id=1, source_target_pairs={{0,1},{1,0},{2,3},{3,2},{4,5},{5,4},{6,7},{7,6},{8,9},{9,8},{10,11... | collective-permute-start | bytes 2359304 | tf_op jit(solution)/shard_map/ppermute | solution.py:410
  429.7 36.5 %collective-permute-start.8 = (bf16[4,64,1536]{2,1,0:T(8,128)(2,1)}, bf16[4,64,1536]{2,1,0:T(8,128)(2,1)S(1)}, u32[]{:S(2)}, u32[]{:S(2)}) collective-permute-start(bf16[4,64,1536]{2,1,0:T(8,128)(2,1)} %get-tuple-element.125), channel_id=1, source_target_pairs={{0,5},{1,4},{2,7},{3,6},{4,1},{5,0},{6,3},{7,2},{8,13},{9,12},{10,... | collective-permute-start | bytes 2359304 | tf_op jit(solution)/shard_map/ppermute | solution.py:410
  461.8 4.5 copy-start.1
  466.2 0.9 copy-start.2
  466.2 1.2 copy-start.3
Sparse Core Ops, SparseCore 0:
  11.5 98.5 all-gather.2
  113.0 75.9 all-gather.4
  205.3 154.3 reduce-scatter.1

commit v6 on v5

--- a/solution.py
+++ b/solution.py
@@ -145,8 +145,35 @@
     stat_ref[0] = jnp.concatenate(stats, axis=1).T
 
 
-def attend_back_kernel(triple_ref, stat_ref, grad_ref, out_ref):
+def attend_back_kernel(tensor, triple_ref, stat_ref, grad_ref, *refs):
+    peers = 2 * tensor - 1
+    parts, (out_ref, planes_ref, landed, send_sem, recv_sem) = refs[: peers + 1], refs[peers + 1 :]
     image = pl.program_id(1)
+    step = pl.program_id(0) * pl.num_programs(1) + image
+    d, y = lax.axis_index("dp"), lax.axis_index("tensor")
+    barrier = pltpu.get_barrier_semaphore()
+    mesh = pl.DeviceIdType.MESH
+    places = [(flip(d, 2 * (k % 2)), flip(y, k // 2)) for k in range(1, peers + 1)]
+
+    @pl.when(step == 0)
+    def _():
+        for where in places:
+            pl.semaphore_signal(barrier, inc=1, device_id=where, device_id_type=mesh)
+
+    copies = [
+        pltpu.make_async_remote_copy(
+            src_ref=parts[k + 1], dst_ref=landed.at[k], send_sem=send_sem.at[k],
+            recv_sem=recv_sem.at[k], device_id=where, device_id_type=mesh,
+        )
+        for k, where in enumerate(places)
+    ]
+
+    @pl.when(step == 1)
+    def _():
+        pl.semaphore_wait(barrier, peers)
+        for item in copies:
+            item.start()
+
     rows = lax.broadcasted_iota(jnp.int32, (WINDOW, 1), 0)
     mask = jnp.where((rows >= image) & (rows < image + SEQ), 0.0, -1e30)
     lanes = lax.broadcasted_iota(jnp.int32, (1, LANES), 1)
@@ -182,9 +209,18 @@
         query_grad = jnp.concatenate(query_grad, axis=0).T[:WINDOW]
         keep_before(image, out_ref, (0, pair), query_grad * LOG_SCALE)
 
-
-def merge_kernel(count, live_ref, ctx_ref, x_ref, vec_ref, w_ref, given_ref, resid_ref, normed_ref, grad_ref):
-    grad_ref[...] = before(given_ref, live_ref[0]).astype(bf16)
+    @pl.when(step == pl.num_programs(0) * pl.num_programs(1) - 1)
+    def _():
+        for item in copies:
+            item.wait()
+        for z in range(planes_ref.shape[0]):
+            total = parts[0][z].astype(f32)
+            for k in range(peers):
+                total = total + landed[k, z].astype(f32)
+            planes_ref[z] = total.astype(bf16)
+
+
+def merge_kernel(count, ctx_ref, x_ref, vec_ref, w_ref, resid_ref, normed_ref):
     tensor, dp, part, width = w_ref.shape
     total = before(x_ref, count) + vec_ref[2:3]
     for t in range(tensor):
@@ -195,7 +231,17 @@
     normed_ref[...] = (hat * vec_ref[3:4] + vec_ref[4:5]).astype(bf16)
 
 
-def expand_kernel(normed_ref, grad_ref, bias_ref, w_ref, act_ref, slope_ref, out_ref):
+def expand_kernel(live_ref, normed_ref, given_ref, bias_ref, w_ref, act_ref, slope_ref, out_ref, grad_ref):
+    @pl.when(pl.program_id(0) == 0)
+    def _():
+        count = given_ref.shape[0]
+        even = count // 16 * 16
+        rows = lax.broadcasted_iota(jnp.int32, (count, 1), 0)
+        grad_ref[:even] = jnp.where(rows[:even] < live_ref[0], given_ref[:even], bf16(0))
+        grad_ref[even:] = jnp.zeros((grad_ref.shape[0] - even, grad_ref.shape[1]), bf16)
+        rest = jnp.where(rows[even:] < live_ref[0], given_ref[even:].astype(f32), 0.0)
+        grad_ref[even:count] = rest.astype(bf16)
+
     _, dp, part, width = w_ref.shape
     w = w_ref[0].reshape(dp * part, width)
     active, slope = gelu_and_slope(matmul(normed_ref[...], w) + bias_ref[...])
@@ -227,12 +273,13 @@
 
 
 def mlp_back_kernel(
-    chunk, grad_ref, slope_ref, resid_ref, vec_ref, e_ref, r_ref, m_ref,
+    chunk, live_ref, given_ref, slope_ref, resid_ref, vec_ref, e_ref, r_ref, m_ref,
     pre_ref, low_ref, ctx_ref, sums_ref, esum_ref,
 ):
     tensor, dp, rows, width = e_ref.shape
     first = pl.program_id(0) == 0
-    grad = grad_ref[...]
+    given = before(given_ref, live_ref[0])
+    grad = given.astype(bf16)
     total = jnp.zeros(grad.shape, f32)
     parts = []
     for t in range(tensor):
@@ -248,7 +295,7 @@
     sums = 0
     half = grad.shape[0] // 2
     for rows_half in (slice(0, half), slice(half, 2 * half)):
-        own = grad_ref[rows_half].astype(f32)
+        own = given[rows_half]
         back, gain_sum, shift_sum = norm_back(resid_ref[rows_half], vec_ref[3:4], total[rows_half])
         resid_grad = own + back
         low_ref[rows_half] = resid_grad.astype(bf16)
@@ -265,18 +312,14 @@
     accumulate(first, esum_ref, jnp.concatenate(lines, axis=0))
 
 
-def qkv_back_kernel(part, count, depth, x_ref, low_ref, vec_ref, grad_ref, w_ref, *refs):
-    reduce_ref, planes, refs = refs[0], refs[1 : depth + 1], refs[depth + 1 :]
-    out_ref, sums_ref, bsum_ref, expand_out_ref, merge_out_ref, reduce_out_ref = refs
+def qkv_back_kernel(part, count, x_ref, low_ref, vec_ref, grad_ref, w_ref, *refs):
+    reduce_ref, middle_ref, out_ref, sums_ref, bsum_ref, expand_out_ref, merge_out_ref, reduce_out_ref = refs
 
     @pl.when(pl.program_id(0) == 0)
     def _():
-        total = planes[0][...].astype(f32)
-        for ref in planes[1:]:
-            total = total + ref[...].astype(f32)
         hidden = expand_out_ref.shape[1]
-        expand_out_ref[...] = total[:, :hidden]
-        merge_out_ref[...] = total[:, hidden:]
+        expand_out_ref[...] = middle_ref[:, :hidden]
+        merge_out_ref[...] = middle_ref[:, hidden:]
         reduce_out_ref[...] = reduce_ref[...].astype(f32)
 
     tensor, dp = w_ref.shape[:2]
@@ -312,10 +355,14 @@
     return total
 
 
-def slot_grad_kernel(tensor, dp, starts, *refs):
+def slot_grad_kernel(tensor, dp, starts, carried, *refs):
     count, steps, depth = len(starts) - 1, starts[-1], dp // 4
-    lefts, rights, outs = refs[:count], refs[count : 2 * count], refs[2 * count : 2 * count + 2 * tensor]
-    total, keep, send, landed, send_sem, recv_sem = refs[2 * count + 2 * tensor :]
+    lefts, rights, refs = refs[:count], refs[count : 2 * count], refs[2 * count :]
+    if carried:
+        line_ref, *refs, arrived, line_send, line_recv = refs
+        sum_ref, refs = refs[0], refs[1:]
+    outs = refs[: 2 * tensor]
+    total, keep, send, landed, send_sem, recv_sem = refs[2 * tensor :]
     step, t = pl.program_id(0), pl.program_id(1)
     d, y = lax.axis_index("dp"), lax.axis_index("tensor")
     part, block = total.shape[0] // dp, total.shape[1]
@@ -333,13 +380,27 @@
             device_id_type=pl.DeviceIdType.MESH,
         )
 
+    def line(z):
+        return pltpu.make_async_remote_copy(
+            src_ref=line_ref.at[z],
+            dst_ref=arrived.at[z - 1],
+            send_sem=line_send.at[z - 1],
+            recv_sem=line_recv.at[z - 1],
+            device_id=(flip(d, 4 * z), y),
+            device_id_type=pl.DeviceIdType.MESH,
+        )
+
     @pl.when((step == 0) & (t == 0))
     def _():
         barrier = pltpu.get_barrier_semaphore()
-        pl.semaphore_signal(
-            barrier, inc=1, device_id=(flip(d, 1), y), device_id_type=pl.DeviceIdType.MESH
-        )
-        pl.semaphore_wait(barrier, 1)
+        masks = [1] + ([4 * z for z in range(1, depth)] if carried else [])
+        for mask in masks:
+            pl.semaphore_signal(
+                barrier, inc=1, device_id=(flip(d, mask), y), device_id_type=pl.DeviceIdType.MESH
+            )
+        pl.semaphore_wait(barrier, len(masks))
+        for z in range(1, depth) if carried else ():
+            line(z).start()
 
     for j in range(count):
         @pl.when((step >= starts[j]) & (step < starts[j + 1]))
@@ -367,8 +428,17 @@
                 both = keep[own, :, cols].astype(f32) + landed[own, :, cols].astype(f32)
                 outs[k][...] = both.astype(bf16)
 
-
-def slot_grads(name, pairs, tensor, dp, block, collective_id):
+    if carried:
+        @pl.when((step == steps) & (t == tensor - 1))
+        def _():
+            whole = line_ref[0].astype(f32)
+            for z in range(1, depth):
+                line(z).wait()
+                whole = whole + arrived[z - 1].astype(f32)
+            sum_ref[...] = whole
+
+
+def slot_grads(name, pairs, tensor, dp, block, collective_id, carried=()):
     rows, deep = pairs[0][0].shape
     part, depth = deep // dp, dp // 4
     block = min([block] + [right.shape[2] // tensor for _, right in pairs])
@@ -386,17 +456,20 @@
 
     spec = pl.BlockSpec((depth, part, block), lambda i, t: (0, 0, jnp.maximum(i - 1, 0)))
     return call(
-        functools.partial(slot_grad_kernel, tensor, dp, starts),
+        functools.partial(slot_grad_kernel, tensor, dp, starts, bool(carried)),
         name,
         (starts[-1] + 1, tensor),
         [full((rows, deep))] * len(pairs)
-        + [pl.BlockSpec((1, rows, block), functools.partial(right_map, j)) for j in range(len(pairs))],
-        [spec] * (2 * tensor),
-        [((depth, part, wide), bf16)] * (2 * tensor),
-        [left for left, _ in pairs] + [right for _, right in pairs],
+        + [pl.BlockSpec((1, rows, block), functools.partial(right_map, j)) for j in range(len(pairs))]
+        + [full(v.shape) for v in carried],
+        [pl.BlockSpec(v.shape[1:], lambda i, t: (0, 0)) for v in carried] + [spec] * (2 * tensor),
+        [(v.shape[1:], f32) for v in carried] + [((depth, part, wide), bf16)] * (2 * tensor),
+        [left for left, _ in pairs] + [right for _, right in pairs] + list(carried),
         [pltpu.VMEM((deep, block), f32)]
         + [pltpu.VMEM((half, part, wide), bf16)] * 3
-        + [pltpu.SemaphoreType.DMA((starts[-1] * tensor,))] * 2,
+        + [pltpu.SemaphoreType.DMA((starts[-1] * tensor,))] * 2
+        + [pltpu.VMEM((depth - 1,) + v.shape[1:], bf16) for v in carried]
+        + [pltpu.SemaphoreType.DMA((depth - 1,))] * (2 * len(carried)),
         collective_id=collective_id,
         has_side_effects=True,
     )
@@ -412,20 +485,6 @@
 
 def send_plane(parts, tensor, dp):
     return [swap(parts[k], 2 * (k % 2), k // 2, tensor, dp) for k in range(1, 2 * tensor)]
-
-
-def sum_plane(part, landed, dp):
-    planes = []
-    for z in range(dp // 4):
-        total = part[z].astype(f32)
-        for piece in landed:
-            total = total + piece[z].astype(f32)
-        planes.append(total.astype(bf16))
-    return planes
-
-
-def send_line(planes, tensor, dp):
-    return [swap(planes[z], 4 * z, 0, tensor, dp) for z in range(1, dp // 4)]
 
 
 def pack_kernel(
@@ -676,7 +735,8 @@
             heads_ref[s] = total[:, s * own : (s + 1) * own]
 
 
-def finish_kernel(sums_ref, heads_ref, out_ref, hb_ref, eb_ref, *vectors):
+def finish_kernel(sums_ref, heads_ref, given_ref, copy_ref, out_ref, hb_ref, eb_ref, *vectors):
+    copy_ref[...] = given_ref[...]
     out_ref[...] = heads_ref[...]
     part = vectors[0].shape[1]
     for r, ref in enumerate(vectors):
@@ -786,37 +846,38 @@
         flops=attend_flops,
     )
 
-    resid, normed_two, grad = call(
+    resid, normed_two = call(
         functools.partial(merge_kernel, rows),
         "merge",
         (blocks,),
-        [by_rows(deep), by_rows(deep), vec, merge_spec, by_rows(deep)],
-        [by_rows(deep), by_rows(deep), by_rows(deep)],
-        [((total_rows, deep), f32), ((total_rows, deep), bf16), ((total_rows, deep), bf16)],
-        (live, context, activations, vectors, wide, output_grad),
+        [by_rows(deep), by_rows(deep), vec, merge_spec],
+        [by_rows(deep), by_rows(deep)],
+        [((total_rows, deep), f32), ((total_rows, deep), bf16)],
+        (context, activations, vectors, wide),
         flops=total_rows * deep * deep,
-        prefetch=1,
     )
 
     chunk = min(512, hidden_own)
     per = hidden_own // chunk
-    chunk_spec = pl.BlockSpec((total_rows, chunk), lambda c: (0, c))
-    shard_spec = pl.BlockSpec((1, dp, part, chunk), lambda c: (c // per, 0, 0, c % per))
+    chunk_spec = pl.BlockSpec((total_rows, chunk), lambda c, *_: (0, c))
+    shard_spec = pl.BlockSpec((1, dp, part, chunk), lambda c, *_: (c // per, 0, 0, c % per))
     active, slope, grad_reduce = call(
         expand_kernel,
         "expand",
         (hidden // chunk,),
         [
-            full((total_rows, deep)), full((total_rows, deep)),
-            pl.BlockSpec((1, chunk), lambda c: (0, c)), shard_spec,
+            full((total_rows, deep)), full((rows, deep)),
+            pl.BlockSpec((1, chunk), lambda c, *_: (0, c)), shard_spec,
         ],
         [chunk_spec, chunk_spec, shard_spec],
         [
             ((total_rows, hidden), bf16), ((total_rows, hidden), bf16),
             ((tensor, dp, part, hidden_own), bf16),
         ],
-        (normed_two, grad, eb, wide),
+        (live, normed_two, output_grad, eb, wide),
+        [pltpu.VMEM((total_rows, deep), bf16)],
         flops=total_rows * deep * hidden * 2,
+        prefetch=1,
     )
     grad_reduce = grad_reduce.reshape(tensor * dp * part, hidden_own)
     grad_reduce = lax.psum_scatter(grad_reduce, AXES, scatter_dimension=0, tiled=True)
@@ -832,49 +893,53 @@
         ],
         [
             by_rows(hidden), by_rows(deep), by_rows(deep),
-            pl.BlockSpec((4, deep), lambda i: (0, 0)), pl.BlockSpec((hidden // 128, 128), lambda i: (0, 0)),
+            pl.BlockSpec((4, deep), lambda *_: (0, 0)), pl.BlockSpec((hidden // 128, 128), lambda *_: (0, 0)),
         ],
         [
             ((total_rows, hidden), bf16), ((total_rows, deep), bf16), ((total_rows, deep), bf16),
             ((4, deep), f32), ((hidden // 128, 128), f32),
         ],
-        (grad, slope, resid, vectors, wide, wide_reduce, wide),
+        (live, output_grad, slope, resid, vectors, wide, wide_reduce, wide),
+        prefetch=1,
     )
     parts = slot_grads(
         "middle_grad", [(normed_two, pre_grad[None]), (resid_low, context[None])], tensor, dp, 512, 2
     )
-    *parts, grad_context = lax.optimization_barrier((*parts, grad_context))
-    landed = send_plane(parts, tensor, dp)
-    grad_triple = call(
-        attend_back_kernel,
+    peers = 2 * tensor - 1
+    shape = parts[0].shape
+    grad_triple, planes = call(
+        functools.partial(attend_back_kernel, tensor),
         "attend_back",
         (groups, images),
-        [head_spec, stat_spec, ctx_spec],
-        [head_spec],
-        [((3, total_rows, deep), bf16)],
-        (triple, stat, grad_context),
-    )[0]
-    *landed, part_own, grad_triple = lax.optimization_barrier((*landed, parts[0], grad_triple))
-    planes = sum_plane(part_own, landed, dp)
-    *planes, grad_triple = lax.optimization_barrier((*planes, grad_triple))
-    landed = send_line(planes, tensor, dp)
-    parts = slot_grads("heads_grad", [(normed_one, grad_triple)], tensor, dp, 512, 3)
-    held = (tuple(parts), tuple(landed), planes[0], resid_low)
-    parts, landed, plane_own, resid_low = lax.optimization_barrier(held)
+        [head_spec, stat_spec, ctx_spec] + [full(shape)] * (peers + 1),
+        [head_spec, pl.BlockSpec(shape, lambda g, i: (0, 0, 0))],
+        [((3, total_rows, deep), bf16), (shape, bf16)],
+        (triple, stat, grad_context, *parts),
+        [
+            pltpu.VMEM((peers,) + shape, bf16),
+            pltpu.SemaphoreType.DMA((peers,)), pltpu.SemaphoreType.DMA((peers,)),
+        ],
+        collective_id=4,
+        has_side_effects=True,
+    )
+    middle, *parts = slot_grads(
+        "heads_grad", [(normed_one, grad_triple)], tensor, dp, 512, 3, (planes,)
+    )
+    *parts, resid_low = lax.optimization_barrier((*parts, resid_low))
     last = send_plane(parts, tensor, dp)
     def whole(shape):
         return pl.BlockSpec(shape, lambda *_: (0,) * len(shape))
 
     shapes = [(2, deep), (2, deep), (part, hidden_own), (part, own), (part, hidden_own)]
     input_grad, sums_one, bsum, grad_expand, grad_merge, grad_reduce = call(
-        functools.partial(qkv_back_kernel, part, rows, dp // 4),
+        functools.partial(qkv_back_kernel, part, rows),
         "qkv_back",
         (blocks,),
         [by_rows(deep), by_rows(deep), vec, triple_spec, full(wide_heads.shape), full(grad_reduce.shape)]
-        + [full(plane_own.shape)] * (dp // 4),
+        + [full(middle.shape)],
         [by_rows(deep)] + [whole(shape) for shape in shapes],
         [((rows, deep), bf16)] + [(shape, f32) for shape in shapes],
-        (activations, resid_low, vectors, grad_triple, wide_heads, grad_reduce, plane_own, *landed),
+        (activations, resid_low, vectors, grad_triple, wide_heads, grad_reduce, middle),
         flops=total_rows * deep * deep * 3,
     )
 
@@ -899,10 +964,15 @@
         collective_id=0,
         has_side_effects=True,
     )
-    grad_heads, hb_grad, eb_grad, *vector = call(
-        finish_kernel, "finish", (), [vmem] * 2, [vmem] * 9,
-        [(heads_sum.shape, f32), ((2, hbs[2], hbs[1]), f32), (ebs[::-1], f32)] + [((1, part), f32)] * 6,
-        (sums, heads_sum),
+    shapes = [heads_sum.shape, (2, hbs[2], hbs[1]), ebs[::-1]] + [(1, part)] * 6
+    output, grad_heads, hb_grad, eb_grad, *vector = call(
+        finish_kernel,
+        "finish",
+        (blocks,),
+        [full(sums.shape), full(heads_sum.shape), by_rows(deep)],
+        [by_rows(deep)] + [whole(shape) for shape in shapes],
+        [((rows, deep), bf16)] + [(shape, f32) for shape in shapes],
+        (sums, heads_sum, output),
     )
     vector = [v.reshape(part) for v in vector]
 

time: 522 us -> 523 us (level)
  Pallas kernels: 462 us -> 487 us
  starting transfers between devices: 14.1 us -> 4.01 us
    pallas_call x13, Pallas kernels: 462 us -> 487 us  [call(): pl.pallas_call(kernel, grid_spec=pltpu.PrefetchScalarGridSpec(num_scalar_...]
    ppermute x9 -> x3, starting transfers between devices: 14 us -> 3.89 us  [swap(): return lax.ppermute(values, ('dp', 'tensor'), moves)]
  transfers between devices with their start and end apart: 12 -> 6, of which waited for: 2 -> 1; matrix products, arithmetic and copies ran while one was open for 1% -> 1% of each run, Pallas kernels for 84% -> 86%
where the time goes in v6:
time: 523 us; the launch traced here: 516 us
  Pallas kernels  487 us (93%)
  between operations  15 us (3%)
  waiting for transfers between devices  5.48 us (1%)
    pallas_call x13, Pallas kernels, call(): pl.pallas_call(kernel, grid_spec=pltpu.PrefetchScalarGridSpec(num_scalar_...  487 us
  transfers between devices with their start and end apart: 6, of which 1 were waited for; matrix products, arithmetic and copies ran while one was open for 1% of the time, Pallas kernels for 86%

profile of v6, /device:TPU:0, one launch (start us, length us, event | category | flops | bytes accessed | tf_op | source)
XLA Modules:
  0.0 516.2 jit_solution(13837394473065235599)
XLA Ops:
  7.2 2.0 pack.1
  9.3 52.6 %gather.1.w_ref = bf16[2,16,72,1536]{3,2,1,0:T(8,128)(2,1)} custom-call(bf16[72,1536]{1,0:T(8,128)(2,1)} %get-tuple-element.67.in_ref), custom_call_target="tpu_custom_call" | custom-call | tf_op jit(solution)/shard_map/gather/pallas_call | solution.py:52
  62.6 0.9 slice_convert_fusion
  63.6 0.7 reshape.91.vec_ref
  64.3 0.5 copy.33
  64.7 0.8 reshape.93.bias_ref
  65.8 0.8 reshape.95.bias_ref
  66.5 22.8 %qkv.1 = (bf16[2320,1024]{1,0:T(8,128)(2,1)}, bf16[3,2320,1024]{2,1,0:T(8,128)(2,1)}) custom-call(bf16[2308,1024]{1,0:T(8,128)(2,1)} %x_ref.5, f32[6,1024]{1,0:T(8,128)} %reshape.91.vec_ref, f32[2,1024]{1,0:T(2,128)} %reshape.93.bias_ref, bf16[2,16,72,1536]{3,2,1,0:T(8,128)(2,1)} %gather.1.w_ref), custom_call_target="tpu_custom_call" | custom-call | flops 14596177920 | bytes 30842880 | tf_op jit(solution)/shard_map/qkv/pallas_call | solution.py:52
  89.4 43.9 %attend.1 = (bf16[2320,1024]{1,0:T(8,128)(2,1)}, f32[16,4,592]{2,1,0:T(4,128)}) custom-call(bf16[3,2320,1024]{2,1,0:T(8,128)(2,1)} %get-tuple-element.69.triple_ref), custom_call_target="tpu_custom_call" | custom-call | flops 29796335616 | bytes 19156992 | tf_op jit(solution)/shard_map/attend/pallas_call | solution.py:52
  133.3 12.6 %merge.1 = (f32[2320,1024]{1,0:T(8,128)}, bf16[2320,1024]{1,0:T(8,128)(2,1)}) custom-call(bf16[2320,1024]{1,0:T(8,128)(2,1)} %get-tuple-element.70.ctx_ref, bf16[2308,1024]{1,0:T(8,128)(2,1)} %x_ref.5, f32[6,1024]{1,0:T(8,128)} %reshape.91.vec_ref, bf16[2,16,64,2560]{3,2,1,0:T(8,128)(2,1)} %bitcast.38), custom_call_target="tpu_custom_call" | custom-call | flops 4865392640 | bytes 34242560 | tf_op jit(solution)/shard_map/merge/pallas_call | solution.py:52
  145.9 56.1 %expand.1 = (bf16[2320,4096]{1,0:T(8,128)(2,1)}, bf16[2320,4096]{1,0:T(8,128)(2,1)}, bf16[2,16,64,2048]{3,2,1,0:T(8,128)(2,1)}) custom-call(s32[1]{0:T(128)S(6)} %mul.7.live_ref, bf16[2320,1024]{1,0:T(8,128)(2,1)} %get-tuple-element.72.normed_ref.refs_0_, bf16[2308,1024]{1,0:T(8,128)(2,1)} %given_ref.3, f32[1,4096]{1,0:T(1,128)} %reshape.95.bias_ref, ...), custom_call_target="tpu_custom_call" | custom-call | flops 38923141120 | bytes 66379780 | tf_op jit(solution)/shard_map/expand/pallas_call | solution.py:52
  202.0 64.8 %mlp_back.1 = (bf16[2320,4096]{1,0:T(8,128)(2,1)}, bf16[2320,1024]{1,0:T(8,128)(2,1)}, bf16[2320,1024]{1,0:T(8,128)(2,1)}, f32[4,1024]{1,0:T(4,128)}, f32[32,128]{1,0:T(8,128)}) custom-call(s32[1]{0:T(128)S(6)} %mul.7.live_ref, bf16[2308,1024]{1,0:T(8,128)(2,1)} %given_ref.3, bf16[2320,4096]{1,0:T(8,128)(2,1)} %get-tuple-element.78.slope_ref, ...), custom_call_target="tpu_custom_call" | custom-call | tf_op jit(solution)/shard_map/mlp_back/pallas_call | solution.py:52
  266.9 41.1 %middle_grad.1 = (bf16[4,64,2560]{2,1,0:T(8,128)(2,1)}, bf16[4,64,2560]{2,1,0:T(8,128)(2,1)}, bf16[4,64,2560]{2,1,0:T(8,128)(2,1)}, bf16[4,64,2560]{2,1,0:T(8,128)(2,1)}) custom-call(bf16[2320,1024]{1,0:T(8,128)(2,1)} %get-tuple-element.72.normed_ref.refs_0_, bf16[2320,1024]{1,0:T(8,128)(2,1)} %get-tuple-element.96.refs_1_.low_ref, ...), custom_call_target="tpu_custom_call" | custom-call | tf_op jit(solution)/shard_map/middle_grad/pallas_call | solution.py:52
  307.9 89.3 %attend_back.1 = (bf16[3,2320,1024]{2,1,0:T(8,128)(2,1)}, bf16[4,64,2560]{2,1,0:T(8,128)(2,1)}) custom-call(bf16[3,2320,1024]{2,1,0:T(8,128)(2,1)} %get-tuple-element.69.triple_ref, f32[16,4,592]{2,1,0:T(4,128)} %get-tuple-element.77.stat_ref, bf16[2320,1024]{1,0:T(8,128)(2,1)} %get-tuple-element.79.grad_ref, ...), custom_call_target="tpu_custom_call" | custom-call | tf_op jit(solution)/shard_map/attend_back/pallas_call | solution.py:52
  397.2 30.8 %heads_grad.1 = (f32[64,2560]{1,0:T(8,128)}, bf16[4,64,1536]{2,1,0:T(8,128)(2,1)}, bf16[4,64,1536]{2,1,0:T(8,128)(2,1)}, bf16[4,64,1536]{2,1,0:T(8,128)(2,1)}, bf16[4,64,1536]{2,1,0:T(8,128)(2,1)}) custom-call(bf16[2320,1024]{1,0:T(8,128)(2,1)} %get-tuple-element.76.refs_0_, bf16[3,2320,1024]{2,1,0:T(8,128)(2,1)} %get-tuple-element.86.refs_1_.grad_ref, ...), custom_call_target="tpu_custom_call" | custom-call | tf_op jit(solution)/shard_map/heads_grad/pallas_call | solution.py:52
  428.0 2.4 collective-permute-start
  430.4 0.7 collective-permute-start.1
  431.0 0.9 collective-permute-start.2
  431.9 28.4 %qkv_back.1 = (bf16[2308,1024]{1,0:T(8,128)(2,1)}, f32[2,1024]{1,0:T(2,128)}, f32[2,1024]{1,0:T(2,128)}, f32[64,2048]{1,0:T(8,128)}, f32[64,512]{1,0:T(8,128)}, /*index=5*/f32[64,2048]{1,0:T(8,128)}) custom-call(bf16[2308,1024]{1,0:T(8,128)(2,1)} %x_ref.5, bf16[2320,1024]{1,0:T(8,128)(2,1)} %get-tuple-element.96.refs_1_.low_ref, f32[6,1024]{1,0:T(8,128)} %reshape.91.vec_ref, ...), custom_call_target="tpu_custom_call" | custom-call | flops 14596177920 | bytes 37675008 | tf_op jit(solution)/shard_map/qkv_back/pallas_call | solution.py:52
  460.3 5.4 %collective-permute-done.1.refs_2_ = bf16[4,64,1536]{2,1,0:T(8,128)(2,1)S(1)} collective-permute-done((bf16[4,64,1536]{2,1,0:T(8,128)(2,1)}, bf16[4,64,1536]{2,1,0:T(8,128)(2,1)S(1)}, u32[]{:S(2)}, u32[]{:S(2)}) %collective-permute-start.1) | collective-permute-done | bytes 786464 | tf_op jit(solution)/shard_map/ppermute | solution.py:483
  465.7 0.9 copy-done.1
  466.6 0.4 copy-done.2
  467.0 35.6 %reduce.1 = (bf16[2308,1024]{1,0:T(8,128)(2,1)}, f32[3,64,512]{2,1,0:T(8,128)}, f32[8,128]{1,0:T(8,128)}) custom-call(bf16[2320,4096]{1,0:T(8,128)(2,1)} %get-tuple-element.73.act_ref, f32[2320,1024]{1,0:T(8,128)} %get-tuple-element.74.resid_ref, f32[6,1024]{1,0:T(8,128)} %reshape.91.vec_ref, bf16[2,16,64,2048]{3,2,1,0:T(8,128)(2,1)} %bitcast.45, ...), custom_call_target="tpu_custom_call" | custom-call | flops 19461570560 | bytes 45240320 | tf_op jit(solution)/shard_map/reduce/pallas_call | solution.py:52
  502.6 6.6 %finish.1 = (bf16[2308,1024]{1,0:T(8,128)(2,1)}, f32[3,64,512]{2,1,0:T(8,128)}, f32[2,4,8]{2,1,0:T(4,128)}, f32[8,16]{1,0:T(8,128)}, f32[1,64]{1,0:T(1,128)}, /*...) custom-call(f32[8,128]{1,0:T(8,128)} %get-tuple-element.103.sums_ref, ...), custom_call_target="tpu_custom_call" | custom-call | tf_op jit(solution)/shard_map/finish/pallas_call | solution.py:52
  (20 shorter events, 0.6 us)
Async XLA Ops:
  7.2 126.1 %all-gather.3.cloned.1.call-start = ((), (), s32[]{:S(2)}) async-start(), calls=%async_computation.1 | async-start | bytes 10813440 | tf_op jit(solution)/shard_map/all_gather | solution.py:784
  9.2 192.8 %all-gather.5.cloned.1.call-start = ((), (), s32[]{:S(2)}) async-start(), calls=%async_computation.2 | async-start | bytes 8650752 | tf_op jit(solution)/shard_map/all_gather | solution.py:784
  61.9 370.0 %reduce-scatter.2.cloned.1.call-start = ((), (), s32[]{:S(2)}) async-start(), calls=%async_computation.3 | async-start | bytes 8650752 | tf_op jit(solution)/shard_map/reduce_scatter | solution.py:883
  428.0 32.3 %collective-permute-start = (bf16[4,64,1536]{2,1,0:T(8,128)(2,1)}, bf16[4,64,1536]{2,1,0:T(8,128)(2,1)S(1)}, u32[]{:S(2)}, u32[]{:S(2)}) collective-permute-start(bf16[4,64,1536]{2,1,0:T(8,128)(2,1)} %get-tuple-element.93), channel_id=1, source_target_pairs={{0,4},{1,5},{2,6},{3,7},{4,0},{5,1},{6,2},{7,3},{8,12},{9,13},{10,... | collective-permute-start | bytes 2359304 | tf_op jit(solution)/shard_map/ppermute | solution.py:483
  430.4 35.3 %collective-permute-start.1 = (bf16[4,64,1536]{2,1,0:T(8,128)(2,1)}, bf16[4,64,1536]{2,1,0:T(8,128)(2,1)S(1)}, u32[]{:S(2)}, u32[]{:S(2)}) collective-permute-start(bf16[4,64,1536]{2,1,0:T(8,128)(2,1)} %get-tuple-element.94), channel_id=1, source_target_pairs={{0,1},{1,0},{2,3},{3,2},{4,5},{5,4},{6,7},{7,6},{8,9},{9,8},{10,11... | collective-permute-start | bytes 2359304 | tf_op jit(solution)/shard_map/ppermute | solution.py:483
  431.0 34.7 %collective-permute-start.2 = (bf16[4,64,1536]{2,1,0:T(8,128)(2,1)}, bf16[4,64,1536]{2,1,0:T(8,128)(2,1)S(1)}, u32[]{:S(2)}, u32[]{:S(2)}) collective-permute-start(bf16[4,64,1536]{2,1,0:T(8,128)(2,1)} %get-tuple-element.95), channel_id=1, source_target_pairs={{0,5},{1,4},{2,7},{3,6},{4,1},{5,0},{6,3},{7,2},{8,13},{9,12},{10,... | collective-permute-start | bytes 2359304 | tf_op jit(solution)/shard_map/ppermute | solution.py:483
  460.3 5.4 %copy-start = (bf16[4,64,1536]{2,1,0:T(8,128)(2,1)}, bf16[4,64,1536]{2,1,0:T(8,128)(2,1)S(1)}, u32[]{:S(2)}) copy-start(bf16[4,64,1536]{2,1,0:T(8,128)(2,1)S(1)} %collective-permute-done.refs_1_) | copy-start | bytes 2359300
  465.7 0.9 copy-start.1
  465.7 1.2 copy-start.2
Sparse Core Ops, SparseCore 0:
  11.5 98.5 all-gather.2
  113.0 75.9 all-gather.4
  202.1 153.6 reduce-scatter.1

commit v7 on v5

--- a/solution.py
+++ b/solution.py
@@ -183,8 +183,7 @@
         keep_before(image, out_ref, (0, pair), query_grad * LOG_SCALE)
 
 
-def merge_kernel(count, live_ref, ctx_ref, x_ref, vec_ref, w_ref, given_ref, resid_ref, normed_ref, grad_ref):
-    grad_ref[...] = before(given_ref, live_ref[0]).astype(bf16)
+def merge_kernel(count, ctx_ref, x_ref, vec_ref, w_ref, resid_ref, normed_ref):
     tensor, dp, part, width = w_ref.shape
     total = before(x_ref, count) + vec_ref[2:3]
     for t in range(tensor):
@@ -195,7 +194,17 @@
     normed_ref[...] = (hat * vec_ref[3:4] + vec_ref[4:5]).astype(bf16)
 
 
-def expand_kernel(normed_ref, grad_ref, bias_ref, w_ref, act_ref, slope_ref, out_ref):
+def expand_kernel(live_ref, normed_ref, given_ref, bias_ref, w_ref, act_ref, slope_ref, out_ref, grad_ref):
+    @pl.when(pl.program_id(0) == 0)
+    def _():
+        count = given_ref.shape[0]
+        even = count // 16 * 16
+        rows = lax.broadcasted_iota(jnp.int32, (count, 1), 0)
+        grad_ref[:even] = jnp.where(rows[:even] < live_ref[0], given_ref[:even], bf16(0))
+        grad_ref[even:] = jnp.zeros((grad_ref.shape[0] - even, grad_ref.shape[1]), bf16)
+        rest = jnp.where(rows[even:] < live_ref[0], given_ref[even:].astype(f32), 0.0)
+        grad_ref[even:count] = rest.astype(bf16)
+
     _, dp, part, width = w_ref.shape
     w = w_ref[0].reshape(dp * part, width)
     active, slope = gelu_and_slope(matmul(normed_ref[...], w) + bias_ref[...])
@@ -227,12 +236,13 @@
 
 
 def mlp_back_kernel(
-    chunk, grad_ref, slope_ref, resid_ref, vec_ref, e_ref, r_ref, m_ref,
+    chunk, live_ref, given_ref, slope_ref, resid_ref, vec_ref, e_ref, r_ref, m_ref,
     pre_ref, low_ref, ctx_ref, sums_ref, esum_ref,
 ):
     tensor, dp, rows, width = e_ref.shape
     first = pl.program_id(0) == 0
-    grad = grad_ref[...]
+    given = before(given_ref, live_ref[0])
+    grad = given.astype(bf16)
     total = jnp.zeros(grad.shape, f32)
     parts = []
     for t in range(tensor):
@@ -248,7 +258,7 @@
     sums = 0
     half = grad.shape[0] // 2
     for rows_half in (slice(0, half), slice(half, 2 * half)):
-        own = grad_ref[rows_half].astype(f32)
+        own = given[rows_half]
         back, gain_sum, shift_sum = norm_back(resid_ref[rows_half], vec_ref[3:4], total[rows_half])
         resid_grad = own + back
         low_ref[rows_half] = resid_grad.astype(bf16)
@@ -265,20 +275,8 @@
     accumulate(first, esum_ref, jnp.concatenate(lines, axis=0))
 
 
-def qkv_back_kernel(part, count, depth, x_ref, low_ref, vec_ref, grad_ref, w_ref, *refs):
-    reduce_ref, planes, refs = refs[0], refs[1 : depth + 1], refs[depth + 1 :]
-    out_ref, sums_ref, bsum_ref, expand_out_ref, merge_out_ref, reduce_out_ref = refs
-
-    @pl.when(pl.program_id(0) == 0)
-    def _():
-        total = planes[0][...].astype(f32)
-        for ref in planes[1:]:
-            total = total + ref[...].astype(f32)
-        hidden = expand_out_ref.shape[1]
-        expand_out_ref[...] = total[:, :hidden]
-        merge_out_ref[...] = total[:, hidden:]
-        reduce_out_ref[...] = reduce_ref[...].astype(f32)
-
+def qkv_back_kernel(part, count, x_ref, low_ref, vec_ref, grad_ref, w_ref, *refs):
+    out_ref, sums_ref, bsum_ref = refs
     tensor, dp = w_ref.shape[:2]
     width = w_ref.shape[3] // 3
     first = pl.program_id(0) == 0
@@ -676,7 +674,23 @@
             heads_ref[s] = total[:, s * own : (s + 1) * own]
 
 
-def finish_kernel(sums_ref, heads_ref, out_ref, hb_ref, eb_ref, *vectors):
+def finish_kernel(depth, given_ref, sums_ref, heads_ref, reduced_ref, *refs):
+    planes, (copy_ref, reduce_ref, expand_ref, merge_ref, out_ref, hb_ref, eb_ref) = refs[:depth], refs[depth : depth + 7]
+    vectors, sem = refs[depth + 7 : -1], refs[-1]
+    copies = []
+    for k in range(sem.shape[0]):
+        width = given_ref.shape[1] // sem.shape[0]
+        cols = pl.ds(k * width, width)
+        copies.append(pltpu.make_async_copy(given_ref.at[:, cols], copy_ref.at[:, cols], sem.at[k]))
+    for item in copies:
+        item.start()
+    total = planes[0][...].astype(f32)
+    for ref in planes[1:]:
+        total = total + ref[...].astype(f32)
+    hidden = expand_ref.shape[1]
+    expand_ref[...] = total[:, :hidden]
+    merge_ref[...] = total[:, hidden:]
+    reduce_ref[...] = reduced_ref[...].astype(f32)
     out_ref[...] = heads_ref[...]
     part = vectors[0].shape[1]
     for r, ref in enumerate(vectors):
@@ -687,6 +701,8 @@
     for k in range(2):
         lane = part + tall + k * count
         hb_ref[k] = sums_ref[:wide, lane : lane + count]
+    for item in copies:
+        item.wait()
 
 
 def shards(
@@ -786,37 +802,38 @@
         flops=attend_flops,
     )
 
-    resid, normed_two, grad = call(
+    resid, normed_two = call(
         functools.partial(merge_kernel, rows),
         "merge",
         (blocks,),
-        [by_rows(deep), by_rows(deep), vec, merge_spec, by_rows(deep)],
-        [by_rows(deep), by_rows(deep), by_rows(deep)],
-        [((total_rows, deep), f32), ((total_rows, deep), bf16), ((total_rows, deep), bf16)],
-        (live, context, activations, vectors, wide, output_grad),
+        [by_rows(deep), by_rows(deep), vec, merge_spec],
+        [by_rows(deep), by_rows(deep)],
+        [((total_rows, deep), f32), ((total_rows, deep), bf16)],
+        (context, activations, vectors, wide),
         flops=total_rows * deep * deep,
-        prefetch=1,
     )
 
     chunk = min(512, hidden_own)
     per = hidden_own // chunk
-    chunk_spec = pl.BlockSpec((total_rows, chunk), lambda c: (0, c))
-    shard_spec = pl.BlockSpec((1, dp, part, chunk), lambda c: (c // per, 0, 0, c % per))
+    chunk_spec = pl.BlockSpec((total_rows, chunk), lambda c, *_: (0, c))
+    shard_spec = pl.BlockSpec((1, dp, part, chunk), lambda c, *_: (c // per, 0, 0, c % per))
     active, slope, grad_reduce = call(
         expand_kernel,
         "expand",
         (hidden // chunk,),
         [
-            full((total_rows, deep)), full((total_rows, deep)),
-            pl.BlockSpec((1, chunk), lambda c: (0, c)), shard_spec,
+            full((total_rows, deep)), full((rows, deep)),
+            pl.BlockSpec((1, chunk), lambda c, *_: (0, c)), shard_spec,
         ],
         [chunk_spec, chunk_spec, shard_spec],
         [
             ((total_rows, hidden), bf16), ((total_rows, hidden), bf16),
             ((tensor, dp, part, hidden_own), bf16),
         ],
-        (normed_two, grad, eb, wide),
+        (live, normed_two, output_grad, eb, wide),
+        [pltpu.VMEM((total_rows, deep), bf16)],
         flops=total_rows * deep * hidden * 2,
+        prefetch=1,
     )
     grad_reduce = grad_reduce.reshape(tensor * dp * part, hidden_own)
     grad_reduce = lax.psum_scatter(grad_reduce, AXES, scatter_dimension=0, tiled=True)
@@ -832,13 +849,14 @@
         ],
         [
             by_rows(hidden), by_rows(deep), by_rows(deep),
-            pl.BlockSpec((4, deep), lambda i: (0, 0)), pl.BlockSpec((hidden // 128, 128), lambda i: (0, 0)),
+            pl.BlockSpec((4, deep), lambda *_: (0, 0)), pl.BlockSpec((hidden // 128, 128), lambda *_: (0, 0)),
         ],
         [
             ((total_rows, hidden), bf16), ((total_rows, deep), bf16), ((total_rows, deep), bf16),
             ((4, deep), f32), ((hidden // 128, 128), f32),
         ],
-        (grad, slope, resid, vectors, wide, wide_reduce, wide),
+        (live, output_grad, slope, resid, vectors, wide, wide_reduce, wide),
+        prefetch=1,
     )
     parts = slot_grads(
         "middle_grad", [(normed_two, pre_grad[None]), (resid_low, context[None])], tensor, dp, 512, 2
@@ -854,33 +872,32 @@
         [((3, total_rows, deep), bf16)],
         (triple, stat, grad_context),
     )[0]
-    *landed, part_own, grad_triple = lax.optimization_barrier((*landed, parts[0], grad_triple))
+    heads = slot_grads("heads_grad", [(normed_one, grad_triple)], tensor, dp, 512, 3)
+    held = (tuple(heads), tuple(landed), parts[0], resid_low)
+    heads, landed, part_own, resid_low = lax.optimization_barrier(held)
+    last = send_plane(heads, tensor, dp)
     planes = sum_plane(part_own, landed, dp)
-    *planes, grad_triple = lax.optimization_barrier((*planes, grad_triple))
-    landed = send_line(planes, tensor, dp)
-    parts = slot_grads("heads_grad", [(normed_one, grad_triple)], tensor, dp, 512, 3)
-    held = (tuple(parts), tuple(landed), planes[0], resid_low)
-    parts, landed, plane_own, resid_low = lax.optimization_barrier(held)
-    last = send_plane(parts, tensor, dp)
+    planes, resid_low = lax.optimization_barrier((tuple(planes), resid_low))
+    line = send_line(planes, tensor, dp)
+
     def whole(shape):
         return pl.BlockSpec(shape, lambda *_: (0,) * len(shape))
 
-    shapes = [(2, deep), (2, deep), (part, hidden_own), (part, own), (part, hidden_own)]
-    input_grad, sums_one, bsum, grad_expand, grad_merge, grad_reduce = call(
-        functools.partial(qkv_back_kernel, part, rows, dp // 4),
+    shapes = [(2, deep), (2, deep)]
+    input_grad, sums_one, bsum = call(
+        functools.partial(qkv_back_kernel, part, rows),
         "qkv_back",
         (blocks,),
-        [by_rows(deep), by_rows(deep), vec, triple_spec, full(wide_heads.shape), full(grad_reduce.shape)]
-        + [full(plane_own.shape)] * (dp // 4),
+        [by_rows(deep), by_rows(deep), vec, triple_spec, full(wide_heads.shape)],
         [by_rows(deep)] + [whole(shape) for shape in shapes],
         [((rows, deep), bf16)] + [(shape, f32) for shape in shapes],
-        (activations, resid_low, vectors, grad_triple, wide_heads, grad_reduce, plane_own, *landed),
+        (activations, resid_low, vectors, grad_triple, wide_heads),
         flops=total_rows * deep * deep * 3,
     )
 
     hbs, ebs = heads_bias.shape, expand_bias.shape
     depth = dp // 4
-    arrays = [parts[0], *last, sums_one, sums_two, bsum, esum]
+    arrays = [heads[0], *last, sums_one, sums_two, bsum, esum]
     output, heads_sum, sums = call(
         functools.partial(last_kernel, dp, tensor),
         "reduce",
@@ -899,10 +916,19 @@
         collective_id=0,
         has_side_effects=True,
     )
-    grad_heads, hb_grad, eb_grad, *vector = call(
-        finish_kernel, "finish", (), [vmem] * 2, [vmem] * 9,
-        [(heads_sum.shape, f32), ((2, hbs[2], hbs[1]), f32), (ebs[::-1], f32)] + [((1, part), f32)] * 6,
-        (sums, heads_sum),
+    shapes = [(part, hidden_own), (part, hidden_own), (part, own)]
+    shapes += [heads_sum.shape, (2, hbs[2], hbs[1]), ebs[::-1]] + [(1, part)] * 6
+    hbm = pl.BlockSpec(memory_space=pl.ANY)
+    arrays = [output, sums, heads_sum, grad_reduce, planes[0], *line]
+    output, grad_reduce, grad_expand, grad_merge, grad_heads, hb_grad, eb_grad, *vector = call(
+        functools.partial(finish_kernel, depth),
+        "finish",
+        (),
+        [hbm] + [vmem] * (len(arrays) - 1),
+        [hbm] + [vmem] * len(shapes),
+        [((rows, deep), bf16)] + [(shape, f32) for shape in shapes],
+        arrays,
+        [pltpu.SemaphoreType.DMA((4,))],
     )
     vector = [v.reshape(part) for v in vector]
 

time: 522 us -> 649 us (1.24)
  Pallas kernels: 462 us -> 605 us
  waiting for transfers between devices: 7.37 us -> 0.12 us
    pallas_call x13, Pallas kernels: 462 us -> 605 us  [call(): pl.pallas_call(kernel, grid_spec=pltpu.PrefetchScalarGridSpec(num_scalar_...]
    ppermute x9, waiting for transfers between devices: 7.29 us -> 0.02 us  [swap(): return lax.ppermute(values, ('dp', 'tensor'), moves)]
  transfers between devices with their start and end apart: 12 -> 12, of which waited for: 2 -> 0; matrix products, arithmetic and copies ran while one was open for 1% -> 1% of each run, Pallas kernels for 84% -> 71%
where the time goes in v7:
time: 649 us; the launch traced here: 642 us
  Pallas kernels  605 us (93%)
  between operations  15.1 us (2%)
  starting transfers between devices  14.4 us (2%)
    pallas_call x13, Pallas kernels, call(): pl.pallas_call(kernel, grid_spec=pltpu.PrefetchScalarGridSpec(num_scalar_...  605 us
    ppermute x9, starting transfers between devices, swap(): return lax.ppermute(values, ('dp', 'tensor'), moves)  14.3 us
  transfers between devices with their start and end apart: 12, of which 0 were waited for; matrix products, arithmetic and copies ran while one was open for 1% of the time, Pallas kernels for 71%

profile of v7, /device:TPU:0, one launch (start us, length us, event | category | flops | bytes accessed | tf_op | source)
XLA Modules:
  0.0 642.3 jit_solution(450066189711883054)
XLA Ops:
  7.2 2.0 pack.1
  9.3 52.6 %gather.1.w_ref = bf16[2,16,72,1536]{3,2,1,0:T(8,128)(2,1)} custom-call(bf16[72,1536]{1,0:T(8,128)(2,1)} %get-tuple-element.78.in_ref), custom_call_target="tpu_custom_call" | custom-call | tf_op jit(solution)/shard_map/gather/pallas_call | solution.py:52
  62.6 0.9 slice_convert_fusion
  63.6 0.7 reshape.123.vec_ref
  64.7 0.8 reshape.125.bias_ref
  65.8 0.8 reshape.127.bias_ref
  66.5 22.9 %qkv.1 = (bf16[2320,1024]{1,0:T(8,128)(2,1)}, bf16[3,2320,1024]{2,1,0:T(8,128)(2,1)}) custom-call(bf16[2308,1024]{1,0:T(8,128)(2,1)} %x_ref.5, f32[6,1024]{1,0:T(8,128)} %reshape.123.vec_ref, f32[2,1024]{1,0:T(2,128)} %reshape.125.bias_ref, bf16[2,16,72,1536]{3,2,1,0:T(8,128)(2,1)} %gather.1.w_ref), custom_call_target="tpu_custom_call" | custom-call | flops 14596177920 | bytes 30842880 | tf_op jit(solution)/shard_map/qkv/pallas_call | solution.py:52
  89.4 43.9 %attend.1 = (bf16[2320,1024]{1,0:T(8,128)(2,1)}, f32[16,4,592]{2,1,0:T(4,128)}) custom-call(bf16[3,2320,1024]{2,1,0:T(8,128)(2,1)} %get-tuple-element.80.triple_ref), custom_call_target="tpu_custom_call" | custom-call | flops 29796335616 | bytes 19156992 | tf_op jit(solution)/shard_map/attend/pallas_call | solution.py:52
  133.3 12.6 %merge.1 = (f32[2320,1024]{1,0:T(8,128)}, bf16[2320,1024]{1,0:T(8,128)(2,1)}) custom-call(bf16[2320,1024]{1,0:T(8,128)(2,1)} %get-tuple-element.81.ctx_ref, bf16[2308,1024]{1,0:T(8,128)(2,1)} %x_ref.5, f32[6,1024]{1,0:T(8,128)} %reshape.123.vec_ref, bf16[2,16,64,2560]{3,2,1,0:T(8,128)(2,1)} %bitcast.46), custom_call_target="tpu_custom_call" | custom-call | flops 4865392640 | bytes 34242560 | tf_op jit(solution)/shard_map/merge/pallas_call | solution.py:52
  145.9 56.1 %expand.1 = (bf16[2320,4096]{1,0:T(8,128)(2,1)}, bf16[2320,4096]{1,0:T(8,128)(2,1)}, bf16[2,16,64,2048]{3,2,1,0:T(8,128)(2,1)}) custom-call(s32[1]{0:T(128)S(6)} %mul.7.live_ref, bf16[2320,1024]{1,0:T(8,128)(2,1)} %get-tuple-element.83.normed_ref.refs_0_, bf16[2308,1024]{1,0:T(8,128)(2,1)} %given_ref.3, f32[1,4096]{1,0:T(1,128)} %reshape.127.bias_ref, ...), custom_call_target="tpu_custom_call" | custom-call | flops 38923141120 | bytes 66379780 | tf_op jit(solution)/shard_map/expand/pallas_call | solution.py:52
  202.1 64.8 %mlp_back.1 = (bf16[2320,4096]{1,0:T(8,128)(2,1)}, bf16[2320,1024]{1,0:T(8,128)(2,1)}, bf16[2320,1024]{1,0:T(8,128)(2,1)}, f32[4,1024]{1,0:T(4,128)}, f32[32,128]{1,0:T(8,128)}) custom-call(s32[1]{0:T(128)S(6)} %mul.7.live_ref, bf16[2308,1024]{1,0:T(8,128)(2,1)} %given_ref.3, bf16[2320,4096]{1,0:T(8,128)(2,1)} %get-tuple-element.89.slope_ref, ...), custom_call_target="tpu_custom_call" | custom-call | tf_op jit(solution)/shard_map/mlp_back/pallas_call | solution.py:52
  266.9 41.1 %middle_grad.1 = (bf16[4,64,2560]{2,1,0:T(8,128)(2,1)}, bf16[4,64,2560]{2,1,0:T(8,128)(2,1)}, bf16[4,64,2560]{2,1,0:T(8,128)(2,1)}, bf16[4,64,2560]{2,1,0:T(8,128)(2,1)}) custom-call(bf16[2320,1024]{1,0:T(8,128)(2,1)} %get-tuple-element.83.normed_ref.refs_0_, bf16[2320,1024]{1,0:T(8,128)(2,1)} %get-tuple-element.115.refs_1_.low_ref, ...), custom_call_target="tpu_custom_call" | custom-call | tf_op jit(solution)/shard_map/middle_grad/pallas_call | solution.py:52
  308.7 4.2 collective-permute-start.1
  312.9 1.4 collective-permute-start.2
  314.3 75.5 %attend_back.1.refs_1_.grad_ref = bf16[3,2320,1024]{2,1,0:T(8,128)(2,1)} custom-call(bf16[3,2320,1024]{2,1,0:T(8,128)(2,1)} %get-tuple-element.80.triple_ref, f32[16,4,592]{2,1,0:T(4,128)} %get-tuple-element.88.stat_ref, bf16[2320,1024]{1,0:T(8,128)(2,1)} %get-tuple-element.97.grad_ref), custom_call_target="tpu_custom_call" | custom-call | tf_op jit(solution)/shard_map/attend_back/pallas_call | solution.py:52
  389.8 25.4 %heads_grad.1 = (bf16[4,64,1536]{2,1,0:T(8,128)(2,1)}, bf16[4,64,1536]{2,1,0:T(8,128)(2,1)}, bf16[4,64,1536]{2,1,0:T(8,128)(2,1)}, bf16[4,64,1536]{2,1,0:T(8,128)(2,1)}) custom-call(bf16[2320,1024]{1,0:T(8,128)(2,1)} %get-tuple-element.87.refs_0_, bf16[3,2320,1024]{2,1,0:T(8,128)(2,1)} %attend_back.1.refs_1_.grad_ref), custom_call_target="tpu_custom_call" | custom-call | tf_op jit(solution)/shard_map/heads_grad/pallas_call | solution.py:52
  415.8 1.6 collective-permute-start.4
  417.4 1.4 collective-permute-start.5
  418.8 2.9 fusion.3
  421.7 3.2 collective-permute-start.7
  424.9 27.7 %qkv_back.1 = (bf16[2308,1024]{1,0:T(8,128)(2,1)}, f32[2,1024]{1,0:T(2,128)}, f32[2,1024]{1,0:T(2,128)}) custom-call(bf16[2308,1024]{1,0:T(8,128)(2,1)} %x_ref.5, bf16[2320,1024]{1,0:T(8,128)(2,1)} %get-tuple-element.115.refs_1_.low_ref, f32[6,1024]{1,0:T(8,128)} %reshape.123.vec_ref, bf16[3,2320,1024]{2,1,0:T(8,128)(2,1)} %attend_back.1.refs_1_.grad_ref, ...), custom_call_target="tpu_custom_call" | custom-call | flops 14596177920 | bytes 35577856 | tf_op jit(solution)/shard_map/qkv_back/pallas_call | solution.py:52
  452.6 1.3 collective-permute-start.8
  453.9 33.2 %reduce.1 = (bf16[2308,1024]{1,0:T(8,128)(2,1)}, f32[3,64,512]{2,1,0:T(8,128)}, f32[8,128]{1,0:T(8,128)}) custom-call(bf16[2320,4096]{1,0:T(8,128)(2,1)} %get-tuple-element.84.act_ref, f32[2320,1024]{1,0:T(8,128)} %get-tuple-element.85.resid_ref, f32[6,1024]{1,0:T(8,128)} %reshape.123.vec_ref, bf16[2,16,64,2048]{3,2,1,0:T(8,128)(2,1)} %bitcast.53, ...), custom_call_target="tpu_custom_call" | custom-call | flops 19461570560 | bytes 45240320 | tf_op jit(solution)/shard_map/reduce/pallas_call | solution.py:52
  488.1 147.2 %finish.1 = (bf16[2308,1024]{1,0:T(8,128)(2,1)}, f32[64,2048]{1,0:T(8,128)}, f32[64,2048]{1,0:T(8,128)}, f32[64,512]{1,0:T(8,128)}, f32[3,64,512]{2,1,0:T(8,128)...) custom-call(bf16[2308,1024]{1,0:T(8,128)(2,1)} %get-tuple-element.12, ...), custom_call_target="tpu_custom_call" | custom-call | tf_op jit(solution)/shard_map/finish/pallas_call | solution.py:52
  (37 shorter events, 3.3 us)
Async XLA Ops:
  7.2 126.1 %all-gather.3.cloned.1.call-start = ((), (), s32[]{:S(2)}) async-start(), calls=%async_computation.1 | async-start | bytes 10813440 | tf_op jit(solution)/shard_map/all_gather | solution.py:740
  9.2 192.8 %all-gather.5.cloned.1.call-start = ((), (), s32[]{:S(2)}) async-start(), calls=%async_computation.2 | async-start | bytes 8650752 | tf_op jit(solution)/shard_map/all_gather | solution.py:740
  61.9 425.2 %reduce-scatter.2.cloned.1.call-start = ((), (), s32[]{:S(2)}) async-start(), calls=%async_computation.3 | async-start | bytes 8650752 | tf_op jit(solution)/shard_map/reduce_scatter | solution.py:839
  308.0 107.2 %collective-permute-start = (bf16[4,64,2560]{2,1,0:T(8,128)(2,1)}, bf16[4,64,2560]{2,1,0:T(8,128)(2,1)S(1)}, u32[]{:S(2)}, u32[]{:S(2)}) collective-permute-start(bf16[4,64,2560]{2,1,0:T(8,128)(2,1)} %get-tuple-element.102), channel_id=1, source_target_pairs={{0,4},{1,5},{2,6},{3,7},{4,0},{5,1},{6,2},{7,3},{8,12},{9,13},{10,... | collective-permute-start | bytes 3932168 | tf_op jit(solution)/shard_map/ppermute | solution.py:408
  308.7 106.5 %collective-permute-start.1 = (bf16[4,64,2560]{2,1,0:T(8,128)(2,1)}, bf16[4,64,2560]{2,1,0:T(8,128)(2,1)S(1)}, u32[]{:S(2)}, u32[]{:S(2)}) collective-permute-start(bf16[4,64,2560]{2,1,0:T(8,128)(2,1)} %get-tuple-element.103), channel_id=1, source_target_pairs={{0,1},{1,0},{2,3},{3,2},{4,5},{5,4},{6,7},{7,6},{8,9},{9,8},{10,11... | collective-permute-start | bytes 3932168 | tf_op jit(solution)/shard_map/ppermute | solution.py:408
  312.9 102.3 %collective-permute-start.2 = (bf16[4,64,2560]{2,1,0:T(8,128)(2,1)}, bf16[4,64,2560]{2,1,0:T(8,128)(2,1)}, u32[]{:S(2)}, u32[]{:S(2)}) collective-permute-start(bf16[4,64,2560]{2,1,0:T(8,128)(2,1)} %get-tuple-element.104), channel_id=1, source_target_pairs={{0,5},{1,4},{2,7},{3,6},{4,1},{5,0},{6,3},{7,2},{8,13},{9,12},{10,... | collective-permute-start | bytes 3932168 | tf_op jit(solution)/shard_map/ppermute | solution.py:408
  389.8 29.1 %copy-start = (bf16[4,64,2560]{2,1,0:T(8,128)(2,1)S(1)}, bf16[4,64,2560]{2,1,0:T(8,128)(2,1)}, u32[]{:S(2)}) copy-start(bf16[4,64,2560]{2,1,0:T(8,128)(2,1)} %get-tuple-element.110) | copy-start | bytes 3932164
  415.2 37.4 %collective-permute-start.3 = (bf16[4,64,1536]{2,1,0:T(8,128)(2,1)}, bf16[4,64,1536]{2,1,0:T(8,128)(2,1)}, u32[]{:S(2)}, u32[]{:S(2)}) collective-permute-start(bf16[4,64,1536]{2,1,0:T(8,128)(2,1)} %get-tuple-element.107), channel_id=1, source_target_pairs={{0,4},{1,5},{2,6},{3,7},{4,0},{5,1},{6,2},{7,3},{8,12},{9,13},{10,... | collective-permute-start | bytes 2359304 | tf_op jit(solution)/shard_map/ppermute | solution.py:408
  415.8 38.0 %collective-permute-start.4 = (bf16[4,64,1536]{2,1,0:T(8,128)(2,1)}, bf16[4,64,1536]{2,1,0:T(8,128)(2,1)}, u32[]{:S(2)}, u32[]{:S(2)}) collective-permute-start(bf16[4,64,1536]{2,1,0:T(8,128)(2,1)} %get-tuple-element.108), channel_id=1, source_target_pairs={{0,1},{1,0},{2,3},{3,2},{4,5},{5,4},{6,7},{7,6},{8,9},{9,8},{10,11... | collective-permute-start | bytes 2359304 | tf_op jit(solution)/shard_map/ppermute | solution.py:408
  417.4 36.4 %collective-permute-start.5 = (bf16[4,64,1536]{2,1,0:T(8,128)(2,1)}, bf16[4,64,1536]{2,1,0:T(8,128)(2,1)}, u32[]{:S(2)}, u32[]{:S(2)}) collective-permute-start(bf16[4,64,1536]{2,1,0:T(8,128)(2,1)} %get-tuple-element.109), channel_id=1, source_target_pairs={{0,5},{1,4},{2,7},{3,6},{4,1},{5,0},{6,3},{7,2},{8,13},{9,12},{10,... | collective-permute-start | bytes 2359304 | tf_op jit(solution)/shard_map/ppermute | solution.py:408
  421.7 30.9 %copy-start.3 = (bf16[64,2560]{1,0:T(8,128)(2,1)S(1)}, bf16[64,2560]{1,0:T(8,128)(2,1)}, u32[]{:S(2)}) copy-start(bf16[64,2560]{1,0:T(8,128)(2,1)} %get-tuple-element.127) | copy-start | bytes 983044
  421.7 65.4 %collective-permute-start.6 = (bf16[64,2560]{1,0:T(8,128)(2,1)}, bf16[64,2560]{1,0:T(8,128)(2,1)S(1)}, u32[]{:S(2)}, u32[]{:S(2)}) collective-permute-start(bf16[64,2560]{1,0:T(8,128)(2,1)} %get-tuple-element.125), channel_id=1, source_target_pairs={{0,8},{1,9},{2,10},{3,11},{4,12},{5,13},{6,14},{7,15},{8,0},{9,1},... | collective-permute-start | bytes 983048 | tf_op jit(solution)/shard_map/ppermute | solution.py:408
  421.7 65.4 %collective-permute-start.7 = (bf16[64,2560]{1,0:T(8,128)(2,1)}, bf16[64,2560]{1,0:T(8,128)(2,1)S(1)}, u32[]{:S(2)}, u32[]{:S(2)}) collective-permute-start(bf16[64,2560]{1,0:T(8,128)(2,1)} %get-tuple-element.126), channel_id=1, source_target_pairs={{0,16},{1,17},{2,18},{3,19},{4,20},{5,21},{6,22},{7,23},{8,24},{9,... | collective-permute-start | bytes 983048 | tf_op jit(solution)/shard_map/ppermute | solution.py:408
  452.6 34.5 %collective-permute-start.8 = (bf16[64,2560]{1,0:T(8,128)(2,1)S(1)}, bf16[64,2560]{1,0:T(8,128)(2,1)S(1)}, u32[]{:S(2)}, u32[]{:S(2)}) collective-permute-start(bf16[64,2560]{1,0:T(8,128)(2,1)S(1)} %copy-done.3), channel_id=1, source_target_pairs={{0,24},{1,25},{2,26},{3,27},{4,28},{5,29},{6,30},{7,31},{8,16},{9,... | collective-permute-start | bytes 983048 | tf_op jit(solution)/shard_map/ppermute | solution.py:408
  487.1 0.7 copy-start.1
  487.1 0.8 copy-start.2
  487.1 1.0 copy-start.4
Sparse Core Ops, SparseCore 0:
  11.5 98.5 all-gather.2
  113.0 75.9 all-gather.4
  202.2 155.2 reduce-scatter.1

commit v8 on v7

--- a/solution.py
+++ b/solution.py
@@ -674,16 +674,13 @@
             heads_ref[s] = total[:, s * own : (s + 1) * own]
 
 
-def finish_kernel(depth, given_ref, sums_ref, heads_ref, reduced_ref, *refs):
-    planes, (copy_ref, reduce_ref, expand_ref, merge_ref, out_ref, hb_ref, eb_ref) = refs[:depth], refs[depth : depth + 7]
-    vectors, sem = refs[depth + 7 : -1], refs[-1]
-    copies = []
-    for k in range(sem.shape[0]):
-        width = given_ref.shape[1] // sem.shape[0]
-        cols = pl.ds(k * width, width)
-        copies.append(pltpu.make_async_copy(given_ref.at[:, cols], copy_ref.at[:, cols], sem.at[k]))
-    for item in copies:
-        item.start()
+def finish_kernel(depth, *refs):
+    given_ref, *refs = refs
+    sums_ref, heads_ref, reduced_ref, *refs = refs
+    planes, refs = refs[:depth], refs[depth:]
+    copy_ref, *refs = refs
+    copy_ref[...] = given_ref[...]
+    reduce_ref, expand_ref, merge_ref, out_ref, hb_ref, eb_ref, *vectors = refs
     total = planes[0][...].astype(f32)
     for ref in planes[1:]:
         total = total + ref[...].astype(f32)
@@ -701,8 +698,6 @@
     for k in range(2):
         lane = part + tall + k * count
         hb_ref[k] = sums_ref[:wide, lane : lane + count]
-    for item in copies:
-        item.wait()
 
 
 def shards(
@@ -918,17 +913,16 @@
     )
     shapes = [(part, hidden_own), (part, hidden_own), (part, own)]
     shapes += [heads_sum.shape, (2, hbs[2], hbs[1]), ebs[::-1]] + [(1, part)] * 6
-    hbm = pl.BlockSpec(memory_space=pl.ANY)
-    arrays = [output, sums, heads_sum, grad_reduce, planes[0], *line]
+    arrays = [sums, heads_sum, grad_reduce, planes[0], *line]
+    piece = pl.BlockSpec((total_rows // 2, deep), lambda i: (i, 0))
     output, grad_reduce, grad_expand, grad_merge, grad_heads, hb_grad, eb_grad, *vector = call(
         functools.partial(finish_kernel, depth),
         "finish",
-        (),
-        [hbm] + [vmem] * (len(arrays) - 1),
-        [hbm] + [vmem] * len(shapes),
+        (2,),
+        [piece] + [full(v.shape) for v in arrays],
+        [piece] + [whole(shape) for shape in shapes],
         [((rows, deep), bf16)] + [(shape, f32) for shape in shapes],
-        arrays,
-        [pltpu.SemaphoreType.DMA((4,))],
+        [output] + arrays,
     )
     vector = [v.reshape(part) for v in vector]
 

time: 649 us -> 507 us (0.78)
  Pallas kernels: 605 us -> 463 us
    pallas_call x13, Pallas kernels: 605 us -> 463 us  [call(): pl.pallas_call(kernel, grid_spec=pltpu.PrefetchScalarGridSpec(num_scalar_...]
  transfers between devices with their start and end apart: 12 -> 12, of which waited for: 0 -> 0; matrix products, arithmetic and copies ran while one was open for 1% -> 1% of each run, Pallas kernels for 71% -> 91%
where the time goes in v8:
time: 507 us; the launch traced here: 500 us
  Pallas kernels  463 us (91%)
  between operations  15.1 us (3%)
  starting transfers between devices  14.4 us (3%)
    pallas_call x13, Pallas kernels, call(): pl.pallas_call(kernel, grid_spec=pltpu.PrefetchScalarGridSpec(num_scalar_...  463 us
    ppermute x9, starting transfers between devices, swap(): return lax.ppermute(values, ('dp', 'tensor'), moves)  14.3 us
  transfers between devices with their start and end apart: 12, of which 0 were waited for; matrix products, arithmetic and copies ran while one was open for 1% of the time, Pallas kernels for 91%

profile of v8, /device:TPU:0, one launch (start us, length us, event | category | flops | bytes accessed | tf_op | source)
XLA Modules:
  0.0 500.5 jit_solution(357470265148948501)
XLA Ops:
  7.2 2.0 pack.1
  9.3 52.6 %gather.1.w_ref = bf16[2,16,72,1536]{3,2,1,0:T(8,128)(2,1)} custom-call(bf16[72,1536]{1,0:T(8,128)(2,1)} %get-tuple-element.78.in_ref), custom_call_target="tpu_custom_call" | custom-call | tf_op jit(solution)/shard_map/gather/pallas_call | solution.py:52
  62.6 0.9 slice_convert_fusion
  63.6 0.7 reshape.123.vec_ref
  64.7 0.8 reshape.125.bias_ref
  65.8 0.8 reshape.127.bias_ref
  66.5 22.9 %qkv.1 = (bf16[2320,1024]{1,0:T(8,128)(2,1)}, bf16[3,2320,1024]{2,1,0:T(8,128)(2,1)}) custom-call(bf16[2308,1024]{1,0:T(8,128)(2,1)} %x_ref.5, f32[6,1024]{1,0:T(8,128)} %reshape.123.vec_ref, f32[2,1024]{1,0:T(2,128)} %reshape.125.bias_ref, bf16[2,16,72,1536]{3,2,1,0:T(8,128)(2,1)} %gather.1.w_ref), custom_call_target="tpu_custom_call" | custom-call | flops 14596177920 | bytes 30842880 | tf_op jit(solution)/shard_map/qkv/pallas_call | solution.py:52
  89.4 43.9 %attend.1 = (bf16[2320,1024]{1,0:T(8,128)(2,1)}, f32[16,4,592]{2,1,0:T(4,128)}) custom-call(bf16[3,2320,1024]{2,1,0:T(8,128)(2,1)} %get-tuple-element.80.triple_ref), custom_call_target="tpu_custom_call" | custom-call | flops 29796335616 | bytes 19156992 | tf_op jit(solution)/shard_map/attend/pallas_call | solution.py:52
  133.3 12.6 %merge.1 = (f32[2320,1024]{1,0:T(8,128)}, bf16[2320,1024]{1,0:T(8,128)(2,1)}) custom-call(bf16[2320,1024]{1,0:T(8,128)(2,1)} %get-tuple-element.81.ctx_ref, bf16[2308,1024]{1,0:T(8,128)(2,1)} %x_ref.5, f32[6,1024]{1,0:T(8,128)} %reshape.123.vec_ref, bf16[2,16,64,2560]{3,2,1,0:T(8,128)(2,1)} %bitcast.46), custom_call_target="tpu_custom_call" | custom-call | flops 4865392640 | bytes 34242560 | tf_op jit(solution)/shard_map/merge/pallas_call | solution.py:52
  145.9 56.1 %expand.1 = (bf16[2320,4096]{1,0:T(8,128)(2,1)}, bf16[2320,4096]{1,0:T(8,128)(2,1)}, bf16[2,16,64,2048]{3,2,1,0:T(8,128)(2,1)}) custom-call(s32[1]{0:T(128)S(6)} %mul.7.live_ref, bf16[2320,1024]{1,0:T(8,128)(2,1)} %get-tuple-element.83.normed_ref.refs_0_, bf16[2308,1024]{1,0:T(8,128)(2,1)} %given_ref.3, f32[1,4096]{1,0:T(1,128)} %reshape.127.bias_ref, ...), custom_call_target="tpu_custom_call" | custom-call | flops 38923141120 | bytes 66379780 | tf_op jit(solution)/shard_map/expand/pallas_call | solution.py:52
  202.1 64.8 %mlp_back.1 = (bf16[2320,4096]{1,0:T(8,128)(2,1)}, bf16[2320,1024]{1,0:T(8,128)(2,1)}, bf16[2320,1024]{1,0:T(8,128)(2,1)}, f32[4,1024]{1,0:T(4,128)}, f32[32,128]{1,0:T(8,128)}) custom-call(s32[1]{0:T(128)S(6)} %mul.7.live_ref, bf16[2308,1024]{1,0:T(8,128)(2,1)} %given_ref.3, bf16[2320,4096]{1,0:T(8,128)(2,1)} %get-tuple-element.89.slope_ref, ...), custom_call_target="tpu_custom_call" | custom-call | tf_op jit(solution)/shard_map/mlp_back/pallas_call | solution.py:52
  266.9 41.1 %middle_grad.1 = (bf16[4,64,2560]{2,1,0:T(8,128)(2,1)}, bf16[4,64,2560]{2,1,0:T(8,128)(2,1)}, bf16[4,64,2560]{2,1,0:T(8,128)(2,1)}, bf16[4,64,2560]{2,1,0:T(8,128)(2,1)}) custom-call(bf16[2320,1024]{1,0:T(8,128)(2,1)} %get-tuple-element.83.normed_ref.refs_0_, bf16[2320,1024]{1,0:T(8,128)(2,1)} %get-tuple-element.115.refs_1_.low_ref, ...), custom_call_target="tpu_custom_call" | custom-call | tf_op jit(solution)/shard_map/middle_grad/pallas_call | solution.py:52
  308.7 4.2 collective-permute-start.1
  312.9 1.4 collective-permute-start.2
  314.3 75.5 %attend_back.1.refs_1_.grad_ref = bf16[3,2320,1024]{2,1,0:T(8,128)(2,1)} custom-call(bf16[3,2320,1024]{2,1,0:T(8,128)(2,1)} %get-tuple-element.80.triple_ref, f32[16,4,592]{2,1,0:T(4,128)} %get-tuple-element.88.stat_ref, bf16[2320,1024]{1,0:T(8,128)(2,1)} %get-tuple-element.97.grad_ref), custom_call_target="tpu_custom_call" | custom-call | tf_op jit(solution)/shard_map/attend_back/pallas_call | solution.py:52
  389.8 25.4 %heads_grad.1 = (bf16[4,64,1536]{2,1,0:T(8,128)(2,1)}, bf16[4,64,1536]{2,1,0:T(8,128)(2,1)}, bf16[4,64,1536]{2,1,0:T(8,128)(2,1)}, bf16[4,64,1536]{2,1,0:T(8,128)(2,1)}) custom-call(bf16[2320,1024]{1,0:T(8,128)(2,1)} %get-tuple-element.87.refs_0_, bf16[3,2320,1024]{2,1,0:T(8,128)(2,1)} %attend_back.1.refs_1_.grad_ref), custom_call_target="tpu_custom_call" | custom-call | tf_op jit(solution)/shard_map/heads_grad/pallas_call | solution.py:52
  415.8 1.6 collective-permute-start.4
  417.4 1.4 collective-permute-start.5
  418.8 2.9 fusion.3
  421.7 3.2 collective-permute-start.7
  424.9 27.7 %qkv_back.1 = (bf16[2308,1024]{1,0:T(8,128)(2,1)}, f32[2,1024]{1,0:T(2,128)}, f32[2,1024]{1,0:T(2,128)}) custom-call(bf16[2308,1024]{1,0:T(8,128)(2,1)} %x_ref.5, bf16[2320,1024]{1,0:T(8,128)(2,1)} %get-tuple-element.115.refs_1_.low_ref, f32[6,1024]{1,0:T(8,128)} %reshape.123.vec_ref, bf16[3,2320,1024]{2,1,0:T(8,128)(2,1)} %attend_back.1.refs_1_.grad_ref, ...), custom_call_target="tpu_custom_call" | custom-call | flops 14596177920 | bytes 35577856 | tf_op jit(solution)/shard_map/qkv_back/pallas_call | solution.py:52
  452.6 1.3 collective-permute-start.8
  453.9 33.2 %reduce.1 = (bf16[2308,1024]{1,0:T(8,128)(2,1)}, f32[3,64,512]{2,1,0:T(8,128)}, f32[8,128]{1,0:T(8,128)}) custom-call(bf16[2320,4096]{1,0:T(8,128)(2,1)} %get-tuple-element.84.act_ref, f32[2320,1024]{1,0:T(8,128)} %get-tuple-element.85.resid_ref, f32[6,1024]{1,0:T(8,128)} %reshape.123.vec_ref, bf16[2,16,64,2048]{3,2,1,0:T(8,128)(2,1)} %bitcast.53, ...), custom_call_target="tpu_custom_call" | custom-call | flops 19461570560 | bytes 45240320 | tf_op jit(solution)/shard_map/reduce/pallas_call | solution.py:52
  488.1 5.4 %finish.1 = (bf16[2308,1024]{1,0:T(8,128)(2,1)}, f32[64,2048]{1,0:T(8,128)}, f32[64,2048]{1,0:T(8,128)}, f32[64,512]{1,0:T(8,128)}, f32[3,64,512]{2,1,0:T(8,128)...) custom-call(bf16[2308,1024]{1,0:T(8,128)(2,1)} %get-tuple-element.12, ...), custom_call_target="tpu_custom_call" | custom-call | tf_op jit(solution)/shard_map/finish/pallas_call | solution.py:52
  (37 shorter events, 3.3 us)
Async XLA Ops:
  7.2 126.1 %all-gather.3.cloned.1.call-start = ((), (), s32[]{:S(2)}) async-start(), calls=%async_computation.1 | async-start | bytes 10813440 | tf_op jit(solution)/shard_map/all_gather | solution.py:735
  9.2 192.8 %all-gather.5.cloned.1.call-start = ((), (), s32[]{:S(2)}) async-start(), calls=%async_computation.2 | async-start | bytes 8650752 | tf_op jit(solution)/shard_map/all_gather | solution.py:735
  61.9 425.2 %reduce-scatter.2.cloned.1.call-start = ((), (), s32[]{:S(2)}) async-start(), calls=%async_computation.3 | async-start | bytes 8650752 | tf_op jit(solution)/shard_map/reduce_scatter | solution.py:834
  308.0 107.2 %collective-permute-start = (bf16[4,64,2560]{2,1,0:T(8,128)(2,1)}, bf16[4,64,2560]{2,1,0:T(8,128)(2,1)S(1)}, u32[]{:S(2)}, u32[]{:S(2)}) collective-permute-start(bf16[4,64,2560]{2,1,0:T(8,128)(2,1)} %get-tuple-element.102), channel_id=1, source_target_pairs={{0,4},{1,5},{2,6},{3,7},{4,0},{5,1},{6,2},{7,3},{8,12},{9,13},{10,... | collective-permute-start | bytes 3932168 | tf_op jit(solution)/shard_map/ppermute | solution.py:408
  308.7 106.5 %collective-permute-start.1 = (bf16[4,64,2560]{2,1,0:T(8,128)(2,1)}, bf16[4,64,2560]{2,1,0:T(8,128)(2,1)S(1)}, u32[]{:S(2)}, u32[]{:S(2)}) collective-permute-start(bf16[4,64,2560]{2,1,0:T(8,128)(2,1)} %get-tuple-element.103), channel_id=1, source_target_pairs={{0,1},{1,0},{2,3},{3,2},{4,5},{5,4},{6,7},{7,6},{8,9},{9,8},{10,11... | collective-permute-start | bytes 3932168 | tf_op jit(solution)/shard_map/ppermute | solution.py:408
  312.9 102.3 %collective-permute-start.2 = (bf16[4,64,2560]{2,1,0:T(8,128)(2,1)}, bf16[4,64,2560]{2,1,0:T(8,128)(2,1)}, u32[]{:S(2)}, u32[]{:S(2)}) collective-permute-start(bf16[4,64,2560]{2,1,0:T(8,128)(2,1)} %get-tuple-element.104), channel_id=1, source_target_pairs={{0,5},{1,4},{2,7},{3,6},{4,1},{5,0},{6,3},{7,2},{8,13},{9,12},{10,... | collective-permute-start | bytes 3932168 | tf_op jit(solution)/shard_map/ppermute | solution.py:408
  389.8 29.1 %copy-start = (bf16[4,64,2560]{2,1,0:T(8,128)(2,1)S(1)}, bf16[4,64,2560]{2,1,0:T(8,128)(2,1)}, u32[]{:S(2)}) copy-start(bf16[4,64,2560]{2,1,0:T(8,128)(2,1)} %get-tuple-element.110) | copy-start | bytes 3932164
  415.2 37.4 %collective-permute-start.3 = (bf16[4,64,1536]{2,1,0:T(8,128)(2,1)}, bf16[4,64,1536]{2,1,0:T(8,128)(2,1)}, u32[]{:S(2)}, u32[]{:S(2)}) collective-permute-start(bf16[4,64,1536]{2,1,0:T(8,128)(2,1)} %get-tuple-element.107), channel_id=1, source_target_pairs={{0,4},{1,5},{2,6},{3,7},{4,0},{5,1},{6,2},{7,3},{8,12},{9,13},{10,... | collective-permute-start | bytes 2359304 | tf_op jit(solution)/shard_map/ppermute | solution.py:408
  415.8 38.0 %collective-permute-start.4 = (bf16[4,64,1536]{2,1,0:T(8,128)(2,1)}, bf16[4,64,1536]{2,1,0:T(8,128)(2,1)}, u32[]{:S(2)}, u32[]{:S(2)}) collective-permute-start(bf16[4,64,1536]{2,1,0:T(8,128)(2,1)} %get-tuple-element.108), channel_id=1, source_target_pairs={{0,1},{1,0},{2,3},{3,2},{4,5},{5,4},{6,7},{7,6},{8,9},{9,8},{10,11... | collective-permute-start | bytes 2359304 | tf_op jit(solution)/shard_map/ppermute | solution.py:408
  417.4 36.4 %collective-permute-start.5 = (bf16[4,64,1536]{2,1,0:T(8,128)(2,1)}, bf16[4,64,1536]{2,1,0:T(8,128)(2,1)}, u32[]{:S(2)}, u32[]{:S(2)}) collective-permute-start(bf16[4,64,1536]{2,1,0:T(8,128)(2,1)} %get-tuple-element.109), channel_id=1, source_target_pairs={{0,5},{1,4},{2,7},{3,6},{4,1},{5,0},{6,3},{7,2},{8,13},{9,12},{10,... | collective-permute-start | bytes 2359304 | tf_op jit(solution)/shard_map/ppermute | solution.py:408
  421.7 30.9 %copy-start.3 = (bf16[64,2560]{1,0:T(8,128)(2,1)S(1)}, bf16[64,2560]{1,0:T(8,128)(2,1)}, u32[]{:S(2)}) copy-start(bf16[64,2560]{1,0:T(8,128)(2,1)} %get-tuple-element.127) | copy-start | bytes 983044
  421.7 65.4 %collective-permute-start.6 = (bf16[64,2560]{1,0:T(8,128)(2,1)}, bf16[64,2560]{1,0:T(8,128)(2,1)S(1)}, u32[]{:S(2)}, u32[]{:S(2)}) collective-permute-start(bf16[64,2560]{1,0:T(8,128)(2,1)} %get-tuple-element.125), channel_id=1, source_target_pairs={{0,8},{1,9},{2,10},{3,11},{4,12},{5,13},{6,14},{7,15},{8,0},{9,1},... | collective-permute-start | bytes 983048 | tf_op jit(solution)/shard_map/ppermute | solution.py:408
  421.7 65.4 %collective-permute-start.7 = (bf16[64,2560]{1,0:T(8,128)(2,1)}, bf16[64,2560]{1,0:T(8,128)(2,1)S(1)}, u32[]{:S(2)}, u32[]{:S(2)}) collective-permute-start(bf16[64,2560]{1,0:T(8,128)(2,1)} %get-tuple-element.126), channel_id=1, source_target_pairs={{0,16},{1,17},{2,18},{3,19},{4,20},{5,21},{6,22},{7,23},{8,24},{9,... | collective-permute-start | bytes 983048 | tf_op jit(solution)/shard_map/ppermute | solution.py:408
  452.6 34.5 %collective-permute-start.8 = (bf16[64,2560]{1,0:T(8,128)(2,1)S(1)}, bf16[64,2560]{1,0:T(8,128)(2,1)S(1)}, u32[]{:S(2)}, u32[]{:S(2)}) collective-permute-start(bf16[64,2560]{1,0:T(8,128)(2,1)S(1)} %copy-done.3), channel_id=1, source_target_pairs={{0,24},{1,25},{2,26},{3,27},{4,28},{5,29},{6,30},{7,31},{8,16},{9,... | collective-permute-start | bytes 983048 | tf_op jit(solution)/shard_map/ppermute | solution.py:408
  487.1 0.7 copy-start.1
  487.1 0.8 copy-start.2
  487.1 1.0 copy-start.4
Sparse Core Ops, SparseCore 0:
  11.5 98.5 all-gather.2
  113.0 75.9 all-gather.4
  202.2 155.2 reduce-scatter.1

commit v9 on v8

--- a/solution.py
+++ b/solution.py
@@ -644,7 +644,7 @@
         copy(k).start()
         return carry
 
-    @pl.when(step == 1)
+    @pl.when(step == 0)
     def _():
         pl.semaphore_wait(barrier, count - 1)
         lax.fori_loop(1, count, start, 0)
@@ -833,7 +833,7 @@
     grad_reduce = grad_reduce.reshape(tensor * dp * part, hidden_own)
     grad_reduce = lax.psum_scatter(grad_reduce, AXES, scatter_dimension=0, tiled=True)
 
-    back_chunk = min(512, hidden_own)
+    back_chunk = min(2048, hidden_own)
     pre_grad, resid_low, grad_context, sums_two, esum = call(
         functools.partial(mlp_back_kernel, back_chunk),
         "mlp_back",

time: 507 us -> 506 us (level)
  no operation moved by 1% of the time
where the time goes in v9:
time: 506 us; the launch traced here: 499 us
  Pallas kernels  462 us (91%)
  between operations  15.1 us (3%)
  starting transfers between devices  14.3 us (3%)
    pallas_call x13, Pallas kernels, call(): pl.pallas_call(kernel, grid_spec=pltpu.PrefetchScalarGridSpec(num_scalar_...  462 us
    ppermute x9, starting transfers between devices, swap(): return lax.ppermute(values, ('dp', 'tensor'), moves)  14.2 us
  transfers between devices with their start and end apart: 12, of which 0 were waited for; matrix products, arithmetic and copies ran while one was open for 1% of the time, Pallas kernels for 91%

profile of v9, /device:TPU:0, one launch (start us, length us, event | category | flops | bytes accessed | tf_op | source)
XLA Modules:
  0.0 499.5 jit_solution(18090886183706228747)
XLA Ops:
  7.2 2.0 pack.1
  9.3 52.6 %gather.1.w_ref = bf16[2,16,72,1536]{3,2,1,0:T(8,128)(2,1)} custom-call(bf16[72,1536]{1,0:T(8,128)(2,1)} %get-tuple-element.78.in_ref), custom_call_target="tpu_custom_call" | custom-call | tf_op jit(solution)/shard_map/gather/pallas_call | solution.py:52
  62.6 0.9 slice_convert_fusion
  63.6 0.7 reshape.123.vec_ref
  64.7 0.8 reshape.125.bias_ref
  65.8 0.8 reshape.127.bias_ref
  66.5 22.9 %qkv.1 = (bf16[2320,1024]{1,0:T(8,128)(2,1)}, bf16[3,2320,1024]{2,1,0:T(8,128)(2,1)}) custom-call(bf16[2308,1024]{1,0:T(8,128)(2,1)} %x_ref.5, f32[6,1024]{1,0:T(8,128)} %reshape.123.vec_ref, f32[2,1024]{1,0:T(2,128)} %reshape.125.bias_ref, bf16[2,16,72,1536]{3,2,1,0:T(8,128)(2,1)} %gather.1.w_ref), custom_call_target="tpu_custom_call" | custom-call | flops 14596177920 | bytes 30842880 | tf_op jit(solution)/shard_map/qkv/pallas_call | solution.py:52
  89.4 43.9 %attend.1 = (bf16[2320,1024]{1,0:T(8,128)(2,1)}, f32[16,4,592]{2,1,0:T(4,128)}) custom-call(bf16[3,2320,1024]{2,1,0:T(8,128)(2,1)} %get-tuple-element.80.triple_ref), custom_call_target="tpu_custom_call" | custom-call | flops 29796335616 | bytes 19156992 | tf_op jit(solution)/shard_map/attend/pallas_call | solution.py:52
  133.3 12.6 %merge.1 = (f32[2320,1024]{1,0:T(8,128)}, bf16[2320,1024]{1,0:T(8,128)(2,1)}) custom-call(bf16[2320,1024]{1,0:T(8,128)(2,1)} %get-tuple-element.81.ctx_ref, bf16[2308,1024]{1,0:T(8,128)(2,1)} %x_ref.5, f32[6,1024]{1,0:T(8,128)} %reshape.123.vec_ref, bf16[2,16,64,2560]{3,2,1,0:T(8,128)(2,1)} %bitcast.46), custom_call_target="tpu_custom_call" | custom-call | flops 4865392640 | bytes 34242560 | tf_op jit(solution)/shard_map/merge/pallas_call | solution.py:52
  145.9 56.1 %expand.1 = (bf16[2320,4096]{1,0:T(8,128)(2,1)}, bf16[2320,4096]{1,0:T(8,128)(2,1)}, bf16[2,16,64,2048]{3,2,1,0:T(8,128)(2,1)}) custom-call(s32[1]{0:T(128)S(6)} %mul.7.live_ref, bf16[2320,1024]{1,0:T(8,128)(2,1)} %get-tuple-element.83.normed_ref.refs_0_, bf16[2308,1024]{1,0:T(8,128)(2,1)} %given_ref.3, f32[1,4096]{1,0:T(1,128)} %reshape.127.bias_ref, ...), custom_call_target="tpu_custom_call" | custom-call | flops 38923141120 | bytes 66379780 | tf_op jit(solution)/shard_map/expand/pallas_call | solution.py:52
  202.1 63.7 %mlp_back.1 = (bf16[2320,4096]{1,0:T(8,128)(2,1)}, bf16[2320,1024]{1,0:T(8,128)(2,1)}, bf16[2320,1024]{1,0:T(8,128)(2,1)}, f32[4,1024]{1,0:T(4,128)}, f32[32,128]{1,0:T(8,128)}) custom-call(s32[1]{0:T(128)S(6)} %mul.7.live_ref, bf16[2308,1024]{1,0:T(8,128)(2,1)} %given_ref.3, bf16[2320,4096]{1,0:T(8,128)(2,1)} %get-tuple-element.89.slope_ref, ...), custom_call_target="tpu_custom_call" | custom-call | tf_op jit(solution)/shard_map/mlp_back/pallas_call | solution.py:52
  265.8 41.1 %middle_grad.1 = (bf16[4,64,2560]{2,1,0:T(8,128)(2,1)}, bf16[4,64,2560]{2,1,0:T(8,128)(2,1)}, bf16[4,64,2560]{2,1,0:T(8,128)(2,1)}, bf16[4,64,2560]{2,1,0:T(8,128)(2,1)}) custom-call(bf16[2320,1024]{1,0:T(8,128)(2,1)} %get-tuple-element.83.normed_ref.refs_0_, bf16[2320,1024]{1,0:T(8,128)(2,1)} %get-tuple-element.115.refs_1_.low_ref, ...), custom_call_target="tpu_custom_call" | custom-call | tf_op jit(solution)/shard_map/middle_grad/pallas_call | solution.py:52
  307.5 4.2 collective-permute-start.1
  311.7 1.4 collective-permute-start.2
  313.1 75.5 %attend_back.1.refs_1_.grad_ref = bf16[3,2320,1024]{2,1,0:T(8,128)(2,1)} custom-call(bf16[3,2320,1024]{2,1,0:T(8,128)(2,1)} %get-tuple-element.80.triple_ref, f32[16,4,592]{2,1,0:T(4,128)} %get-tuple-element.88.stat_ref, bf16[2320,1024]{1,0:T(8,128)(2,1)} %get-tuple-element.97.grad_ref), custom_call_target="tpu_custom_call" | custom-call | tf_op jit(solution)/shard_map/attend_back/pallas_call | solution.py:52
  388.6 25.4 %heads_grad.1 = (bf16[4,64,1536]{2,1,0:T(8,128)(2,1)}, bf16[4,64,1536]{2,1,0:T(8,128)(2,1)}, bf16[4,64,1536]{2,1,0:T(8,128)(2,1)}, bf16[4,64,1536]{2,1,0:T(8,128)(2,1)}) custom-call(bf16[2320,1024]{1,0:T(8,128)(2,1)} %get-tuple-element.87.refs_0_, bf16[3,2320,1024]{2,1,0:T(8,128)(2,1)} %attend_back.1.refs_1_.grad_ref), custom_call_target="tpu_custom_call" | custom-call | tf_op jit(solution)/shard_map/heads_grad/pallas_call | solution.py:52
  414.7 1.6 collective-permute-start.4
  416.2 1.4 collective-permute-start.5
  417.6 2.9 fusion.3
  420.5 3.2 collective-permute-start.7
  423.7 27.7 %qkv_back.1 = (bf16[2308,1024]{1,0:T(8,128)(2,1)}, f32[2,1024]{1,0:T(2,128)}, f32[2,1024]{1,0:T(2,128)}) custom-call(bf16[2308,1024]{1,0:T(8,128)(2,1)} %x_ref.5, bf16[2320,1024]{1,0:T(8,128)(2,1)} %get-tuple-element.115.refs_1_.low_ref, f32[6,1024]{1,0:T(8,128)} %reshape.123.vec_ref, bf16[3,2320,1024]{2,1,0:T(8,128)(2,1)} %attend_back.1.refs_1_.grad_ref, ...), custom_call_target="tpu_custom_call" | custom-call | flops 14596177920 | bytes 35577856 | tf_op jit(solution)/shard_map/qkv_back/pallas_call | solution.py:52
  451.4 1.3 collective-permute-start.8
  452.6 33.4 %reduce.1 = (bf16[2308,1024]{1,0:T(8,128)(2,1)}, f32[3,64,512]{2,1,0:T(8,128)}, f32[8,128]{1,0:T(8,128)}) custom-call(bf16[2320,4096]{1,0:T(8,128)(2,1)} %get-tuple-element.84.act_ref, f32[2320,1024]{1,0:T(8,128)} %get-tuple-element.85.resid_ref, f32[6,1024]{1,0:T(8,128)} %reshape.123.vec_ref, bf16[2,16,64,2048]{3,2,1,0:T(8,128)(2,1)} %bitcast.53, ...), custom_call_target="tpu_custom_call" | custom-call | flops 19461570560 | bytes 45240320 | tf_op jit(solution)/shard_map/reduce/pallas_call | solution.py:52
  487.1 5.4 %finish.1 = (bf16[2308,1024]{1,0:T(8,128)(2,1)}, f32[64,2048]{1,0:T(8,128)}, f32[64,2048]{1,0:T(8,128)}, f32[64,512]{1,0:T(8,128)}, f32[3,64,512]{2,1,0:T(8,128)...) custom-call(bf16[2308,1024]{1,0:T(8,128)(2,1)} %get-tuple-element.12, ...), custom_call_target="tpu_custom_call" | custom-call | tf_op jit(solution)/shard_map/finish/pallas_call | solution.py:52
  (37 shorter events, 3.2 us)
Async XLA Ops:
  7.2 126.1 %all-gather.3.cloned.1.call-start = ((), (), s32[]{:S(2)}) async-start(), calls=%async_computation.1 | async-start | bytes 10813440 | tf_op jit(solution)/shard_map/all_gather | solution.py:735
  9.2 192.8 %all-gather.5.cloned.1.call-start = ((), (), s32[]{:S(2)}) async-start(), calls=%async_computation.2 | async-start | bytes 8650752 | tf_op jit(solution)/shard_map/all_gather | solution.py:735
  61.9 424.2 %reduce-scatter.2.cloned.1.call-start = ((), (), s32[]{:S(2)}) async-start(), calls=%async_computation.3 | async-start | bytes 8650752 | tf_op jit(solution)/shard_map/reduce_scatter | solution.py:834
  306.9 107.1 %collective-permute-start = (bf16[4,64,2560]{2,1,0:T(8,128)(2,1)}, bf16[4,64,2560]{2,1,0:T(8,128)(2,1)S(1)}, u32[]{:S(2)}, u32[]{:S(2)}) collective-permute-start(bf16[4,64,2560]{2,1,0:T(8,128)(2,1)} %get-tuple-element.102), channel_id=1, source_target_pairs={{0,4},{1,5},{2,6},{3,7},{4,0},{5,1},{6,2},{7,3},{8,12},{9,13},{10,... | collective-permute-start | bytes 3932168 | tf_op jit(solution)/shard_map/ppermute | solution.py:408
  307.5 106.5 %collective-permute-start.1 = (bf16[4,64,2560]{2,1,0:T(8,128)(2,1)}, bf16[4,64,2560]{2,1,0:T(8,128)(2,1)S(1)}, u32[]{:S(2)}, u32[]{:S(2)}) collective-permute-start(bf16[4,64,2560]{2,1,0:T(8,128)(2,1)} %get-tuple-element.103), channel_id=1, source_target_pairs={{0,1},{1,0},{2,3},{3,2},{4,5},{5,4},{6,7},{7,6},{8,9},{9,8},{10,11... | collective-permute-start | bytes 3932168 | tf_op jit(solution)/shard_map/ppermute | solution.py:408
  311.7 102.3 %collective-permute-start.2 = (bf16[4,64,2560]{2,1,0:T(8,128)(2,1)}, bf16[4,64,2560]{2,1,0:T(8,128)(2,1)}, u32[]{:S(2)}, u32[]{:S(2)}) collective-permute-start(bf16[4,64,2560]{2,1,0:T(8,128)(2,1)} %get-tuple-element.104), channel_id=1, source_target_pairs={{0,5},{1,4},{2,7},{3,6},{4,1},{5,0},{6,3},{7,2},{8,13},{9,12},{10,... | collective-permute-start | bytes 3932168 | tf_op jit(solution)/shard_map/ppermute | solution.py:408
  388.6 29.1 %copy-start = (bf16[4,64,2560]{2,1,0:T(8,128)(2,1)S(1)}, bf16[4,64,2560]{2,1,0:T(8,128)(2,1)}, u32[]{:S(2)}) copy-start(bf16[4,64,2560]{2,1,0:T(8,128)(2,1)} %get-tuple-element.110) | copy-start | bytes 3932164
  414.0 37.3 %collective-permute-start.3 = (bf16[4,64,1536]{2,1,0:T(8,128)(2,1)}, bf16[4,64,1536]{2,1,0:T(8,128)(2,1)}, u32[]{:S(2)}, u32[]{:S(2)}) collective-permute-start(bf16[4,64,1536]{2,1,0:T(8,128)(2,1)} %get-tuple-element.107), channel_id=1, source_target_pairs={{0,4},{1,5},{2,6},{3,7},{4,0},{5,1},{6,2},{7,3},{8,12},{9,13},{10,... | collective-permute-start | bytes 2359304 | tf_op jit(solution)/shard_map/ppermute | solution.py:408
  414.7 38.0 %collective-permute-start.4 = (bf16[4,64,1536]{2,1,0:T(8,128)(2,1)}, bf16[4,64,1536]{2,1,0:T(8,128)(2,1)}, u32[]{:S(2)}, u32[]{:S(2)}) collective-permute-start(bf16[4,64,1536]{2,1,0:T(8,128)(2,1)} %get-tuple-element.108), channel_id=1, source_target_pairs={{0,1},{1,0},{2,3},{3,2},{4,5},{5,4},{6,7},{7,6},{8,9},{9,8},{10,11... | collective-permute-start | bytes 2359304 | tf_op jit(solution)/shard_map/ppermute | solution.py:408
  416.2 36.4 %collective-permute-start.5 = (bf16[4,64,1536]{2,1,0:T(8,128)(2,1)}, bf16[4,64,1536]{2,1,0:T(8,128)(2,1)}, u32[]{:S(2)}, u32[]{:S(2)}) collective-permute-start(bf16[4,64,1536]{2,1,0:T(8,128)(2,1)} %get-tuple-element.109), channel_id=1, source_target_pairs={{0,5},{1,4},{2,7},{3,6},{4,1},{5,0},{6,3},{7,2},{8,13},{9,12},{10,... | collective-permute-start | bytes 2359304 | tf_op jit(solution)/shard_map/ppermute | solution.py:408
  420.5 30.9 %copy-start.3 = (bf16[64,2560]{1,0:T(8,128)(2,1)S(1)}, bf16[64,2560]{1,0:T(8,128)(2,1)}, u32[]{:S(2)}) copy-start(bf16[64,2560]{1,0:T(8,128)(2,1)} %get-tuple-element.127) | copy-start | bytes 983044
  420.5 65.6 %collective-permute-start.6 = (bf16[64,2560]{1,0:T(8,128)(2,1)}, bf16[64,2560]{1,0:T(8,128)(2,1)S(1)}, u32[]{:S(2)}, u32[]{:S(2)}) collective-permute-start(bf16[64,2560]{1,0:T(8,128)(2,1)} %get-tuple-element.125), channel_id=1, source_target_pairs={{0,8},{1,9},{2,10},{3,11},{4,12},{5,13},{6,14},{7,15},{8,0},{9,1},... | collective-permute-start | bytes 983048 | tf_op jit(solution)/shard_map/ppermute | solution.py:408
  420.5 65.6 %collective-permute-start.7 = (bf16[64,2560]{1,0:T(8,128)(2,1)}, bf16[64,2560]{1,0:T(8,128)(2,1)S(1)}, u32[]{:S(2)}, u32[]{:S(2)}) collective-permute-start(bf16[64,2560]{1,0:T(8,128)(2,1)} %get-tuple-element.126), channel_id=1, source_target_pairs={{0,16},{1,17},{2,18},{3,19},{4,20},{5,21},{6,22},{7,23},{8,24},{9,... | collective-permute-start | bytes 983048 | tf_op jit(solution)/shard_map/ppermute | solution.py:408
  451.4 34.7 %collective-permute-start.8 = (bf16[64,2560]{1,0:T(8,128)(2,1)S(1)}, bf16[64,2560]{1,0:T(8,128)(2,1)S(1)}, u32[]{:S(2)}, u32[]{:S(2)}) collective-permute-start(bf16[64,2560]{1,0:T(8,128)(2,1)S(1)} %copy-done.3), channel_id=1, source_target_pairs={{0,24},{1,25},{2,26},{3,27},{4,28},{5,29},{6,30},{7,31},{8,16},{9,... | collective-permute-start | bytes 983048 | tf_op jit(solution)/shard_map/ppermute | solution.py:408
  486.1 0.7 copy-start.1
  486.1 0.8 copy-start.2
  486.1 1.0 copy-start.4
Sparse Core Ops, SparseCore 0:
  11.5 98.5 all-gather.2
  113.0 75.9 all-gather.4
  202.2 155.5 reduce-scatter.1
